TPU v7x, 512 devices: a whole 4x4x16 slice. The times are simulated.
512 devices in a mesh: lon: 16 (over y, x_lo, core), lat: 32 (over x_hi, z).
Axes of the slice: x: 4 (x_hi: 2, x_lo: 2; x = x_hi * 2 + x_lo), y: 4, z: 16, core: 2. Of those that a mesh axis runs over, the one named last changes fastest.
Arguments:
- tokens: bfloat16 [256, 256, 768], P('lat', 'lon'), may hold values from -6 to 6
- patch_valid: int32 [256, 256], P('lat', 'lon'), may hold values 0 or 1
- block_mask: int32 [32, 16, 16], P('lat', 'lon'), may hold values from 0 to 1, as said below
- gain_attn: float32 [768], replicated, may hold values from 0.1 to 1.9
- gain_mlp: float32 [768], replicated, may hold values from 0.1 to 1.9
- w_qkv: bfloat16 [768, 2304], P('lat'), may hold values from -1.5 to 1.5
- w_out: bfloat16 [768, 768], P('lat'), may hold values from -0.21875 to 0.21875
- w_up: bfloat16 [768, 1536], P('lat'), may hold values from -0.21875 to 0.21875
- w_down: bfloat16 [1536, 768], P('lat'), may hold values from -0.15625 to 0.15625
Outputs:
- mixed: bfloat16 [256, 256, 768], P('lat', 'lon')
Inputs may be any that keep to these rules, and one draw needn't show every extreme that they name: block_mask[s, b, b] is 1 for every strip s and band b.
All inputs are finite; a program needn't handle non-finite values. No bound on the sum of `patch_valid` on one device may be relied on, other than what follows from the above.
Results may differ from a plain program's by a relative error of at most 0.013.
Values may be sent and summed in bfloat16 or wider, within the bound.
No kernel may reach another device: no remote copies, remote signals or barrier semaphores. Data moves between devices by JAX's collectives and lax.ppermute only.
A program may use at most 64 MiB of HBM per device.

v0:
```python
import jax
import jax.numpy as jnp
from jax import lax
from jax.sharding import PartitionSpec as P

D = 768
HEADS = 12
HEAD = 64
HALO = 2


MASKED = -1e30


def with_halo(block, sides, width):
    for axis, dim in sides:
        count = lax.axis_size(axis)
        forward = [(i, i + 1) for i in range(count - 1)]
        backward = [(target, source) for source, target in forward]
        low = lax.ppermute(
            lax.slice_in_dim(block, block.shape[dim] - width, None, axis=dim), axis, forward
        )
        high = lax.ppermute(lax.slice_in_dim(block, 0, width, axis=dim), axis, backward)
        block = jnp.concatenate([low, block, high], axis=dim)
    return block


def layer_norm(inputs, gain_vec):
    centre = jnp.mean(inputs, axis=-1, keepdims=True)
    spread = jnp.mean((inputs - centre) ** 2, axis=-1, keepdims=True)
    return (inputs - centre) * lax.rsqrt(spread + 1e-05) * gain_vec


def attend(running, queries, key_values, allowed):
    maxima, totals, weighted = running
    count_keys = key_values.shape[0]
    key_part = key_values[:, :D].reshape(count_keys, HEADS, HEAD)
    value_part = key_values[:, D:].reshape(count_keys, HEADS, HEAD)
    scores = jnp.einsum("qhd,khd->hqk", queries, key_part, preferred_element_type=jnp.float32)
    scores = jnp.where(allowed[None, None, :], scores, MASKED)
    new_max = jnp.maximum(maxima, jnp.max(scores, axis=-1))
    factor = jnp.exp(maxima - new_max)
    probs = jnp.where(allowed[None, None, :], jnp.exp(scores - new_max[..., None]), 0.0)
    totals = totals * factor + jnp.sum(probs, axis=-1)
    weighted = weighted * factor[..., None] + jnp.einsum(
        "hqk,khd->hqd", probs.astype(jnp.bfloat16), value_part, preferred_element_type=jnp.float32
    )
    return (new_max, totals, weighted)


def body(tokens, patch_valid, block_mask, gain_attn, gain_mlp, w_qkv, w_out, w_up, w_down):
    lat_rows, lon_cols = (tokens.shape[0], tokens.shape[1])
    tile_count = lat_rows * lon_cols
    full_qkv, full_out, full_up, full_down = (
        lax.all_gather(w_qkv, "lat", axis=0, tiled=True),
        lax.all_gather(w_out, "lat", axis=0, tiled=True),
        lax.all_gather(w_up, "lat", axis=0, tiled=True),
        lax.all_gather(w_down, "lat", axis=0, tiled=True),
    )
    residual_in = tokens.reshape(tile_count, D).astype(jnp.float32)
    normed = layer_norm(residual_in, gain_attn).astype(jnp.bfloat16)
    projected = jnp.dot(normed, full_qkv, preferred_element_type=jnp.float32)
    queries = (
        (projected[:, :D] * HEAD ** (-0.5)).astype(jnp.bfloat16).reshape(tile_count, HEADS, HEAD)
    )
    key_values = projected[:, D:].astype(jnp.bfloat16)
    kv_grid = key_values.reshape(lat_rows, lon_cols, 2 * D)
    padded = with_halo(kv_grid, (("lat", 0),), HALO)
    lat_place = lax.axis_index("lat")
    lat_count = lax.axis_size("lat")
    beside = jnp.concatenate([padded[:HALO], padded[lat_rows + HALO :]], axis=0).reshape(
        2 * HALO * lon_cols, 2 * D
    )
    beside_allowed = jnp.concatenate(
        [
            jnp.broadcast_to(lat_place > 0, (HALO * lon_cols,)),
            jnp.broadcast_to(lat_place < lat_count - 1, (HALO * lon_cols,)),
        ],
        axis=0,
    )
    running = (
        jnp.full((HEADS, tile_count), MASKED, jnp.float32),
        jnp.zeros((HEADS, tile_count), jnp.float32),
        jnp.zeros((HEADS, tile_count, HEAD), jnp.float32),
    )
    running = attend(running, queries, beside, beside_allowed)
    mask_row = block_mask.reshape(-1)
    band_total = mask_row.shape[0]
    portion = jax.tree.map(lambda a: lax.all_gather(a, "lon", axis=1, tiled=True), kv_grid)
    count_cols = portion.shape[1]
    channels = portion.shape[2]
    divisor = 1
    for candidate in range(min(count_cols, max(1, 1024 // lat_rows)), 0, -1):
        if count_cols % candidate == 0:
            divisor = candidate
            break
    groups = count_cols // divisor
    bands = (jnp.int32(0) + lax.iota(jnp.int32, count_cols)) // lon_cols
    hits = bands[:, None] == lax.iota(jnp.int32, band_total)[None, :]
    col_ok = (jnp.sum(jnp.where(hits, mask_row[None, :], 0), axis=1) > 0).reshape(groups, divisor)
    blocks = jnp.moveaxis(portion.reshape(lat_rows, groups, divisor, channels), 1, 0)

    def advance(state_now, item):
        block, block_ok = item
        flattened = block.reshape(lat_rows * divisor, channels)
        key_ok = jnp.broadcast_to(block_ok[None, :], (lat_rows, divisor)).reshape(-1)
        return (attend(state_now, queries, flattened, key_ok), None)

    state_out, unused = lax.scan(advance, running, (blocks, col_ok))
    running = state_out
    maxima, totals, weighted = running
    context = weighted / totals[..., None]
    context = jnp.transpose(context, (1, 0, 2)).reshape(tile_count, D).astype(jnp.bfloat16)
    validity = patch_valid.reshape(tile_count, 1).astype(jnp.float32)
    attended = jnp.dot(context, full_out, preferred_element_type=jnp.float32)
    hidden_state = (residual_in + validity * attended).astype(jnp.bfloat16)
    residual = hidden_state.astype(jnp.float32)
    normed_two = layer_norm(residual, gain_mlp).astype(jnp.bfloat16)
    inner = jax.nn.gelu(jnp.dot(normed_two, full_up, preferred_element_type=jnp.float32)).astype(
        jnp.bfloat16
    )
    mixed = residual + validity * jnp.dot(inner, full_down, preferred_element_type=jnp.float32)
    return mixed.astype(jnp.bfloat16).reshape(lat_rows, lon_cols, D)


def solution(mesh):
    in_specs = (
        P("lat", "lon", None),
        P("lat", "lon"),
        P("lat", "lon", None),
        P(),
        P(),
        P("lat", None),
        P("lat", None),
        P("lat", None),
        P("lat", None),
    )
    out_specs = P("lat", "lon", None)
    return jax.shard_map(body, mesh=mesh, in_specs=in_specs, out_specs=out_specs, check_vma=False)
```

profile of v0, /device:TPU:1, one launch (start us, length us, event | category | flops | bytes accessed | tf_op | source)
XLA Modules:
  0.0 672.3 jit_solution(9554029814059372410)
XLA Ops:
  7.3 1.0 convert_reduce_fusion
  8.4 1.1 multiply_reduce_fusion.1
  9.6 1.1 fusion.30
  10.8 156.0 %all-gather.6.cloned.1.call-done = bf16[768,2304]{1,0:T(8,128)(2,1)} async-done(((bf16[24,2304]{1,0:T(8,128)(2,1)}), bf16[768,2304]{1,0:T(8,128)(2,1)}) %all-gather.6.cloned.1.call-update) | async-done | bytes 3538960 | tf_op jit(solution)/shard_map/all_gather | solution.py:55
  166.8 2.6 fusion.58
  169.5 0.8 slice.48
  173.6 3.0 collective-permute-start
  176.6 1.3 collective-permute-start.1
  178.2 3.7 collective-permute-done.1
  183.3 1.0 convolution_add_fusion
  184.3 40.0 %all-gather.8.cloned.1.call-done = bf16[8,256,1536]{2,1,0:T(8,128)(2,1)} async-done(((bf16[8,16,1536]{2,1,0:T(8,128)(2,1)}), bf16[8,256,1536]{2,1,0:T(8,128)(2,1)}) %all-gather.8.cloned.1.call-update) | async-done | bytes 6291472 | tf_op jit(solution)/shard_map/all_gather | solution.py:89
  224.4 35.1 %while.14 = (s32[]{:T(128)}, f32[12,128]{1,0:T(8,128)S(1)}, f32[12,128]{1,0:T(8,128)}, f32[12,128,64]{1,2,0:T(8,128)}, pred[2,128]{1,0:T(4,128)(4,1)}, /*index=5...) while((s32[]{:T(128)}, f32[12,128]{1,0:T(8,128)S(1)}, f32[12,128]{1,0:T(8,128)}, ...), condition=%wide.region_8.9_spmd, body=%wide.region_5.8_spmd.sunk | while | flops 418581504 | bytes 67224168 | solution.py:109
  225.1 2.1 constant_dynamic-slice_fusion.2
  227.2 1.4 fusion.83
  228.6 1.7 copy.35
  230.3 1.4 bitcast_reduce_fusion.2
  231.8 2.5 fusion.84
  235.6 0.7 copy.36
  236.4 5.6 fusion.85
  242.6 2.1 constant_dynamic-slice_fusion.2
  244.7 1.4 fusion.83
  246.1 1.7 copy.35
  247.8 1.4 bitcast_reduce_fusion.2
  249.3 2.5 fusion.84
  253.1 0.7 copy.36
  253.9 5.6 fusion.85
  259.5 1.0 divide_convert_fusion
  260.5 102.4 %all-gather.10.cloned.1.call-done = bf16[768,768]{1,0:T(8,128)(2,1)} async-done(((bf16[24,768]{1,0:T(8,128)(2,1)}), bf16[768,768]{1,0:T(8,128)(2,1)}) %all-gather.10.cloned.1.call-update) | async-done | bytes 1179664 | tf_op jit(solution)/shard_map/all_gather | solution.py:56
  362.9 1.7 fusion.60
  364.9 147.2 %all-gather.12.cloned.1.call-done = bf16[768,1536]{1,0:T(8,128)(2,1)} async-done(((bf16[24,1536]{1,0:T(8,128)(2,1)}), bf16[768,1536]{1,0:T(8,128)(2,1)}) %all-gather.12.cloned.1.call-update) | async-done | bytes 2359312 | tf_op jit(solution)/shard_map/all_gather | solution.py:57
  512.1 149.6 %all-gather.14.cloned.1.call-done = bf16[1536,768]{1,0:T(8,128)(2,1)} async-done(((bf16[48,768]{1,0:T(8,128)(2,1)}), bf16[1536,768]{1,0:T(8,128)(2,1)}) %all-gather.14.cloned.1.call-update) | async-done | bytes 2359312 | tf_op jit(solution)/shard_map/all_gather | solution.py:58
  661.7 4.1 fusion.17
  (76 shorter events, 10.0 us)
Async XLA Ops:
  6.5 160.3 %all-gather.6.cloned.1.call-start = ((), (), s32[]{:S(2)}) async-start(), calls=%async_computation | async-start | bytes 3649536 | tf_op jit(solution)/shard_map/all_gather | solution.py:55
  7.3 217.1 %all-gather.8.cloned.1.call-start = ((), (), s32[]{:S(2)}) async-start(), calls=%async_computation.1 | async-start | bytes 6684672 | tf_op jit(solution)/shard_map/all_gather | solution.py:89
  10.7 161.5 %copy-start.8 = (s32[1,1,16]{2,1,0:T(1,128)S(1)}, s32[1,1,16]{2,1,0:T(1,128)}, u32[]{:S(2)}) copy-start(s32[1,1,16]{2,1,0:T(1,128)} %param.13) | copy-start | bytes 196
  10.8 162.1 %copy-start.6 = (s32[8,16]{1,0:T(8,128)S(1)}, s32[8,16]{1,0:T(8,128)}, u32[]{:S(2)}) copy-start(s32[8,16]{1,0:T(8,128)} %param.12) | copy-start | bytes 1540
  170.3 192.6 %all-gather.10.cloned.1.call-start = ((), (), s32[]{:S(2)}) async-start(), calls=%async_computation.2 | async-start | bytes 1216512 | tf_op jit(solution)/shard_map/all_gather | solution.py:56
  171.0 341.1 %all-gather.12.cloned.1.call-start = ((), (), s32[]{:S(2)}) async-start(), calls=%async_computation.3 | async-start | bytes 2433024 | tf_op jit(solution)/shard_map/all_gather | solution.py:57
  171.6 490.1 %all-gather.14.cloned.1.call-start = ((), (), s32[]{:S(2)}) async-start(), calls=%async_computation.4 | async-start | bytes 2433024 | tf_op jit(solution)/shard_map/all_gather | solution.py:58
  173.6 4.6 collective-permute-start
  176.6 5.4 collective-permute-start.1
  224.4 138.6 %copy-start.1 = (bf16[8,16,768]{2,1,0:T(8,128)(2,1)S(1)}, bf16[8,16,768]{2,1,0:T(8,128)(2,1)}, u32[]{:S(2)}) copy-start(bf16[8,16,768]{2,1,0:T(8,128)(2,1)} %param.11) | copy-start | bytes 589828
  225.1 5.2 copy-start.4
  231.7 2.7 copy-start
  231.7 2.6 copy-start.2
  235.0 0.6 copy-start.3
  235.0 1.4 copy-start.5
  242.6 5.2 copy-start.4
  249.3 2.7 copy-start
  249.3 2.6 copy-start.2
  252.5 0.6 copy-start.3
  252.5 1.4 copy-start.5
  259.5 402.2 %copy-start.7 = (f32[128]{0:T(128)S(1)}, f32[128]{0:T(128)}, u32[]{:S(2)}) copy-start(f32[128]{0:T(128)} %convert_element_type.61) | copy-start | bytes 1540
  259.5 402.2 %copy-start.9 = (f32[768]{0:T(1024)S(1)}, f32[768]{0:T(1024)}, u32[]{:S(2)}) copy-start(f32[768]{0:T(1024)} %param.15) | copy-start | bytes 9220
Sparse Core Ops, SparseCore 0:
  10.5 156.2 all-gather.5
  170.4 53.9 all-gather.7
  227.5 135.4 all-gather.9
  365.9 146.1 all-gather.11
  515.0 146.6 all-gather.13
where the time goes:
time: 681 us; the launch traced here: 672 us
  waiting for transfers between devices  602 us (88%)
  matrix products  23.7 us (3%)
  local copies, waits for them, and re-layouts  16.8 us (2%)
  between operations  13.3 us (2%)
  other arithmetic  12.3 us (2%)
    all_gather x1, waiting for transfers between devices, body(): lax.all_gather(w_qkv, 'lat', axis=0, tiled=True)  156 us
    all_gather x1, waiting for transfers between devices, body(): lax.all_gather(w_down, 'lat', axis=0, tiled=True)  150 us
    all_gather x1, waiting for transfers between devices, body(): lax.all_gather(w_up, 'lat', axis=0, tiled=True)  147 us
    all_gather x1, waiting for transfers between devices, body(): lax.all_gather(w_out, 'lat', axis=0, tiled=True)  102 us
    all_gather x1, waiting for transfers between devices, body(): lax.all_gather(a, 'lon', axis=1, tiled=True)  40 us
  transfers between devices with their start and end apart: 7, of which 7 were waited for; matrix products, arithmetic and copies ran while one was open for 7% of the time, Pallas kernels for 0%

commit v1 on v0

v1 whole, which is shorter than its diff:
```python
import functools

import jax
import jax.numpy as jnp
from jax import lax
from jax.experimental import pallas as pl
from jax.experimental.pallas import tpu as pltpu
from jax.sharding import Mesh, PartitionSpec as P

D = 768
HEADS = 12
HEAD = 64
FFW = 1536
TOK = 128
STRIPES = 16
LANES = 128
EDGE = 32
WIDE = 256
MASKED = -1e30
LON = ("y", "xl", "c")
CHIPS = ("y", "xl")
LAT = ("xh", "z")
BF = jnp.bfloat16
F32 = jnp.float32
VMEM_BYTES = 56 << 20


def norm_rows(x, gain):
    centre = jnp.mean(x, axis=-1, keepdims=True)
    diff = x - centre
    spread = jnp.mean(diff * diff, axis=-1, keepdims=True)
    return diff * lax.rsqrt(spread + 1e-05) * gain


def params():
    return pltpu.CompilerParams(vmem_limit_bytes=VMEM_BYTES)


def whole():
    return pl.BlockSpec(memory_space=pltpu.VMEM)


def scalar():
    return pl.BlockSpec(memory_space=pltpu.SMEM)


def cut_weights(place, qkv_ref, out_ref, up_ref, down_ref, piece_out):
    place_j = place[0]
    head = lax.rem(place_j, HEADS)
    block = head // 2
    odd = lax.rem(head, 2) == 1
    parts = []
    for which in range(3):
        start = pl.multiple_of(which * D + block * LANES, LANES)
        pair = qkv_ref[:, pl.ds(start, LANES)].astype(F32)
        parts.append(jnp.where(odd, pltpu.roll(pair, HEAD, 1), pair))
    low = lax.broadcasted_iota(jnp.int32, (24, LANES), 1) < HEAD
    piece_out[pl.ds(0, 24), :] = jnp.where(low, parts[0], pltpu.roll(parts[1], HEAD, 1)).astype(BF)
    piece_out[pl.ds(24, 24), :] = jnp.where(low, parts[2], 0.0).astype(BF)

    def fill(top, bottom):
        piece_out[pl.ds(48, 24), :] = top
        piece_out[pl.ds(72, 24), :] = bottom

    @pl.when(place_j < 6)
    def _():
        span = pl.ds(pl.multiple_of(place_j * LANES, LANES), LANES)
        fill(down_ref[pl.ds(0, 24), span], down_ref[pl.ds(24, 24), span])

    @pl.when((place_j >= 6) & (place_j < 9))
    def _():
        start = pl.multiple_of((place_j - 6) * 2 * LANES, LANES)
        fill(out_ref[:, pl.ds(start, LANES)], out_ref[:, pl.ds(start + LANES, LANES)])

    @pl.when(place_j >= 9)
    def _():
        start = pl.multiple_of(jnp.minimum(place_j - 9, 5) * 2 * LANES, LANES)
        fill(up_ref[:, pl.ds(start, LANES)], up_ref[:, pl.ds(start + LANES, LANES)])


def sort_mlp(place, rows_ref, mlp_out):
    place_j = place[0]

    @pl.when(place_j < 6)
    def _():
        for part in range(32):
            source = rows_ref.at[part % 16, (part // 16) ^ place[4]]
            mlp_out[pl.ds(part * 48, 48), :] = source[pl.ds(48, 48), :]

    @pl.when(place_j >= 6)
    def _():
        for part in range(32):
            source = rows_ref.at[part % 16, (part // 16) ^ place[4]]
            mlp_out[pl.ds(part * 24, 24), :] = source[pl.ds(48, 24), :]
            mlp_out[pl.ds(D + part * 24, 24), :] = source[pl.ds(72, 24), :]


def sort_head(place, rows_ref, head_out):
    for part in range(32):
        source = rows_ref.at[part % 16, (part // 16) ^ place[4]]
        head_out[pl.ds(part * 24, 24), pl.ds(0, LANES)] = source[pl.ds(0, 24), :]
        head_out[pl.ds(part * 24, 24), pl.ds(LANES, LANES)] = source[pl.ds(24, 24), :]


def first_norm(tokens_ref, gain_ref, mask_ref, spread_out):
    normed = norm_rows(tokens_ref[...].astype(F32), gain_ref[...].reshape(1, D)).astype(BF)
    seen = jnp.broadcast_to(mask_ref[0].astype(F32), (8, STRIPES))
    extra = jnp.concatenate([seen, jnp.zeros((8, D - STRIPES), F32)], axis=1).astype(BF)
    for peer in range(8):
        spread_out[peer, pl.ds(0, TOK), :] = normed
        spread_out[peer, pl.ds(TOK, 8), :] = extra


def project(near_ref, far_ref, weight_ref, q_out, k_out, vt_out, up_out, down_out, bias_out):
    weight = weight_ref[...]
    tops = []
    ends = []
    for tile in range(STRIPES):
        ref = near_ref if tile < 8 else far_ref
        rows = ref[tile % 8, pl.ds(0, TOK), :]
        full = jnp.dot(rows, weight, preferred_element_type=F32)
        qk = full[:, :LANES]
        qk_t = jnp.transpose(qk)
        v_t = jnp.transpose(full[:, LANES:])[:HEAD]
        span = pl.ds(tile * TOK, TOK)
        q_out[:, span] = (qk_t[:HEAD] * HEAD ** (-0.5)).astype(BF)
        k_out[span, :] = qk[:, HEAD:].astype(BF)
        vt_out[:, span] = v_t.astype(BF)
        kv_t = jnp.concatenate([qk_t[HEAD:], v_t], axis=0)
        seen = jnp.broadcast_to(ref[tile % 8, pl.ds(TOK, 8), :LANES].astype(F32)[:1], (LANES, LANES))
        bias_out[:, span] = jnp.where(jnp.transpose(seen)[:STRIPES] > 0, 0.0, MASKED)
        tops.append(kv_t[:, :EDGE])
        ends.append(kv_t[:, TOK - EDGE :])
    for group in range(4):
        span = pl.ds(group * LANES, LANES)
        up_out[:, span] = jnp.concatenate(tops[group * 4 : group * 4 + 4], axis=1).astype(BF)
        down_out[:, span] = jnp.concatenate(ends[group * 4 : group * 4 + 4], axis=1).astype(BF)


def attend_strip(
    place, q_ref, k_ref, vt_ref, bias_ref, acc_out, max_out, sum_out, even_scores, odd_scores, even_top, odd_top
):
    def score_chunk(group, chunk, scores, top):
        span = pl.ds(pl.multiple_of(group * WIDE, WIDE), WIDE)
        part = jnp.dot(k_ref[pl.ds(chunk * WIDE, WIDE), :], q_ref[:, span], preferred_element_type=F32)
        for half in range(2):
            tile = chunk * 2 + half
            side = place[3] if tile < 8 else 1 - place[3]
            row = bias_ref[pl.ds(2 * (tile % 8) + side, 1), span]
            piece = part[half * TOK : (half + 1) * TOK] + row
            scores[chunk, pl.ds(half * TOK, TOK), :] = piece
            best = jnp.max(piece.reshape(16, 8, WIDE), axis=0)
            top = best if top is None else jnp.maximum(top, best)
        return top

    def step(group, scores, top_ref, coming, next_scores, next_top):
        peak = jnp.max(top_ref[...], axis=0, keepdims=True)
        total = jnp.zeros((8, WIDE), F32)
        acc = jnp.zeros((HEAD, WIDE), F32)
        top = None
        for chunk in range(8):
            top = score_chunk(coming, chunk, next_scores, top)
            weights = jnp.exp(scores[chunk] - peak)
            total = total + jnp.sum(weights.reshape(32, 8, WIDE), axis=0)
            acc = acc + jnp.dot(
                vt_ref[:, pl.ds(chunk * WIDE, WIDE)], weights.astype(BF), preferred_element_type=F32
            )
        next_top[...] = top
        span = pl.ds(pl.multiple_of(group * WIDE, WIDE), WIDE)
        acc_out[:, span] = acc
        max_out[:, span] = jnp.broadcast_to(peak, (8, WIDE))
        sum_out[:, span] = jnp.broadcast_to(jnp.sum(total, axis=0, keepdims=True), (8, WIDE))

    top = None
    for chunk in range(8):
        top = score_chunk(0, chunk, even_scores, top)
    even_top[...] = top

    def pair(index, carry):
        first = index * 2
        step(first, even_scores, even_top, first + 1, odd_scores, odd_top)
        step(first + 1, odd_scores, odd_top, jnp.minimum(first + 2, 7), even_scores, even_top)
        return carry

    lax.fori_loop(0, 4, pair, 0)


def attend_edges(place, q_ref, above_ref, below_ref, acc_ref, max_ref, sum_ref, out_ref):
    core = place[3]
    key_band = lax.broadcasted_iota(jnp.int32, (LANES, 4 * TOK), 0) // EDGE
    query_band = lax.broadcasted_iota(jnp.int32, (LANES, 4 * TOK), 1) // TOK
    same = key_band == query_band
    for group in range(4):
        wide = slice(group * 4 * TOK, (group + 1) * 4 * TOK)
        keys = slice(group * LANES, (group + 1) * LANES)
        queries = q_ref[:, wide]
        scores = []
        for ref, flag in ((above_ref, place[1]), (below_ref, place[2])):
            part = lax.dot_general(
                ref[:HEAD, keys], queries, (((0,), (0,)), ((), ())), preferred_element_type=F32
            )
            scores.append(jnp.where(same & (flag > 0), part, MASKED))
        old = max_ref[:1, wide]
        peak = jnp.maximum(old, jnp.max(jnp.maximum(scores[0], scores[1]), axis=0, keepdims=True))
        factor = jnp.exp(old - peak)
        acc = acc_ref[:, wide] * factor
        total = sum_ref[:1, wide] * factor
        for ref, part in ((above_ref, scores[0]), (below_ref, scores[1])):
            weights = jnp.exp(part - peak)
            total = total + jnp.sum(weights, axis=0, keepdims=True)
            acc = acc + jnp.dot(ref[HEAD:, keys], weights.astype(BF), preferred_element_type=F32)
        result = (acc / total).astype(BF)
        for index in range(4):
            tile = group * 4 + index
            side = core if tile < 8 else 1 - core
            out_ref[2 * (tile % 8) + side] = result[:, index * TOK : (index + 1) * TOK]


def finish(ctx_ref, weights_hbm, tokens_ref, valid_ref, gain_ref, out_ref, w_out, w_up, w_down, sems):
    base = 6 * FFW
    jobs = [(w_out, unit, base + unit * D, D) for unit in range(6)]
    jobs += [(w_up, unit, base + (6 + unit) * D, D) for unit in range(12)]
    jobs += [(w_down, unit, unit * FFW, FFW) for unit in range(6)]
    copies = []
    for index, (target, unit, start, size) in enumerate(jobs):
        copy = pltpu.make_async_copy(
            weights_hbm.at[pl.ds(start, size), :], target.at[:, pl.ds(unit * LANES, LANES)], sems.at[index]
        )
        copy.start()
        copies.append(copy)
    context_t = ctx_ref[pl.ds(0, HEADS)].reshape(D, TOK)
    context = jnp.transpose(context_t.astype(F32)).astype(BF)
    valid = valid_ref[...].astype(F32)

    def wide_dot(rows, weight, chunk, first):
        copies[first + 2 * chunk].wait()
        copies[first + 2 * chunk + 1].wait()
        return jnp.dot(rows, weight[:, pl.ds(chunk * WIDE, WIDE)], preferred_element_type=F32)

    attended = jnp.concatenate([wide_dot(context, w_out, chunk, 0) for chunk in range(3)], axis=1)
    hidden = (tokens_ref[...].astype(F32) + valid * attended).astype(BF)
    residual = hidden.astype(F32)
    normed = norm_rows(residual, gain_ref[...].reshape(1, D)).astype(BF)
    inner = jnp.concatenate(
        [jax.nn.gelu(wide_dot(normed, w_up, chunk, 6)).astype(BF) for chunk in range(6)], axis=1
    )
    for chunk in range(3):
        down = wide_dot(inner, w_down, chunk, 18)
        span = slice(chunk * WIDE, (chunk + 1) * WIDE)
        out_ref[:, span] = (residual[:, span] + valid * down).astype(BF)


def body(tokens, patch_valid, block_mask, gain_attn, gain_mlp, w_qkv, w_out, w_up, w_down):
    lat_rows, lon_cols = tokens.shape[0], tokens.shape[1]
    place_j = lax.axis_index(LON)
    core = lax.axis_index("c")
    place_i = lax.axis_index(LAT)
    place = jnp.stack(
        [
            place_j,
            (place_i > 0).astype(jnp.int32),
            (place_i < 31).astype(jnp.int32),
            core,
            lax.axis_index("xh"),
        ]
    ).astype(jnp.int32)
    own = tokens.reshape(TOK, D)
    piece = pl.pallas_call(
        cut_weights,
        out_shape=jax.ShapeDtypeStruct((96, LANES), BF),
        in_specs=[scalar()] + [whole()] * 4,
        out_specs=whole(),
        compiler_params=params(),
        name="cut_weights",
    )(place, w_qkv, w_out, w_up, w_down)
    twin = lax.ppermute(piece, "xh", [(0, 1), (1, 0)])
    own, piece = lax.optimization_barrier((own, piece))
    spread = pl.pallas_call(
        first_norm,
        out_shape=jax.ShapeDtypeStruct((8, TOK + 8, D), BF),
        in_specs=[whole()] * 3,
        out_specs=whole(),
        compiler_params=params(),
        name="first_norm",
    )(own, gain_attn, block_mask)
    both = jnp.stack([piece, twin])
    both, spread = lax.optimization_barrier((both, spread))
    near = lax.all_to_all(spread, CHIPS, 0, 0)
    rows = lax.all_gather(both, "z", axis=0)
    near, rows = lax.optimization_barrier((near, rows))
    far = lax.ppermute(near, "c", [(0, 1), (1, 0)])
    mlp_rows = pl.pallas_call(
        sort_mlp,
        out_shape=jax.ShapeDtypeStruct((FFW, LANES), BF),
        in_specs=[scalar(), whole()],
        out_specs=whole(),
        compiler_params=params(),
        name="sort_mlp",
    )(place, rows)
    head_w = pl.pallas_call(
        sort_head,
        out_shape=jax.ShapeDtypeStruct((D, 2 * LANES), BF),
        in_specs=[scalar(), whole()],
        out_specs=whole(),
        compiler_params=params(),
        name="sort_head",
    )(place, rows)
    mlp_all = lax.all_gather(mlp_rows, LON, axis=0, tiled=True)

    halo = jax.ShapeDtypeStruct((LANES, 4 * LANES), BF)
    keys = STRIPES * TOK
    q_t, k_n, v_t, to_up, to_down, bias = pl.pallas_call(
        project,
        out_shape=(
            jax.ShapeDtypeStruct((HEAD, keys), BF),
            jax.ShapeDtypeStruct((keys, HEAD), BF),
            jax.ShapeDtypeStruct((HEAD, keys), BF),
            halo,
            halo,
            jax.ShapeDtypeStruct((STRIPES, keys), F32),
        ),
        in_specs=[whole()] * 3,
        out_specs=(whole(),) * 6,
        compiler_params=params(),
        cost_estimate=pl.CostEstimate(flops=2 * 2048 * 768 * 256, bytes_accessed=5 << 20, transcendentals=0),
        name="project",
    )(near, far, head_w)
    above = lax.ppermute(to_down, LAT, [(i, i + 1) for i in range(31)])
    below = lax.ppermute(to_up, LAT, [(i + 1, i) for i in range(31)])

    stat = jax.ShapeDtypeStruct((8, keys), F32)
    acc, peaks, sums = pl.pallas_call(
        attend_strip,
        out_shape=(jax.ShapeDtypeStruct((HEAD, keys), F32), stat, stat),
        in_specs=[scalar()] + [whole()] * 4,
        out_specs=(whole(),) * 3,
        scratch_shapes=[
            pltpu.VMEM((8, WIDE, WIDE), F32),
            pltpu.VMEM((8, WIDE, WIDE), F32),
            pltpu.VMEM((8, WIDE), F32),
            pltpu.VMEM((8, WIDE), F32),
        ],
        compiler_params=params(),
        cost_estimate=pl.CostEstimate(
            flops=4 * 2048 * 2048 * 256, bytes_accessed=3 << 20, transcendentals=2048 * 2048
        ),
        name="attend_strip",
    )(place, q_t, k_n, v_t, bias)

    context = pl.pallas_call(
        attend_edges,
        out_shape=jax.ShapeDtypeStruct((STRIPES, HEAD, TOK), BF),
        in_specs=[scalar()] + [whole()] * 6,
        out_specs=whole(),
        compiler_params=params(),
        name="attend_edges",
    )(place, q_t, above, below, acc, peaks, sums)

    mine = lax.all_to_all(context, LON, 0, 0)
    mixed = pl.pallas_call(
        finish,
        out_shape=jax.ShapeDtypeStruct((TOK, D), BF),
        in_specs=[whole(), pl.BlockSpec(memory_space=pl.ANY)] + [whole()] * 3,
        out_specs=whole(),
        scratch_shapes=[
            pltpu.VMEM((D, D), BF),
            pltpu.VMEM((D, FFW), BF),
            pltpu.VMEM((FFW, D), BF),
            pltpu.SemaphoreType.DMA((24,)),
        ],
        compiler_params=params(),
        cost_estimate=pl.CostEstimate(flops=2 * 128 * 768 * 3840, bytes_accessed=7 << 20, transcendentals=128 * 1536),
        name="finish",
    )(mine, mlp_all, own, patch_valid.reshape(TOK, 1), gain_mlp)
    return mixed.reshape(lat_rows, lon_cols, D)


def solution(mesh):
    fine = Mesh(mesh.devices.reshape(4, 2, 2, 2, 16), ("y", "xl", "c", "xh", "z"))
    in_specs = (
        P(LAT, LON, None),
        P(LAT, LON),
        P(LAT, LON, None),
        P(),
        P(),
        P(LAT, None),
        P(LAT, None),
        P(LAT, None),
        P(LAT, None),
    )
    out_specs = P(LAT, LON, None)
    return jax.shard_map(body, mesh=fine, in_specs=in_specs, out_specs=out_specs, check_vma=False)
```

time: 681 us -> 134 us (0.20); the launches traced: 672 us -> 134 us
  waiting for transfers between devices: 602 us -> 20.2 us
  blocking collectives: 0 us -> 36.4 us
  Pallas kernels: 0 us -> 31.2 us
  starting transfers between devices: 4.47 us -> 29.1 us
  matrix products: 23.7 us -> 0 us
  local copies, waits for them, and re-layouts: 16.8 us -> 3.33 us
  other arithmetic: 12.3 us -> 0.01 us
    all_gather x5 -> x1, waiting for transfers between devices: 595 us -> 9.61 us  [body(): mlp_all = lax.all_gather(mlp_rows, LON, axis=0, tiled=True)]
    all_gather x0 -> x1, blocking collectives: none -> 36.4 us  [body(): rows = lax.all_gather(both, 'z', axis=0)]
    pallas_call x0 -> x8, Pallas kernels: none -> 31.2 us  [the longest x1 8.26 us: body(): pl.pallas_call(attend_strip, out_shape=(jax.ShapeDtypeStruct((HEAD, keys)...]
    dot_general x9 -> x0, matrix products: 23.7 us -> none  [the longest x3 12.2 us: attend(): jnp.einsum('hqk,khd->hqd', probs.astype(jnp.bfloat16), value_part, prefer...]
    ppermute x2 -> x4, starting transfers between devices: 4.31 us -> 18.5 us  [the longest x1 10.3 us: body(): far = lax.ppermute(near, 'c', [(0, 1), (1, 0)])]
    all_to_all x0 -> x2, starting transfers between devices: none -> 10.5 us  [the longest x1 6.21 us: body(): mine = lax.all_to_all(context, LON, 0, 0)]
    all_to_all x0 -> x2, waiting for transfers between devices: none -> 9.35 us  [the longest x1 9.35 us: body(): mine = lax.all_to_all(context, LON, 0, 0)]
    reduce_sum x7 -> x0, other arithmetic: 7.62 us -> none  [the longest x3 5.2 us: attend(): totals = totals * factor + jnp.sum(probs, axis=-1)]
  transfers between devices with their start and end apart: 7 -> 7, of which waited for: 7 -> 3; matrix products, arithmetic and copies ran while one was open for 7% -> 1% of each run, Pallas kernels for 0% -> 15%
where the time goes in v1:
time: 134 us
  blocking collectives  36.4 us (27%)
  Pallas kernels  31.2 us (23%)
  starting transfers between devices  29.1 us (22%)
  waiting for transfers between devices  20.2 us (15%)
  between operations  13.5 us (10%)
  local copies, waits for them, and re-layouts  3.33 us (2%)
    all_gather x1, blocking collectives, body(): rows = lax.all_gather(both, 'z', axis=0)  36.4 us
    ppermute x1, starting transfers between devices, body(): far = lax.ppermute(near, 'c', [(0, 1), (1, 0)])  10.3 us
    all_gather x1, waiting for transfers between devices, body(): mlp_all = lax.all_gather(mlp_rows, LON, axis=0, tiled=True)  9.61 us
    all_to_all x1, waiting for transfers between devices, body(): mine = lax.all_to_all(context, LON, 0, 0)  9.35 us
    pallas_call x1, Pallas kernels, body(): pl.pallas_call(attend_strip, out_shape=(jax.ShapeDtypeStruct((HEAD, keys)...  8.26 us
    pallas_call x1, Pallas kernels, body(): pl.pallas_call(finish, out_shape=jax.ShapeDtypeStruct((TOK, D), BF), in_s...  6.59 us
    all_to_all x1, starting transfers between devices, body(): mine = lax.all_to_all(context, LON, 0, 0)  6.21 us
    ppermute x1, starting transfers between devices, body(): twin = lax.ppermute(piece, 'xh', [(0, 1), (1, 0)])  5.6 us
  transfers between devices with their start and end apart: 7, of which 3 were waited for; matrix products, arithmetic and copies ran while one was open for 1% of the time, Pallas kernels for 15%

profile of v1, /device:TPU:1, one launch (start us, length us, event | category | flops | bytes accessed | tf_op | source)
XLA Modules:
  0.0 133.6 jit_solution(7211874918049731647)
XLA Ops:
  6.5 0.7 stack.40.place
  7.2 1.8 %cut_weights.1 = bf16[96,128]{1,0:T(8,128)(2,1)} custom-call(s32[5]{0:T(128)} %stack.40.place, bf16[24,2304]{1,0:T(8,128)(2,1)} %qkv_ref.1, bf16[24,768]{1,0:T(8,128)(2,1)} %out_ref.1, bf16[24,1536]{1,0:T(8,128)(2,1)} %up_ref.1, bf16[48,768]{1,0:T(8,128)(2,1)} %down_ref.1), custom_call_target="tpu_custom_call" | custom-call | tf_op jit(solution)/shard_map/cut_weights/pallas_call | solution.py:268
  9.0 5.6 %collective-permute-start = (bf16[96,128]{1,0:T(8,128)(2,1)}, bf16[96,128]{1,0:T(8,128)(2,1)S(1)}, u32[]{:S(2)}, u32[]{:S(2)}) collective-permute-start(bf16[96,128]{1,0:T(8,128)(2,1)} %cut_weights.1), channel_id=1, source_target_pairs={{0,16},{16,0},{1,17},{17,1},{2,18},{18,2},{3,19},{19,3},{4,20},{20... | collective-permute-start | bytes 73736 | tf_op jit(solution)/shard_map/ppermute | solution.py:276
  14.6 2.4 %first_norm.1 = bf16[8,136,768]{2,1,0:T(8,128)(2,1)} custom-call(bf16[128,768]{1,0:T(8,128)(2,1)} %bitcast.12, f32[768]{0:T(1024)} %gain_ref.2, s32[1,1,16]{2,1,0:T(1,128)} %mask_ref.1), custom_call_target="tpu_custom_call" | custom-call | tf_op jit(solution)/shard_map/first_norm/pallas_call | solution.py:278
  17.0 0.0 collective-permute-done
  17.0 0.0 copy-done.5
  17.0 4.3 %all-to-all-start = ((bf16[8,136,768]{2,1,0:T(8,128)(2,1)}), bf16[8,136,768]{2,1,0:T(8,128)(2,1)S(1)}, u32[]{:S(2)}, u32[]{:S(2)}) async-start(bf16[8,136,768]{2,1,0:T(8,128)(2,1)} %first_norm.1), calls=%async_computation | async-start | bytes 3342336 | tf_op jit(solution)/shard_map/all_to_all | solution.py:288
  21.4 0.0 all-gather.3.cloned.1.call-start
  21.4 36.4 %all-gather = bf16[32,96,128]{2,1,0:T(8,128)(2,1)} all-gather(bf16[2,96,128]{2,1,0:T(8,128)(2,1)S(1)} %pad_maximum_fusion), channel_id=2, replica_groups=mesh['y'=4,'xl'=2,'c'=2,'xh'=2,'z'=16] {'z'}, dimensions={0}, use_global_device_ids=true | all-gather | bytes 835584 | tf_op jit(solution)/shard_map/all_gather | solution.py:289
  57.8 0.0 all-to-all-done.near_ref
  57.8 2.5 %sort_mlp.1 = bf16[1536,128]{1,0:T(8,128)(2,1)} custom-call(s32[5]{0:T(128)} %stack.40.place, bf16[16,2,96,128]{3,2,1,0:T(8,128)(2,1)} %bitcast.10), custom_call_target="tpu_custom_call" | custom-call | tf_op jit(solution)/shard_map/sort_mlp/pallas_call | solution.py:292
  60.3 0.0 all-gather.3.cloned.1.call-update
  60.4 10.3 %collective-permute-start.1 = (bf16[8,136,768]{2,1,0:T(8,128)(2,1)S(1)}, bf16[8,136,768]{2,1,0:T(8,128)(2,1)S(1)}, u32[]{:S(2)}, u32[]{:S(2)}) collective-permute-start(bf16[8,136,768]{2,1,0:T(8,128)(2,1)S(1)} %all-to-all-done.near_ref), channel_id=1, source_target_pairs={{0,32},{32,0},{1,33},{33,1},{2,34},{34,2},{3,35},{35,3},{4,36},{36... | collective-permute-start | bytes 5013512 | tf_op jit(solution)/shard_map/ppermute | solution.py:291
  70.7 2.0 %sort_head.1.weight_ref = bf16[768,256]{1,0:T(8,128)(2,1)} custom-call(s32[5]{0:T(128)} %stack.40.place, bf16[16,2,96,128]{3,2,1,0:T(8,128)(2,1)} %bitcast.11), custom_call_target="tpu_custom_call" | custom-call | tf_op jit(solution)/shard_map/sort_head/pallas_call | solution.py:300
  72.6 1.2 collective-permute-done.1.far_ref
  73.8 0.0 copy-done
  73.8 1.3 copy-done.1
  75.1 4.3 %project.1 = (bf16[64,2048]{1,0:T(8,128)(2,1)}, bf16[2048,64]{1,0:T(8,128)(2,1)}, bf16[64,2048]{1,0:T(8,128)(2,1)}, bf16[128,512]{1,0:T(8,128)(2,1)}, bf16[128,512]{1,0:T(8,128)(2,1)}, /*index=5*/f32[16,2048]{1,0:T(8,128)}) custom-call(bf16[8,136,768]{2,1,0:T(8,128)(2,1)} %copy-done, bf16[8,136,768]{2,1,0:T(8,128)(2,1)} %copy-done.1, ...), custom_call_target="tpu_custom_call" | custom-call | flops 805306368 | bytes 5242880 | tf_op jit(solution)/shard_map/project/pallas_call | solution.py:312
  79.4 1.3 collective-permute-start.2
  80.7 1.3 collective-permute-start.3
  82.0 8.3 %attend_strip.1 = (f32[64,2048]{1,0:T(8,128)}, f32[8,2048]{1,0:T(8,128)}, f32[8,2048]{1,0:T(8,128)}) custom-call(s32[5]{0:T(128)} %stack.40.place, bf16[64,2048]{1,0:T(8,128)(2,1)} %get-tuple-element.26.q_ref, bf16[2048,64]{1,0:T(8,128)(2,1)} %get-tuple-element.29.k_ref, bf16[64,2048]{1,0:T(8,128)(2,1)} %get-tuple-element.30.vt_ref, ...), custom_call_target="tpu_custom_call" | custom-call | flops 4294967296 | bytes 3145728 | tf_op jit(solution)/shard_map/attend_strip/pallas_call | solution.py:332
  90.2 0.0 collective-permute-done.2.above_ref
  90.2 0.0 collective-permute-done.3.below_ref
  90.3 0.0 copy-start.4
  90.3 0.6 copy-done.3
  90.9 0.0 copy-done.4
  90.9 3.3 %attend_edges.1 = bf16[16,64,128]{2,1,0:T(8,128)(2,1)} custom-call(s32[5]{0:T(128)} %stack.40.place, bf16[64,2048]{1,0:T(8,128)(2,1)} %get-tuple-element.26.q_ref, bf16[128,512]{1,0:T(8,128)(2,1)} %copy-done.3, bf16[128,512]{1,0:T(8,128)(2,1)} %copy-done.4, f32[64,2048]{1,0:T(8,128)} %get-tuple-element.32.acc_ref, f32[8,2048]{1,0:T(8,128)} %get-tuple-element.33.max_ref, ...), custom_call_target="tpu_custom_call" | custom-call | tf_op jit(solution)/shard_map/attend_edges/pallas_call | solution.py:350
  94.3 6.2 %all-to-all-start.1 = ((bf16[16,64,128]{2,1,0:T(8,128)(2,1)}), bf16[16,64,128]{2,1,0:T(8,128)(2,1)S(1)}, u32[]{:S(2)}, u32[]{:S(2)}) async-start(bf16[16,64,128]{2,1,0:T(8,128)(2,1)} %attend_edges.1), calls=%async_computation.1 | async-start | bytes 524288 | tf_op jit(solution)/shard_map/all_to_all | solution.py:359
  100.5 0.7 reshape.15.valid_ref
  101.2 9.4 %all-to-all-done.1.ctx_ref = bf16[16,64,128]{2,1,0:T(8,128)(2,1)S(1)} async-done(((bf16[16,64,128]{2,1,0:T(8,128)(2,1)}), bf16[16,64,128]{2,1,0:T(8,128)(2,1)S(1)}, u32[]{:S(2)}, u32[]{:S(2)}) %all-to-all-start.1) | async-done | bytes 262176 | tf_op jit(solution)/shard_map/all_to_all | solution.py:359
  110.6 9.6 %all-gather.3.cloned.1.call-done.weights_hbm = bf16[24576,128]{1,0:T(8,128)(2,1)} async-done(((bf16[1536,128]{1,0:T(8,128)(2,1)}), bf16[24576,128]{1,0:T(8,128)(2,1)}) %all-gather.3.cloned.1.call-update) | async-done | bytes 6291472 | tf_op jit(solution)/shard_map/all_gather | solution.py:308
  120.2 6.6 %finish.1 = bf16[128,768]{1,0:T(8,128)(2,1)} custom-call(bf16[16,64,128]{2,1,0:T(8,128)(2,1)} %copy-done.2, bf16[24576,128]{1,0:T(8,128)(2,1)} %all-gather.3.cloned.1.call-done.weights_hbm, bf16[128,768]{1,0:T(8,128)(2,1)} %bitcast.13, s32[128,1]{1,0:T(8,128)} %reshape.15.valid_ref, f32[768]{0:T(1024)} %gain_ref.3), custom_call_target="tpu_custom_call" | custom-call | flops 754974720 | bytes 7340032 | tf_op jit(solution)/shard_map/finish/pallas_call | solution.py:360
  (9 shorter events, 0.0 us)
Async XLA Ops:
  9.0 8.0 %copy-start.5 = (bf16[96,128]{1,0:T(8,128)(2,1)S(1)}, bf16[96,128]{1,0:T(8,128)(2,1)}, u32[]{:S(2)}) copy-start(bf16[96,128]{1,0:T(8,128)(2,1)} %cut_weights.1) | copy-start | bytes 73732
  9.0 8.0 %collective-permute-start = (bf16[96,128]{1,0:T(8,128)(2,1)}, bf16[96,128]{1,0:T(8,128)(2,1)S(1)}, u32[]{:S(2)}, u32[]{:S(2)}) collective-permute-start(bf16[96,128]{1,0:T(8,128)(2,1)} %cut_weights.1), channel_id=1, source_target_pairs={{0,16},{16,0},{1,17},{17,1},{2,18},{18,2},{3,19},{19,3},{4,20},{20... | collective-permute-start | bytes 73736 | tf_op jit(solution)/shard_map/ppermute | solution.py:276
  17.0 40.8 %all-to-all-start = ((bf16[8,136,768]{2,1,0:T(8,128)(2,1)}), bf16[8,136,768]{2,1,0:T(8,128)(2,1)S(1)}, u32[]{:S(2)}, u32[]{:S(2)}) async-start(bf16[8,136,768]{2,1,0:T(8,128)(2,1)} %first_norm.1), calls=%async_computation | async-start | bytes 3342336 | tf_op jit(solution)/shard_map/all_to_all | solution.py:288
  21.4 98.8 %all-gather.3.cloned.1.call-start = ((), (), s32[]{:S(2)}) async-start(), calls=%async_computation.2 | async-start | bytes 6684672 | tf_op jit(solution)/shard_map/all_gather | solution.py:308
  57.8 16.0 %copy-start = (bf16[8,136,768]{2,1,0:T(8,128)(2,1)}, bf16[8,136,768]{2,1,0:T(8,128)(2,1)S(1)}, u32[]{:S(2)}) copy-start(bf16[8,136,768]{2,1,0:T(8,128)(2,1)S(1)} %all-to-all-done.near_ref) | copy-start | bytes 5013508
  60.4 13.5 %collective-permute-start.1 = (bf16[8,136,768]{2,1,0:T(8,128)(2,1)S(1)}, bf16[8,136,768]{2,1,0:T(8,128)(2,1)S(1)}, u32[]{:S(2)}, u32[]{:S(2)}) collective-permute-start(bf16[8,136,768]{2,1,0:T(8,128)(2,1)S(1)} %all-to-all-done.near_ref), channel_id=1, source_target_pairs={{0,32},{32,0},{1,33},{33,1},{2,34},{34,2},{3,35},{35,3},{4,36},{36... | collective-permute-start | bytes 5013512 | tf_op jit(solution)/shard_map/ppermute | solution.py:291
  73.8 1.3 copy-start.1
  79.4 10.9 %collective-permute-start.2 = (bf16[128,512]{1,0:T(8,128)(2,1)}, bf16[128,512]{1,0:T(8,128)(2,1)S(1)}, u32[]{:S(2)}, u32[]{:S(2)}) collective-permute-start(bf16[128,512]{1,0:T(8,128)(2,1)} %get-tuple-element.27), channel_id=1, source_target_pairs={{0,1},{1,2},{2,3},{3,4},{4,5},{5,6},{6,7},{7,8},{8,9},{9,10},{10,1... | collective-permute-start | bytes 393224 | tf_op jit(solution)/shard_map/ppermute | solution.py:328
  80.7 9.6 %collective-permute-start.3 = (bf16[128,512]{1,0:T(8,128)(2,1)}, bf16[128,512]{1,0:T(8,128)(2,1)S(1)}, u32[]{:S(2)}, u32[]{:S(2)}) collective-permute-start(bf16[128,512]{1,0:T(8,128)(2,1)} %get-tuple-element.28), channel_id=1, source_target_pairs={{1,0},{2,1},{3,2},{4,3},{5,4},{6,5},{7,6},{8,7},{9,8},{10,9},{11,1... | collective-permute-start | bytes 393224 | tf_op jit(solution)/shard_map/ppermute | solution.py:329
  90.2 10.3 %copy-start.6 = (s32[8,16]{1,0:T(8,128)S(1)}, s32[8,16]{1,0:T(8,128)}, u32[]{:S(2)}) copy-start(s32[8,16]{1,0:T(8,128)} %param.10) | copy-start | bytes 1540
  90.2 0.7 copy-start.3
  90.3 0.7 copy-start.4
  94.3 16.3 %all-to-all-start.1 = ((bf16[16,64,128]{2,1,0:T(8,128)(2,1)}), bf16[16,64,128]{2,1,0:T(8,128)(2,1)S(1)}, u32[]{:S(2)}, u32[]{:S(2)}) async-start(bf16[16,64,128]{2,1,0:T(8,128)(2,1)} %attend_edges.1), calls=%async_computation.1 | async-start | bytes 524288 | tf_op jit(solution)/shard_map/all_to_all | solution.py:359
  110.5 9.6 %copy-start.2 = (bf16[16,64,128]{2,1,0:T(8,128)(2,1)}, bf16[16,64,128]{2,1,0:T(8,128)(2,1)S(1)}, u32[]{:S(2)}) copy-start(bf16[16,64,128]{2,1,0:T(8,128)(2,1)S(1)} %all-to-all-done.1.ctx_ref) | copy-start | bytes 786436
Sparse Core Ops, SparseCore 0:
  60.5 59.6 all-gather.2

commit v2 on v1

v2 whole, which is shorter than its diff:
```python
import functools

import jax
import jax.numpy as jnp
from jax import lax
from jax.experimental import pallas as pl
from jax.experimental.pallas import tpu as pltpu
from jax.sharding import Mesh, PartitionSpec as P

D = 768
HEADS = 12
HEAD = 64
FFW = 1536
TOK = 128
STRIPES = 16
LANES = 128
EDGE = 32
WIDE = 256
MASKED = -1e30
LON = ("y", "xl", "c")
CHIPS = ("y", "xl")
LAT = ("xh", "z")
BF = jnp.bfloat16
F32 = jnp.float32
VMEM_BYTES = 56 << 20


def norm_rows(x, gain):
    centre = jnp.mean(x, axis=-1, keepdims=True)
    diff = x - centre
    spread = jnp.mean(diff * diff, axis=-1, keepdims=True)
    return diff * lax.rsqrt(spread + 1e-05) * gain


def params():
    return pltpu.CompilerParams(vmem_limit_bytes=VMEM_BYTES)


def whole():
    return pl.BlockSpec(memory_space=pltpu.VMEM)


def scalar():
    return pl.BlockSpec(memory_space=pltpu.SMEM)


def first_norm(tokens_ref, gain_ref, mask_ref, norm_out):
    norm_out[pl.ds(0, TOK), :] = norm_rows(
        tokens_ref[...].astype(F32), gain_ref[...].reshape(1, D)
    ).astype(BF)
    seen = jnp.broadcast_to(mask_ref[0].astype(F32), (8, STRIPES))
    norm_out[pl.ds(TOK, 8), :] = jnp.concatenate([seen, jnp.zeros((8, D - STRIPES), F32)], axis=1).astype(BF)


def cut_weights(place, qkv_ref, out_ref, up_ref, down_ref, order_ref, piece_out):
    place_j = place[0]
    head = lax.rem(place_j, HEADS)
    block = head // 2
    odd = lax.rem(head, 2) == 1
    parts = []
    for which in range(3):
        start = pl.multiple_of(which * D + block * LANES, LANES)
        pair = qkv_ref[:, pl.ds(start, LANES)].astype(F32)
        parts.append(jnp.where(odd, pltpu.roll(pair, HEAD, 1), pair))
    low = lax.broadcasted_iota(jnp.int32, (24, LANES), 1) < HEAD
    qk = jnp.where(low, parts[0], pltpu.roll(parts[1], HEAD, 1)).astype(BF)
    v = jnp.where(low, parts[2], 0.0).astype(BF)
    for peer in range(32):
        piece_out[peer, pl.ds(0, 24), :] = qk
        piece_out[peer, pl.ds(24, 24), :] = v

    def fill(top, bottom):
        for peer in range(32):
            piece_out[peer, pl.ds(48, 24), :] = top
            piece_out[peer, pl.ds(72, 24), :] = bottom

    @pl.when(place_j < 6)
    def _():
        span = pl.ds(pl.multiple_of(place_j * LANES, LANES), LANES)
        fill(down_ref[pl.ds(0, 24), span], down_ref[pl.ds(24, 24), span])

    @pl.when((place_j >= 6) & (place_j < 9))
    def _():
        start = pl.multiple_of((place_j - 6) * 2 * LANES, LANES)
        fill(out_ref[:, pl.ds(start, LANES)], out_ref[:, pl.ds(start + LANES, LANES)])

    @pl.when(place_j >= 9)
    def _():
        start = pl.multiple_of(jnp.minimum(place_j - 9, 5) * 2 * LANES, LANES)
        fill(up_ref[:, pl.ds(start, LANES)], up_ref[:, pl.ds(start + LANES, LANES)])


def sort_mlp(place, rows_ref, mlp_out):
    place_j = place[0]

    @pl.when(place_j < 6)
    def _():
        for part in range(32):
            rows = rows_ref[part, pl.ds(48, 48), :]
            for peer in range(8):
                mlp_out[peer, pl.ds(part * 48, 48), :] = rows

    @pl.when(place_j >= 6)
    def _():
        for part in range(32):
            top = rows_ref[part, pl.ds(48, 24), :]
            bottom = rows_ref[part, pl.ds(72, 24), :]
            for peer in range(8):
                mlp_out[peer, pl.ds(part * 24, 24), :] = top
                mlp_out[peer, pl.ds(D + part * 24, 24), :] = bottom


def sort_head(rows_ref, head_out):
    for part in range(32):
        head_out[pl.ds(part * 24, 24), pl.ds(0, LANES)] = rows_ref[part, pl.ds(0, 24), :]
        head_out[pl.ds(part * 24, 24), pl.ds(LANES, LANES)] = rows_ref[part, pl.ds(24, 24), :]


def project(normed_ref, weight_ref, q_out, k_out, vt_out, up_out, down_out, bias_out):
    weight = weight_ref[...]
    tops = []
    ends = []
    for tile in range(4):
        full = jnp.dot(normed_ref[tile, pl.ds(0, TOK), :], weight, preferred_element_type=F32)
        qk = full[:, :LANES]
        qk_t = jnp.transpose(qk)
        v_t = jnp.transpose(full[:, LANES:])[:HEAD]
        span = pl.ds(tile * TOK, TOK)
        q_out[:, span] = (qk_t[:HEAD] * HEAD ** (-0.5)).astype(BF)
        k_out[span, :] = qk[:, HEAD:].astype(BF)
        vt_out[:, span] = v_t.astype(BF)
        kv_t = jnp.concatenate([qk_t[HEAD:], v_t], axis=0)
        seen = jnp.broadcast_to(normed_ref[tile, pl.ds(TOK, 8), :LANES].astype(F32)[:1], (LANES, LANES))
        bias_out[:, span] = jnp.where(jnp.transpose(seen)[:STRIPES] > 0, 0.0, MASKED)
        tops.append(kv_t[:, :EDGE])
        ends.append(kv_t[:, TOK - EDGE :])
    up_out[...] = jnp.concatenate(tops, axis=1).astype(BF)
    down_out[...] = jnp.concatenate(ends, axis=1).astype(BF)


def attend_strip(
    q_ref, k_ref, vt_ref, bias_ref, acc_out, max_out, sum_out, even_scores, odd_scores, even_top, odd_top
):
    def score_chunk(group, chunk, scores, top):
        span = pl.ds(pl.multiple_of(group * WIDE, WIDE), WIDE)
        part = jnp.dot(k_ref[pl.ds(chunk * WIDE, WIDE), :], q_ref[:, span], preferred_element_type=F32)
        for half in range(2):
            row = bias_ref[pl.ds(chunk * 2 + half, 1), span]
            piece = part[half * TOK : (half + 1) * TOK] + row
            scores[chunk, pl.ds(half * TOK, TOK), :] = piece
            best = jnp.max(piece.reshape(16, 8, WIDE), axis=0)
            top = best if top is None else jnp.maximum(top, best)
        return top

    def step(group, scores, top_ref, coming, next_scores, next_top):
        peak = jnp.max(top_ref[...], axis=0, keepdims=True)
        total = jnp.zeros((8, WIDE), F32)
        acc = jnp.zeros((HEAD, WIDE), F32)
        top = None
        for chunk in range(8):
            top = score_chunk(coming, chunk, next_scores, top)
            weights = jnp.exp(scores[chunk] - peak)
            total = total + jnp.sum(weights.reshape(32, 8, WIDE), axis=0)
            acc = acc + jnp.dot(
                vt_ref[:, pl.ds(chunk * WIDE, WIDE)], weights.astype(BF), preferred_element_type=F32
            )
        next_top[...] = top
        span = pl.ds(pl.multiple_of(group * WIDE, WIDE), WIDE)
        acc_out[:, span] = acc
        max_out[:, span] = jnp.broadcast_to(peak, (8, WIDE))
        sum_out[:, span] = jnp.broadcast_to(jnp.sum(total, axis=0, keepdims=True), (8, WIDE))

    top = None
    for chunk in range(8):
        top = score_chunk(0, chunk, even_scores, top)
    even_top[...] = top

    def pair(index, carry):
        first = index * 2
        step(first, even_scores, even_top, first + 1, odd_scores, odd_top)
        step(first + 1, odd_scores, odd_top, jnp.minimum(first + 2, 7), even_scores, even_top)
        return carry

    lax.fori_loop(0, 4, pair, 0)


def attend_edges(place, q_ref, above_ref, below_ref, acc_ref, max_ref, sum_ref, out_ref):
    key_band = lax.broadcasted_iota(jnp.int32, (LANES, 4 * TOK), 0) // EDGE
    query_band = lax.broadcasted_iota(jnp.int32, (LANES, 4 * TOK), 1) // TOK
    same = key_band == query_band
    for group in range(4):
        wide = slice(group * 4 * TOK, (group + 1) * 4 * TOK)
        keys = slice(group * LANES, (group + 1) * LANES)
        queries = q_ref[:, wide]
        scores = []
        for ref, flag in ((above_ref, place[1]), (below_ref, place[2])):
            part = lax.dot_general(
                ref[:HEAD, keys], queries, (((0,), (0,)), ((), ())), preferred_element_type=F32
            )
            scores.append(jnp.where(same & (flag > 0), part, MASKED))
        old = max_ref[:1, wide]
        peak = jnp.maximum(old, jnp.max(jnp.maximum(scores[0], scores[1]), axis=0, keepdims=True))
        factor = jnp.exp(old - peak)
        acc = acc_ref[:, wide] * factor
        total = sum_ref[:1, wide] * factor
        for ref, part in ((above_ref, scores[0]), (below_ref, scores[1])):
            weights = jnp.exp(part - peak)
            total = total + jnp.sum(weights, axis=0, keepdims=True)
            acc = acc + jnp.dot(ref[HEAD:, keys], weights.astype(BF), preferred_element_type=F32)
        result = (acc / total).astype(BF)
        for index in range(4):
            out_ref[group * 4 + index] = result[:, index * TOK : (index + 1) * TOK]


def finish(
    place, ctx_ref, near_hbm, far_hbm, tokens_ref, valid_ref, gain_ref, out_ref, w_in, w_down, sems
):
    core = place[3]

    def start(source, chip, side):
        part = 2 * chip + side
        if chip < 3:
            pltpu.make_async_copy(
                source.at[chip],
                w_down.at[:, pl.ds(pl.multiple_of(part * LANES, LANES), LANES)],
                sems.at[2 * part],
            ).start()
        else:
            for half in range(2):
                unit = 2 * (part - 6) + half
                pltpu.make_async_copy(
                    source.at[chip, pl.ds(half * D, D), :],
                    w_in.at[:, pl.ds(pl.multiple_of(unit * LANES, LANES), LANES)],
                    sems.at[2 * part + half],
                ).start()

    for chip in (3, 4, 5, 6, 7, 0, 1, 2):
        start(near_hbm, chip, core)
        start(far_hbm, chip, 1 - core)

    def settle(part):
        if part < 6:
            pltpu.make_async_copy(
                near_hbm.at[0], w_down.at[:, pl.ds(part * LANES, LANES)], sems.at[2 * part]
            ).wait()
        else:
            for half in range(2):
                unit = 2 * (part - 6) + half
                pltpu.make_async_copy(
                    near_hbm.at[0, pl.ds(0, D), :],
                    w_in.at[:, pl.ds(unit * LANES, LANES)],
                    sems.at[2 * part + half],
                ).wait()

    context_t = ctx_ref[pl.ds(0, HEADS)].reshape(D, TOK)
    context = jnp.transpose(context_t.astype(F32)).astype(BF)
    valid = valid_ref[...].astype(F32)

    def into(rows, part):
        settle(part)
        return jnp.dot(rows, w_in[:, pl.ds((part - 6) * WIDE, WIDE)], preferred_element_type=F32)

    attended = jnp.concatenate([into(context, part) for part in range(6, 9)], axis=1)
    hidden = (tokens_ref[...].astype(F32) + valid * attended).astype(BF)
    residual = hidden.astype(F32)
    normed = norm_rows(residual, gain_ref[...].reshape(1, D)).astype(BF)
    inner = jnp.concatenate([jax.nn.gelu(into(normed, part)).astype(BF) for part in range(9, 15)], axis=1)
    settle(15)
    for chunk in range(3):
        settle(2 * chunk)
        settle(2 * chunk + 1)
        span = slice(chunk * WIDE, (chunk + 1) * WIDE)
        down = jnp.dot(inner, w_down[:, span], preferred_element_type=F32)
        out_ref[:, span] = (residual[:, span] + valid * down).astype(BF)


def body(tokens, patch_valid, block_mask, gain_attn, gain_mlp, w_qkv, w_out, w_up, w_down):
    lat_rows, lon_cols = tokens.shape[0], tokens.shape[1]
    place_j = lax.axis_index(LON)
    core = lax.axis_index("c")
    place_i = lax.axis_index(LAT)
    place = jnp.stack(
        [
            place_j,
            (place_i > 0).astype(jnp.int32),
            (place_i < 31).astype(jnp.int32),
            core,
        ]
    ).astype(jnp.int32)
    own = tokens.reshape(TOK, D)
    normed = pl.pallas_call(
        first_norm,
        out_shape=jax.ShapeDtypeStruct((TOK + 8, D), BF),
        in_specs=[whole()] * 3,
        out_specs=whole(),
        compiler_params=params(),
        name="first_norm",
    )(own, gain_attn, block_mask)
    piece = pl.pallas_call(
        cut_weights,
        out_shape=jax.ShapeDtypeStruct((32, 96, LANES), BF),
        in_specs=[scalar()] + [whole()] * 4 + [pl.BlockSpec(memory_space=pl.ANY)],
        out_specs=whole(),
        compiler_params=params(),
        name="cut_weights",
    )(place, w_qkv, w_out, w_up, w_down, normed)
    strip = lax.all_gather(normed, LON, axis=0)
    rows = lax.all_to_all(piece, LAT, 0, 0)
    mlp_rows = pl.pallas_call(
        sort_mlp,
        out_shape=jax.ShapeDtypeStruct((8, FFW, LANES), BF),
        in_specs=[scalar(), whole()],
        out_specs=whole(),
        compiler_params=params(),
        name="sort_mlp",
    )(place, rows)
    near = lax.all_to_all(mlp_rows, CHIPS, 0, 0)
    head_w = pl.pallas_call(
        sort_head,
        out_shape=jax.ShapeDtypeStruct((D, 2 * LANES), BF),
        in_specs=[whole()],
        out_specs=whole(),
        compiler_params=params(),
        name="sort_head",
    )(rows)
    halo = jax.ShapeDtypeStruct((LANES, 4 * LANES), BF)
    keys = STRIPES * TOK
    q_t, k_n, v_t, to_up, to_down, bias = pl.pallas_call(
        project,
        out_shape=(
            jax.ShapeDtypeStruct((HEAD, keys), BF),
            jax.ShapeDtypeStruct((keys, HEAD), BF),
            jax.ShapeDtypeStruct((HEAD, keys), BF),
            halo,
            halo,
            jax.ShapeDtypeStruct((STRIPES, keys), F32),
        ),
        grid=(4,),
        in_specs=[
            pl.BlockSpec((4, TOK + 8, D), lambda g: (g, 0, 0)),
            pl.BlockSpec((D, 2 * LANES), lambda g: (0, 0)),
        ],
        out_specs=(
            pl.BlockSpec((HEAD, 4 * TOK), lambda g: (0, g)),
            pl.BlockSpec((4 * TOK, HEAD), lambda g: (g, 0)),
            pl.BlockSpec((HEAD, 4 * TOK), lambda g: (0, g)),
            pl.BlockSpec((LANES, LANES), lambda g: (0, g)),
            pl.BlockSpec((LANES, LANES), lambda g: (0, g)),
            pl.BlockSpec((STRIPES, 4 * TOK), lambda g: (0, g)),
        ),
        compiler_params=params(),
        cost_estimate=pl.CostEstimate(flops=2 * 2048 * 768 * 256, bytes_accessed=5 << 20, transcendentals=0),
        name="project",
    )(strip, head_w)
    above = lax.ppermute(to_down, LAT, [(i, i + 1) for i in range(31)])
    below = lax.ppermute(to_up, LAT, [(i + 1, i) for i in range(31)])

    stat = jax.ShapeDtypeStruct((8, keys), F32)
    acc, peaks, sums = pl.pallas_call(
        attend_strip,
        out_shape=(jax.ShapeDtypeStruct((HEAD, keys), F32), stat, stat),
        in_specs=[whole()] * 4,
        out_specs=(whole(),) * 3,
        scratch_shapes=[
            pltpu.VMEM((8, WIDE, WIDE), F32),
            pltpu.VMEM((8, WIDE, WIDE), F32),
            pltpu.VMEM((8, WIDE), F32),
            pltpu.VMEM((8, WIDE), F32),
        ],
        compiler_params=params(),
        cost_estimate=pl.CostEstimate(
            flops=4 * 2048 * 2048 * 256, bytes_accessed=3 << 20, transcendentals=2048 * 2048
        ),
        name="attend_strip",
    )(q_t, k_n, v_t, bias)

    context = pl.pallas_call(
        attend_edges,
        out_shape=jax.ShapeDtypeStruct((STRIPES, HEAD, TOK), BF),
        in_specs=[scalar()] + [whole()] * 6,
        out_specs=whole(),
        compiler_params=params(),
        name="attend_edges",
    )(place, q_t, above, below, acc, peaks, sums)

    near, context = lax.optimization_barrier((near, context))
    far = lax.ppermute(near, "c", [(0, 1), (1, 0)])
    mine = lax.all_to_all(context, LON, 0, 0)
    mixed = pl.pallas_call(
        finish,
        out_shape=jax.ShapeDtypeStruct((TOK, D), BF),
        in_specs=[scalar(), whole()] + [pl.BlockSpec(memory_space=pl.ANY)] * 2 + [whole()] * 3,
        out_specs=whole(),
        scratch_shapes=[
            pltpu.VMEM((D, 20 * LANES), BF),
            pltpu.VMEM((FFW, D), BF),
            pltpu.SemaphoreType.DMA((32,)),
        ],
        compiler_params=params(),
        cost_estimate=pl.CostEstimate(flops=2 * 128 * 768 * 3840, bytes_accessed=7 << 20, transcendentals=128 * 1536),
        name="finish",
    )(place, mine, near, far, own, patch_valid.reshape(TOK, 1), gain_mlp)
    return mixed.reshape(lat_rows, lon_cols, D)


def solution(mesh):
    fine = Mesh(mesh.devices.reshape(4, 2, 2, 2, 16), ("y", "xl", "c", "xh", "z"))
    in_specs = (
        P(LAT, LON, None),
        P(LAT, LON),
        P(LAT, LON, None),
        P(),
        P(),
        P(LAT, None),
        P(LAT, None),
        P(LAT, None),
        P(LAT, None),
    )
    out_specs = P(LAT, LON, None)
    return jax.shard_map(body, mesh=fine, in_specs=in_specs, out_specs=out_specs, check_vma=False)
```

time: 134 us -> 149 us (1.11)
  blocking collectives: 36.4 us -> 60.4 us
  starting transfers between devices: 29.1 us -> 18.8 us
  Pallas kernels: 31.2 us -> 33.1 us
    all_to_all x0 -> x1, blocking collectives: none -> 60.4 us  [body(): rows = lax.all_to_all(piece, LAT, 0, 0)]
    all_gather x1 -> x0, blocking collectives: 36.4 us -> none  [body(): rows = lax.all_gather(both, 'z', axis=0)]
    all_to_all x1, waiting for transfers between devices: 0.01 us -> 13.1 us  [body(): near = lax.all_to_all(mlp_rows, CHIPS, 0, 0)]
    all_gather x1, waiting for transfers between devices: 9.61 us -> 0.01 us  [body(): strip = lax.all_gather(normed, LON, axis=0)]
    ppermute x1, starting transfers between devices: 10.3 us -> 4.62 us  [body(): far = lax.ppermute(near, 'c', [(0, 1), (1, 0)])]
    ppermute x1 -> x0, starting transfers between devices: 5.6 us -> none  [body(): twin = lax.ppermute(piece, 'xh', [(0, 1), (1, 0)])]
    ppermute x1, starting transfers between devices: 1.29 us -> 5.13 us  [body(): above = lax.ppermute(to_down, LAT, [(i, i + 1) for i in range(31)])]
    all_to_all x1, waiting for transfers between devices: 9.35 us -> 6.4 us  [body(): mine = lax.all_to_all(context, LON, 0, 0)]
  transfers between devices with their start and end apart: 7 -> 6, of which waited for: 3 -> 2; matrix products, arithmetic and copies ran while one was open for 1% -> 1% of each run, Pallas kernels for 15% -> 16%
where the time goes in v2:
time: 149 us; the launch traced here: 148 us
  blocking collectives  60.4 us (41%)
  Pallas kernels  33.1 us (22%)
  waiting for transfers between devices  19.5 us (13%)
  starting transfers between devices  18.8 us (13%)
  between operations  13.5 us (9%)
  local copies, waits for them, and re-layouts  2.09 us (1%)
    all_to_all x1, blocking collectives, body(): rows = lax.all_to_all(piece, LAT, 0, 0)  60.4 us
    all_to_all x1, waiting for transfers between devices, body(): near = lax.all_to_all(mlp_rows, CHIPS, 0, 0)  13.1 us
    pallas_call x1, Pallas kernels, body(): pl.pallas_call(attend_strip, out_shape=(jax.ShapeDtypeStruct((HEAD, keys)...  8.25 us
    pallas_call x1, Pallas kernels, body(): pl.pallas_call(finish, out_shape=jax.ShapeDtypeStruct((TOK, D), BF), in_s...  6.87 us
    all_to_all x1, waiting for transfers between devices, body(): mine = lax.all_to_all(context, LON, 0, 0)  6.4 us
    pallas_call x1, Pallas kernels, body(): pl.pallas_call(project, out_shape=(jax.ShapeDtypeStruct((HEAD, keys), BF)...  5.52 us
    ppermute x1, starting transfers between devices, body(): above = lax.ppermute(to_down, LAT, [(i, i + 1) for i in range(31)])  5.13 us
    ppermute x1, starting transfers between devices, body(): far = lax.ppermute(near, 'c', [(0, 1), (1, 0)])  4.62 us
  transfers between devices with their start and end apart: 6, of which 2 were waited for; matrix products, arithmetic and copies ran while one was open for 1% of the time, Pallas kernels for 16%

profile of v2, /device:TPU:1, one launch (start us, length us, event | category | flops | bytes accessed | tf_op | source)
XLA Modules:
  0.0 148.0 jit_solution(1482936706093149843)
XLA Ops:
  6.5 0.0 all-gather.3.cloned.1.call-start
  6.5 1.9 %first_norm.1.order_ref = bf16[136,768]{1,0:T(8,128)(2,1)} custom-call(bf16[128,768]{1,0:T(8,128)(2,1)} %bitcast.8, f32[768]{0:T(1024)} %gain_ref.2, s32[1,1,16]{2,1,0:T(1,128)} %mask_ref.1), custom_call_target="tpu_custom_call" | custom-call | tf_op jit(solution)/shard_map/first_norm/pallas_call | solution.py:291
  8.4 0.0 all-gather.3.cloned.1.call-update
  8.4 0.7 pad_add_fusion.place
  9.1 2.1 %cut_weights.1 = bf16[32,96,128]{2,1,0:T(8,128)(2,1)} custom-call(s32[4]{0:T(128)} %pad_add_fusion.place, bf16[24,2304]{1,0:T(8,128)(2,1)} %qkv_ref.1, bf16[24,768]{1,0:T(8,128)(2,1)} %out_ref.1, bf16[24,1536]{1,0:T(8,128)(2,1)} %up_ref.1, bf16[48,768]{1,0:T(8,128)(2,1)} %down_ref.1, bf16[136,768]{1,0:T(8,128)(2,1)} %first_norm.1.order_ref), custom_call_target="tpu_custom_call" | custom-call | tf_op jit(solution)/shard_map/cut_weights/pallas_call | solution.py:299
  11.2 60.4 %all_to_all.15.rows_ref = bf16[32,96,128]{2,1,0:T(8,128)(2,1)} all-to-all(bf16[32,96,128]{2,1,0:T(8,128)(2,1)} %cut_weights.1), channel_id=1, replica_groups=mesh['y'=4,'xl'=2,'c'=2,'xh'=2,'z'=16] {'xh','z'}, dimensions={0} | all-to-all | bytes 1572864 | tf_op jit(solution)/shard_map/all_to_all | solution.py:308
  71.5 3.2 %sort_mlp.1 = bf16[8,1536,128]{2,1,0:T(8,128)(2,1)} custom-call(s32[4]{0:T(128)} %pad_add_fusion.place, bf16[32,96,128]{2,1,0:T(8,128)(2,1)} %all_to_all.15.rows_ref), custom_call_target="tpu_custom_call" | custom-call | tf_op jit(solution)/shard_map/sort_mlp/pallas_call | solution.py:309
  74.8 4.3 %all-to-all-start.1 = ((bf16[8,1536,128]{2,1,0:T(8,128)(2,1)}), bf16[8,1536,128]{2,1,0:T(8,128)(2,1)S(1)}, u32[]{:S(2)}, u32[]{:S(2)}) async-start(bf16[8,1536,128]{2,1,0:T(8,128)(2,1)} %sort_mlp.1), calls=%async_computation.1 | async-start | bytes 6291456 | tf_op jit(solution)/shard_map/all_to_all | solution.py:317
  79.0 1.9 %sort_head.1.weight_ref = bf16[768,256]{1,0:T(8,128)(2,1)} custom-call(bf16[32,96,128]{2,1,0:T(8,128)(2,1)} %all_to_all.15.rows_ref), custom_call_target="tpu_custom_call" | custom-call | tf_op jit(solution)/shard_map/sort_head/pallas_call | solution.py:318
  81.0 0.0 all-gather.3.cloned.1.call-done
  81.0 5.5 %project.1 = (bf16[64,2048]{1,0:T(8,128)(2,1)}, bf16[2048,64]{1,0:T(8,128)(2,1)}, bf16[64,2048]{1,0:T(8,128)(2,1)}, bf16[128,512]{1,0:T(8,128)(2,1)}, bf16[128,512]{1,0:T(8,128)(2,1)}, /*index=5*/f32[16,2048]{1,0:T(8,128)}) custom-call(bf16[16,136,768]{2,1,0:T(8,128)(2,1)} %bitcast.7, bf16[768,256]{1,0:T(8,128)(2,1)} %sort_head.1.weight_ref), custom_call_target="tpu_custom_call" | custom-call | flops 805306368 | bytes 5242880 | tf_op jit(solution)/shard_map/project/pallas_call | solution.py:328
  86.5 5.1 %collective-permute-start = (bf16[128,512]{1,0:T(8,128)(2,1)}, bf16[128,512]{1,0:T(8,128)(2,1)S(1)}, u32[]{:S(2)}, u32[]{:S(2)}) collective-permute-start(bf16[128,512]{1,0:T(8,128)(2,1)} %get-tuple-element.17), channel_id=1, source_target_pairs={{0,1},{1,2},{2,3},{3,4},{4,5},{5,6},{6,7},{7,8},{8,9},{9,10},{10,1... | collective-permute-start | bytes 393224 | tf_op jit(solution)/shard_map/ppermute | solution.py:355
  91.6 1.3 collective-permute-start.1
  92.9 0.0 copy-start.4
  92.9 8.2 %attend_strip.1 = (f32[64,2048]{1,0:T(8,128)}, f32[8,2048]{1,0:T(8,128)}, f32[8,2048]{1,0:T(8,128)}) custom-call(bf16[64,2048]{1,0:T(8,128)(2,1)} %get-tuple-element.16.q_ref, bf16[2048,64]{1,0:T(8,128)(2,1)} %get-tuple-element.19.k_ref, bf16[64,2048]{1,0:T(8,128)(2,1)} %get-tuple-element.20.vt_ref, f32[16,2048]{1,0:T(8,128)} %get-tuple-element.21.bias_ref), custom_call_target="tpu_custom_call" | custom-call | flops 4294967296 | bytes 3145728 | tf_op jit(solution)/shard_map/attend_strip/pallas_call | solution.py:359
  101.2 0.0 collective-permute-done.above_ref
  101.2 0.0 copy-start.2
  101.2 0.0 collective-permute-done.1.below_ref
  101.2 0.0 copy-start.3
  101.2 0.6 copy-done.2
  101.8 0.1 copy-done.3
  101.9 3.3 %attend_edges.1 = bf16[16,64,128]{2,1,0:T(8,128)(2,1)} custom-call(s32[4]{0:T(128)} %pad_add_fusion.place, bf16[64,2048]{1,0:T(8,128)(2,1)} %get-tuple-element.16.q_ref, bf16[128,512]{1,0:T(8,128)(2,1)} %copy-done.2, bf16[128,512]{1,0:T(8,128)(2,1)} %copy-done.3, f32[64,2048]{1,0:T(8,128)} %get-tuple-element.22.acc_ref, ...), custom_call_target="tpu_custom_call" | custom-call | tf_op jit(solution)/shard_map/attend_edges/pallas_call | solution.py:377
  105.2 13.1 %all-to-all-done.1.near_hbm = bf16[8,1536,128]{2,1,0:T(8,128)(2,1)S(1)} async-done(((bf16[8,1536,128]{2,1,0:T(8,128)(2,1)}), bf16[8,1536,128]{2,1,0:T(8,128)(2,1)S(1)}, u32[]{:S(2)}, u32[]{:S(2)}) %all-to-all-start.1) | async-done | bytes 3145760 | tf_op jit(solution)/shard_map/all_to_all | solution.py:317
  118.3 4.6 %collective-permute-start.2 = (bf16[8,1536,128]{2,1,0:T(8,128)(2,1)S(1)}, bf16[8,1536,128]{2,1,0:T(8,128)(2,1)}, u32[]{:S(2)}, u32[]{:S(2)}) collective-permute-start(bf16[8,1536,128]{2,1,0:T(8,128)(2,1)S(1)} %all-to-all-done.1.near_hbm), channel_id=1, source_target_pairs={{0,32},{32,0},{1,33},{33,1},{2,34},{34,2},{3,35},{35,3},{4,36},{36... | collective-permute-start | bytes 9437192 | tf_op jit(solution)/shard_map/ppermute | solution.py:387
  123.0 3.4 %all-to-all-start.2 = ((bf16[16,64,128]{2,1,0:T(8,128)(2,1)}), bf16[16,64,128]{2,1,0:T(8,128)(2,1)S(1)}, u32[]{:S(2)}, u32[]{:S(2)}) async-start(bf16[16,64,128]{2,1,0:T(8,128)(2,1)} %attend_edges.1), calls=%async_computation.2 | async-start | bytes 524288 | tf_op jit(solution)/shard_map/all_to_all | solution.py:388
  126.4 0.0 copy-done.4
  126.4 0.7 reshape.15.valid_ref
  127.1 6.4 %all-to-all-done.2.ctx_ref = bf16[16,64,128]{2,1,0:T(8,128)(2,1)S(1)} async-done(((bf16[16,64,128]{2,1,0:T(8,128)(2,1)}), bf16[16,64,128]{2,1,0:T(8,128)(2,1)S(1)}, u32[]{:S(2)}, u32[]{:S(2)}) %all-to-all-start.2) | async-done | bytes 262176 | tf_op jit(solution)/shard_map/all_to_all | solution.py:388
  133.5 0.0 collective-permute-done.2.far_hbm
  133.5 0.0 copy-done
  133.5 0.7 copy-done.1
  134.2 6.9 %finish.1 = bf16[128,768]{1,0:T(8,128)(2,1)} custom-call(s32[4]{0:T(128)} %pad_add_fusion.place, bf16[16,64,128]{2,1,0:T(8,128)(2,1)} %copy-done.1, bf16[8,1536,128]{2,1,0:T(8,128)(2,1)} %copy-done, bf16[8,1536,128]{2,1,0:T(8,128)(2,1)} %collective-permute-done.2.far_hbm, bf16[128,768]{1,0:T(8,128)(2,1)} %bitcast.9, s32[128,1]{1,0:T(8,128)} %reshape.15.valid_ref, ...), custom_call_target="tpu_custom_call" | custom-call | flops 754974720 | bytes 7340032 | tf_op jit(solution)/shard_map/finish/pallas_call | solution.py:389
  (2 shorter events, 0.0 us)
Async XLA Ops:
  6.5 74.4 %all-gather.3.cloned.1.call-start = ((), (), s32[]{:S(2)}) async-start(), calls=%async_computation.3 | async-start | bytes 3551232 | tf_op jit(solution)/shard_map/all_gather | solution.py:307
  74.8 43.6 %all-to-all-start.1 = ((bf16[8,1536,128]{2,1,0:T(8,128)(2,1)}), bf16[8,1536,128]{2,1,0:T(8,128)(2,1)S(1)}, u32[]{:S(2)}, u32[]{:S(2)}) async-start(bf16[8,1536,128]{2,1,0:T(8,128)(2,1)} %sort_mlp.1), calls=%async_computation.1 | async-start | bytes 6291456 | tf_op jit(solution)/shard_map/all_to_all | solution.py:317
  86.5 14.7 %collective-permute-start = (bf16[128,512]{1,0:T(8,128)(2,1)}, bf16[128,512]{1,0:T(8,128)(2,1)S(1)}, u32[]{:S(2)}, u32[]{:S(2)}) collective-permute-start(bf16[128,512]{1,0:T(8,128)(2,1)} %get-tuple-element.17), channel_id=1, source_target_pairs={{0,1},{1,2},{2,3},{3,4},{4,5},{5,6},{6,7},{7,8},{8,9},{9,10},{10,1... | collective-permute-start | bytes 393224 | tf_op jit(solution)/shard_map/ppermute | solution.py:355
  91.6 9.6 %collective-permute-start.1 = (bf16[128,512]{1,0:T(8,128)(2,1)}, bf16[128,512]{1,0:T(8,128)(2,1)S(1)}, u32[]{:S(2)}, u32[]{:S(2)}) collective-permute-start(bf16[128,512]{1,0:T(8,128)(2,1)} %get-tuple-element.18), channel_id=1, source_target_pairs={{1,0},{2,1},{3,2},{4,3},{5,4},{6,5},{7,6},{8,7},{9,8},{10,9},{11,1... | collective-permute-start | bytes 393224 | tf_op jit(solution)/shard_map/ppermute | solution.py:356
  92.9 33.5 %copy-start.4 = (s32[8,16]{1,0:T(8,128)S(1)}, s32[8,16]{1,0:T(8,128)}, u32[]{:S(2)}) copy-start(s32[8,16]{1,0:T(8,128)} %param.10) | copy-start | bytes 1540
  101.2 0.6 copy-start.2
  101.2 0.7 copy-start.3
  118.3 15.2 %copy-start = (bf16[8,1536,128]{2,1,0:T(8,128)(2,1)}, bf16[8,1536,128]{2,1,0:T(8,128)(2,1)S(1)}, u32[]{:S(2)}) copy-start(bf16[8,1536,128]{2,1,0:T(8,128)(2,1)S(1)} %all-to-all-done.1.near_hbm) | copy-start | bytes 9437188
  118.3 15.2 %collective-permute-start.2 = (bf16[8,1536,128]{2,1,0:T(8,128)(2,1)S(1)}, bf16[8,1536,128]{2,1,0:T(8,128)(2,1)}, u32[]{:S(2)}, u32[]{:S(2)}) collective-permute-start(bf16[8,1536,128]{2,1,0:T(8,128)(2,1)S(1)} %all-to-all-done.1.near_hbm), channel_id=1, source_target_pairs={{0,32},{32,0},{1,33},{33,1},{2,34},{34,2},{3,35},{35,3},{4,36},{36... | collective-permute-start | bytes 9437192 | tf_op jit(solution)/shard_map/ppermute | solution.py:387
  123.0 10.6 %all-to-all-start.2 = ((bf16[16,64,128]{2,1,0:T(8,128)(2,1)}), bf16[16,64,128]{2,1,0:T(8,128)(2,1)S(1)}, u32[]{:S(2)}, u32[]{:S(2)}) async-start(bf16[16,64,128]{2,1,0:T(8,128)(2,1)} %attend_edges.1), calls=%async_computation.2 | async-start | bytes 524288 | tf_op jit(solution)/shard_map/all_to_all | solution.py:388
  133.5 0.7 copy-start.1
Sparse Core Ops, SparseCore 0:
  9.5 50.2 all-gather.2

commit v3 on v1

v3 whole, which is shorter than its diff:
```python
import functools

import jax
import jax.numpy as jnp
from jax import lax
from jax.experimental import pallas as pl
from jax.experimental.pallas import tpu as pltpu
from jax.sharding import Mesh, PartitionSpec as P

D = 768
HEADS = 12
HEAD = 64
FFW = 1536
TOK = 128
STRIPES = 16
LANES = 128
EDGE = 32
WIDE = 256
MASKED = -1e30
LON = ("y", "xl", "c")
PLANE = ("xh", "y", "xl")
LAT = ("xh", "z")
BF = jnp.bfloat16
F32 = jnp.float32


def norm_rows(x, gain):
    centre = jnp.mean(x, axis=-1, keepdims=True)
    diff = x - centre
    spread = jnp.mean(diff * diff, axis=-1, keepdims=True)
    return diff * lax.rsqrt(spread + 1e-05) * gain


def params(mib):
    return pltpu.CompilerParams(vmem_limit_bytes=mib << 20)


def whole():
    return pl.BlockSpec(memory_space=pltpu.VMEM)


def prepare(tokens_ref, gain_ref, mask_ref, qkv_ref, out_ref, up_ref, down_ref, norm_out, piece_out):
    norm_out[pl.ds(0, TOK), :] = norm_rows(
        tokens_ref[...].astype(F32), gain_ref[...].reshape(1, D)
    ).astype(BF)
    seen = jnp.broadcast_to(mask_ref[0].astype(F32), (8, STRIPES))
    norm_out[pl.ds(TOK, 8), :] = jnp.concatenate([seen, jnp.zeros((8, D - STRIPES), F32)], axis=1).astype(BF)

    place_j = (lax.axis_index("y") * 2 + lax.axis_index("xl")) * 2 + lax.axis_index("c")
    head = lax.rem(place_j, HEADS)
    block = head // 2
    odd = lax.rem(head, 2) == 1
    parts = []
    for which in range(3):
        start = pl.multiple_of(which * D + block * LANES, LANES)
        pair = qkv_ref[:, pl.ds(start, LANES)].astype(F32)
        parts.append(jnp.where(odd, pltpu.roll(pair, HEAD, 1), pair))
    low = lax.broadcasted_iota(jnp.int32, (24, LANES), 1) < HEAD
    qk = jnp.where(low, parts[0], pltpu.roll(parts[1], HEAD, 1)).astype(BF)
    v = jnp.where(low, parts[2], 0.0).astype(BF)
    piece_out[pl.ds(0, 24), :] = qk
    piece_out[pl.ds(24, 24), :] = v

    def fill(top, bottom):
        piece_out[pl.ds(48, 24), :] = top
        piece_out[pl.ds(72, 24), :] = bottom

    @pl.when(place_j < 6)
    def _():
        span = pl.ds(pl.multiple_of(place_j * LANES, LANES), LANES)
        fill(down_ref[pl.ds(0, 24), span], down_ref[pl.ds(24, 24), span])

    @pl.when((place_j >= 6) & (place_j < 9))
    def _():
        start = pl.multiple_of((place_j - 6) * 2 * LANES, LANES)
        fill(out_ref[:, pl.ds(start, LANES)], out_ref[:, pl.ds(start + LANES, LANES)])

    @pl.when(place_j >= 9)
    def _():
        start = pl.multiple_of(jnp.minimum(place_j - 9, 5) * 2 * LANES, LANES)
        fill(up_ref[:, pl.ds(start, LANES)], up_ref[:, pl.ds(start + LANES, LANES)])


def sort_rows(rows_ref, mlp_hbm, head_out, mlp_rows, sems):
    place_j = (lax.axis_index("y") * 2 + lax.axis_index("xl")) * 2 + lax.axis_index("c")

    @pl.when(place_j < 6)
    def _():
        for part in range(16):
            mlp_rows[pl.ds(part * 48, 48), :] = rows_ref[part, pl.ds(48, 48), :]

    @pl.when(place_j >= 6)
    def _():
        for part in range(16):
            mlp_rows[pl.ds(part * 24, 24), :] = rows_ref[part, pl.ds(48, 24), :]
            mlp_rows[pl.ds(D // 2 + part * 24, 24), :] = rows_ref[part, pl.ds(72, 24), :]

    copies = [pltpu.make_async_copy(mlp_rows, mlp_hbm.at[peer], sems.at[peer]) for peer in range(16)]
    for copy in copies:
        copy.start()
    for part in range(16):
        head_out[pl.ds(part * 24, 24), pl.ds(0, LANES)] = rows_ref[part, pl.ds(0, 24), :]
        head_out[pl.ds(part * 24, 24), pl.ds(LANES, LANES)] = rows_ref[part, pl.ds(24, 24), :]
    for copy in copies:
        copy.wait()


def project(normed_ref, mine_ref, twin_ref, q_out, k_out, vt_out, up_out, down_out, bias_out):
    lower = lax.axis_index("xh") == 0
    first = jnp.where(lower, mine_ref[...], twin_ref[...])
    last = jnp.where(lower, twin_ref[...], mine_ref[...])
    weight = jnp.concatenate([first, last], axis=0)
    tops = []
    ends = []
    for tile in range(STRIPES):
        full = jnp.dot(normed_ref[tile, pl.ds(0, TOK), :], weight, preferred_element_type=F32)
        qk = full[:, :LANES]
        qk_t = jnp.transpose(qk)
        v_t = jnp.transpose(full[:, LANES:])[:HEAD]
        span = pl.ds(tile * TOK, TOK)
        q_out[:, span] = (qk_t[:HEAD] * HEAD ** (-0.5)).astype(BF)
        k_out[span, :] = qk[:, HEAD:].astype(BF)
        vt_out[:, span] = v_t.astype(BF)
        kv_t = jnp.concatenate([qk_t[HEAD:], v_t], axis=0)
        seen = jnp.broadcast_to(normed_ref[tile, pl.ds(TOK, 8), :LANES].astype(F32)[:1], (LANES, LANES))
        bias_out[:, span] = jnp.where(jnp.transpose(seen)[:STRIPES] > 0, 0.0, MASKED)
        tops.append(kv_t[:, :EDGE])
        ends.append(kv_t[:, TOK - EDGE :])
    for group in range(4):
        span = pl.ds(group * LANES, LANES)
        up_out[:, span] = jnp.concatenate(tops[group * 4 : group * 4 + 4], axis=1).astype(BF)
        down_out[:, span] = jnp.concatenate(ends[group * 4 : group * 4 + 4], axis=1).astype(BF)


def attend_strip(
    q_ref, k_ref, vt_ref, bias_ref, acc_out, max_out, sum_out, even_scores, odd_scores, even_top, odd_top
):
    def score_chunk(group, chunk, scores, top):
        span = pl.ds(pl.multiple_of(group * WIDE, WIDE), WIDE)
        part = jnp.dot(k_ref[pl.ds(chunk * WIDE, WIDE), :], q_ref[:, span], preferred_element_type=F32)
        for half in range(2):
            row = bias_ref[pl.ds(chunk * 2 + half, 1), span]
            piece = part[half * TOK : (half + 1) * TOK] + row
            scores[chunk, pl.ds(half * TOK, TOK), :] = piece
            best = jnp.max(piece.reshape(16, 8, WIDE), axis=0)
            top = best if top is None else jnp.maximum(top, best)
        return top

    def step(group, scores, top_ref, coming, next_scores, next_top):
        peak = jnp.max(top_ref[...], axis=0, keepdims=True)
        total = jnp.zeros((8, WIDE), F32)
        acc = jnp.zeros((HEAD, WIDE), F32)
        top = None
        for chunk in range(8):
            top = score_chunk(coming, chunk, next_scores, top)
            weights = jnp.exp(scores[chunk] - peak)
            total = total + jnp.sum(weights.reshape(32, 8, WIDE), axis=0)
            acc = acc + jnp.dot(
                vt_ref[:, pl.ds(chunk * WIDE, WIDE)], weights.astype(BF), preferred_element_type=F32
            )
        next_top[...] = top
        span = pl.ds(pl.multiple_of(group * WIDE, WIDE), WIDE)
        acc_out[:, span] = acc
        max_out[:, span] = jnp.broadcast_to(peak, (8, WIDE))
        sum_out[:, span] = jnp.broadcast_to(jnp.sum(total, axis=0, keepdims=True), (8, WIDE))

    top = None
    for chunk in range(8):
        top = score_chunk(0, chunk, even_scores, top)
    even_top[...] = top

    def pair(index, carry):
        first = index * 2
        step(first, even_scores, even_top, first + 1, odd_scores, odd_top)
        step(first + 1, odd_scores, odd_top, jnp.minimum(first + 2, 7), even_scores, even_top)
        return carry

    lax.fori_loop(0, 4, pair, 0)


def attend_edges(q_ref, above_ref, below_ref, acc_ref, max_ref, sum_ref, out_ref):
    row = lax.axis_index("xh") * 16 + lax.axis_index("z")
    key_band = lax.broadcasted_iota(jnp.int32, (LANES, 4 * TOK), 0) // EDGE
    query_band = lax.broadcasted_iota(jnp.int32, (LANES, 4 * TOK), 1) // TOK
    same = key_band == query_band
    for group in range(4):
        wide = slice(group * 4 * TOK, (group + 1) * 4 * TOK)
        keys = slice(group * LANES, (group + 1) * LANES)
        queries = q_ref[:, wide]
        scores = []
        for ref, flag in ((above_ref, row > 0), (below_ref, row < 31)):
            part = lax.dot_general(
                ref[:HEAD, keys], queries, (((0,), (0,)), ((), ())), preferred_element_type=F32
            )
            scores.append(jnp.where(same & flag, part, MASKED))
        old = max_ref[:1, wide]
        peak = jnp.maximum(old, jnp.max(jnp.maximum(scores[0], scores[1]), axis=0, keepdims=True))
        factor = jnp.exp(old - peak)
        acc = acc_ref[:, wide] * factor
        total = sum_ref[:1, wide] * factor
        for ref, part in ((above_ref, scores[0]), (below_ref, scores[1])):
            weights = jnp.exp(part - peak)
            total = total + jnp.sum(weights, axis=0, keepdims=True)
            acc = acc + jnp.dot(ref[HEAD:, keys], weights.astype(BF), preferred_element_type=F32)
        result = (acc / total).astype(BF)
        for index in range(4):
            out_ref[group * 4 + index] = result[:, index * TOK : (index + 1) * TOK]


def finish(ctx_ref, near_ref, far_ref, tokens_ref, valid_ref, gain_ref, out_ref):
    core = lax.axis_index("c")

    def run(even_ref, odd_ref):
        context_t = ctx_ref[pl.ds(0, HEADS)].reshape(D, TOK)
        context = jnp.transpose(context_t.astype(F32)).astype(BF)
        valid = valid_ref[...].astype(F32)

        def block(part, half, start, size):
            ref = odd_ref if part % 2 else even_ref
            return ref[half * 8 + part // 2, pl.ds(start, size), :]

        def into(rows, part):
            sides = []
            for unit in range(2):
                low = block(part, 0, unit * D // 2, D // 2)
                high = block(part, 1, unit * D // 2, D // 2)
                sides.append(jnp.concatenate([low, high], axis=0))
            return jnp.dot(rows, jnp.concatenate(sides, axis=1), preferred_element_type=F32)

        attended = jnp.concatenate([into(context, part) for part in range(6, 9)], axis=1)
        hidden = (tokens_ref[...].astype(F32) + valid * attended).astype(BF)
        residual = hidden.astype(F32)
        normed = norm_rows(residual, gain_ref[...].reshape(1, D)).astype(BF)
        inner = jnp.concatenate([jax.nn.gelu(into(normed, part)).astype(BF) for part in range(9, 15)], axis=1)
        for chunk in range(3):
            parts = (2 * chunk, 2 * chunk + 1)
            low = jnp.concatenate([block(part, 0, 0, D) for part in parts], axis=1)
            high = jnp.concatenate([block(part, 1, 0, D) for part in parts], axis=1)
            down = jnp.dot(inner, jnp.concatenate([low, high], axis=0), preferred_element_type=F32)
            span = slice(chunk * WIDE, (chunk + 1) * WIDE)
            out_ref[:, span] = (residual[:, span] + valid * down).astype(BF)

    @pl.when(core == 0)
    def _():
        run(near_ref, far_ref)

    @pl.when(core == 1)
    def _():
        run(far_ref, near_ref)


def body(tokens, patch_valid, block_mask, gain_attn, gain_mlp, w_qkv, w_out, w_up, w_down):
    lat_rows, lon_cols = tokens.shape[0], tokens.shape[1]
    own = tokens.reshape(TOK, D)
    normed, piece = pl.pallas_call(
        prepare,
        out_shape=(
            jax.ShapeDtypeStruct((TOK + 8, D), BF),
            jax.ShapeDtypeStruct((96, LANES), BF),
        ),
        in_specs=[whole()] * 7,
        out_specs=(whole(),) * 2,
        compiler_params=params(56),
        name="prepare",
    )(own, gain_attn, block_mask, w_qkv, w_out, w_up, w_down)
    strip = lax.all_gather(normed, LON, axis=0)
    rows = lax.all_gather(piece, "z", axis=0)
    mlp_rows, head_half = pl.pallas_call(
        sort_rows,
        out_shape=(
            jax.ShapeDtypeStruct((16, D, LANES), BF),
            jax.ShapeDtypeStruct((D // 2, 2 * LANES), BF),
        ),
        in_specs=[whole()],
        out_specs=(pl.BlockSpec(memory_space=pl.ANY), whole()),
        scratch_shapes=[pltpu.VMEM((D, LANES), BF), pltpu.SemaphoreType.DMA((16,))],
        compiler_params=params(56),
        name="sort_rows",
    )(rows)
    near = lax.all_to_all(mlp_rows, PLANE, 0, 0)
    twin = lax.ppermute(head_half, "xh", [(0, 1), (1, 0)])
    halo = jax.ShapeDtypeStruct((LANES, 4 * LANES), BF)
    keys = STRIPES * TOK
    q_t, k_n, v_t, to_up, to_down, bias = pl.pallas_call(
        project,
        out_shape=(
            jax.ShapeDtypeStruct((HEAD, keys), BF),
            jax.ShapeDtypeStruct((keys, HEAD), BF),
            jax.ShapeDtypeStruct((HEAD, keys), BF),
            halo,
            halo,
            jax.ShapeDtypeStruct((STRIPES, keys), F32),
        ),
        in_specs=[whole()] * 3,
        out_specs=(whole(),) * 6,
        compiler_params=params(14),
        cost_estimate=pl.CostEstimate(flops=2 * 2048 * 768 * 256, bytes_accessed=5 << 20, transcendentals=0),
        name="project",
    )(strip, head_half, twin)
    above = lax.ppermute(to_down, LAT, [(i, i + 1) for i in range(31)])
    below = lax.ppermute(to_up, LAT, [(i + 1, i) for i in range(31)])

    stat = jax.ShapeDtypeStruct((8, keys), F32)
    acc, peaks, sums = pl.pallas_call(
        attend_strip,
        out_shape=(jax.ShapeDtypeStruct((HEAD, keys), F32), stat, stat),
        in_specs=[whole()] * 4,
        out_specs=(whole(),) * 3,
        scratch_shapes=[
            pltpu.VMEM((8, WIDE, WIDE), F32),
            pltpu.VMEM((8, WIDE, WIDE), F32),
            pltpu.VMEM((8, WIDE), F32),
            pltpu.VMEM((8, WIDE), F32),
        ],
        compiler_params=params(14),
        cost_estimate=pl.CostEstimate(
            flops=4 * 2048 * 2048 * 256, bytes_accessed=3 << 20, transcendentals=2048 * 2048
        ),
        name="attend_strip",
    )(q_t, k_n, v_t, bias)

    context = pl.pallas_call(
        attend_edges,
        out_shape=jax.ShapeDtypeStruct((STRIPES, HEAD, TOK), BF),
        in_specs=[whole()] * 6,
        out_specs=whole(),
        compiler_params=params(8),
        name="attend_edges",
    )(q_t, above, below, acc, peaks, sums)

    near, context = lax.optimization_barrier((near, context))
    far = lax.ppermute(near, "c", [(0, 1), (1, 0)])
    mine = lax.all_to_all(context, LON, 0, 0)
    mixed = pl.pallas_call(
        finish,
        out_shape=jax.ShapeDtypeStruct((TOK, D), BF),
        in_specs=[whole()] * 6,
        out_specs=whole(),
        compiler_params=params(20),
        cost_estimate=pl.CostEstimate(flops=2 * 128 * 768 * 3840, bytes_accessed=7 << 20, transcendentals=128 * 1536),
        name="finish",
    )(mine, near, far, own, patch_valid.reshape(TOK, 1), gain_mlp)
    return mixed.reshape(lat_rows, lon_cols, D)


def solution(mesh):
    fine = Mesh(mesh.devices.reshape(4, 2, 2, 2, 16), ("y", "xl", "c", "xh", "z"))
    in_specs = (
        P(LAT, LON, None),
        P(LAT, LON),
        P(LAT, LON, None),
        P(),
        P(),
        P(LAT, None),
        P(LAT, None),
        P(LAT, None),
        P(LAT, None),
    )
    out_specs = P(LAT, LON, None)
    return jax.shard_map(body, mesh=fine, in_specs=in_specs, out_specs=out_specs, check_vma=False)
```

time: 134 us -> 148 us (1.10)
  the two profiles are of different devices: /device:TPU:1 before, /device:TPU:4 now
where the time goes in v3:
time: 148 us
  waiting for transfers between devices  47.3 us (32%)
  blocking collectives  40.1 us (27%)
  starting transfers between devices  24.5 us (17%)
  Pallas kernels  18.8 us (13%)
  between operations  13.5 us (9%)
  local copies, waits for them, and re-layouts  3.7 us (2%)
    all_gather x1, blocking collectives, body(): rows = lax.all_gather(piece, 'z', axis=0)  40.1 us
    ppermute x1, waiting for transfers between devices, body(): twin = lax.ppermute(head_half, 'xh', [(0, 1), (1, 0)])  39.3 us
    all_to_all x1, waiting for transfers between devices, body(): mine = lax.all_to_all(context, LON, 0, 0)  7.91 us
    all_to_all x1, starting transfers between devices, body(): near = lax.all_to_all(mlp_rows, PLANE, 0, 0)  7.6 us
    ppermute x1, starting transfers between devices, body(): below = lax.ppermute(to_up, LAT, [(i + 1, i) for i in range(31)])  7.54 us
    pallas_call x1, Pallas kernels, body(): pl.pallas_call(attend_strip, out_shape=(jax.ShapeDtypeStruct((HEAD, keys)...  6.21 us
    pallas_call x1, Pallas kernels, body(): pl.pallas_call(finish, out_shape=jax.ShapeDtypeStruct((TOK, D), BF), in_s...  4.07 us
    unnamed x12, local copies, waits for them, and re-layouts  3.61 us
  transfers between devices with their start and end apart: 7, of which 2 were waited for; matrix products, arithmetic and copies ran while one was open for 0% of the time, Pallas kernels for 9%

profile of v3, /device:TPU:4, one launch (start us, length us, event | category | flops | bytes accessed | tf_op | source)
XLA Modules:
  0.0 148.0 jit_solution(13117827655541314798)
XLA Ops:
  6.5 0.0 all-gather.4.cloned.1.call-start
  6.5 2.0 %prepare.1 = (bf16[136,768]{1,0:T(8,128)(2,1)}, bf16[96,128]{1,0:T(8,128)(2,1)}) custom-call(bf16[128,768]{1,0:T(8,128)(2,1)} %bitcast.5, f32[768]{0:T(1024)} %gain_ref.2, s32[1,1,16]{2,1,0:T(1,128)} %mask_ref.1, bf16[24,2304]{1,0:T(8,128)(2,1)} %qkv_ref.1, bf16[24,768]{1,0:T(8,128)(2,1)} %out_ref.1, bf16[24,1536]{1,0:T(8,128)(2,1)} %up_ref.1, ...), custom_call_target="tpu_custom_call" | custom-call | tf_op jit(solution)/shard_map/prepare/pallas_call | solution.py:255
  8.6 0.0 all-gather.4.cloned.1.call-update
  8.6 40.1 %all-gather = bf16[1536,128]{1,0:T(8,128)(2,1)} all-gather(bf16[96,128]{1,0:T(8,128)(2,1)} %get-tuple-element.20), channel_id=2, replica_groups=mesh['y'=4,'xl'=2,'c'=2,'xh'=2,'z'=16] {'z'}, dimensions={0}, use_global_device_ids=true | all-gather | bytes 417792 | tf_op jit(solution)/shard_map/all_gather | solution.py:267
  48.7 3.5 %sort_rows.1 = (bf16[16,768,128]{2,1,0:T(8,128)(2,1)}, bf16[384,256]{1,0:T(8,128)(2,1)}) custom-call(bf16[16,96,128]{2,1,0:T(8,128)(2,1)} %bitcast.7), custom_call_target="tpu_custom_call" | custom-call | tf_op jit(solution)/shard_map/sort_rows/pallas_call | solution.py:268
  52.2 0.0 copy-start.3
  52.2 7.6 %all-to-all-start = ((bf16[16,768,128]{2,1,0:T(8,128)(2,1)}), bf16[16,768,128]{2,1,0:T(8,128)(2,1)S(1)}, u32[]{:S(2)}, u32[]{:S(2)}) async-start(bf16[16,768,128]{2,1,0:T(8,128)(2,1)} %get-tuple-element.21), calls=%async_computation | async-start | bytes 6291456 | tf_op jit(solution)/shard_map/all_to_all | solution.py:280
  59.9 0.0 copy-done.3
  59.9 2.0 %collective-permute-start = (bf16[384,256]{1,0:T(8,128)(2,1)S(1)}, bf16[384,256]{1,0:T(8,128)(2,1)S(1)}, u32[]{:S(2)}, u32[]{:S(2)}) collective-permute-start(bf16[384,256]{1,0:T(8,128)(2,1)S(1)} %copy-done.3), channel_id=1, source_target_pairs={{0,16},{16,0},{1,17},{17,1},{2,18},{18,2},{3,19},{19,3},{4,20},{20... | collective-permute-start | bytes 589832 | tf_op jit(solution)/shard_map/ppermute | solution.py:281
  61.9 39.3 %collective-permute-done.twin_ref = bf16[384,256]{1,0:T(8,128)(2,1)S(1)} collective-permute-done((bf16[384,256]{1,0:T(8,128)(2,1)S(1)}, bf16[384,256]{1,0:T(8,128)(2,1)S(1)}, u32[]{:S(2)}, u32[]{:S(2)}) %collective-permute-start) | collective-permute-done | bytes 196640 | tf_op jit(solution)/shard_map/ppermute | solution.py:281
  101.2 1.9 %copy-done = bf16[2176,768]{1,0:T(8,128)(2,1)S(1)} copy-done((bf16[2176,768]{1,0:T(8,128)(2,1)S(1)}, bf16[2176,768]{1,0:T(8,128)(2,1)}, u32[]{:S(2)}) %copy-start) | copy-done | bytes 3342360
  103.2 1.5 %project.1 = (bf16[64,2048]{1,0:T(8,128)(2,1)S(1)}, bf16[2048,64]{1,0:T(8,128)(2,1)S(1)}, bf16[64,2048]{1,0:T(8,128)(2,1)S(1)}, bf16[128,512]{1,0:T(8,128)(2,1)S...) custom-call(bf16[16,136,768]{2,1,0:T(8,128)(2,1)S(1)} %bitcast.4, bf16[384,256]{1,0:T(8,128)(2,1)S(1)} %copy-done.3, ...), custom_call_target="tpu_custom_call" | custom-call | flops 805306368 | bytes 5242880 | tf_op jit(solution)/shard_map/project/pallas_call | solution.py:284
  104.7 1.9 %collective-permute-start.1 = (bf16[128,512]{1,0:T(8,128)(2,1)S(1)}, bf16[128,512]{1,0:T(8,128)(2,1)S(1)}, u32[]{:S(2)}, u32[]{:S(2)}) collective-permute-start(bf16[128,512]{1,0:T(8,128)(2,1)S(1)} %get-tuple-element.25), channel_id=1, source_target_pairs={{0,1},{1,2},{2,3},{3,4},{4,5},{5,6},{6,7},{7,8},{8,9},{9,10},{10,1... | collective-permute-start | bytes 393224 | tf_op jit(solution)/shard_map/ppermute | solution.py:300
  106.6 7.5 %collective-permute-start.2 = (bf16[128,512]{1,0:T(8,128)(2,1)S(1)}, bf16[128,512]{1,0:T(8,128)(2,1)S(1)}, u32[]{:S(2)}, u32[]{:S(2)}) collective-permute-start(bf16[128,512]{1,0:T(8,128)(2,1)S(1)} %get-tuple-element.26), channel_id=1, source_target_pairs={{1,0},{2,1},{3,2},{4,3},{5,4},{6,5},{7,6},{8,7},{9,8},{10,9},{11,1... | collective-permute-start | bytes 393224 | tf_op jit(solution)/shard_map/ppermute | solution.py:301
  114.2 0.0 copy-start.5
  114.2 0.0 copy-start.4
  114.2 6.2 %attend_strip.1 = (f32[64,2048]{1,0:T(8,128)S(1)}, f32[8,2048]{1,0:T(8,128)S(1)}, f32[8,2048]{1,0:T(8,128)S(1)}) custom-call(bf16[64,2048]{1,0:T(8,128)(2,1)S(1)} %get-tuple-element.24.q_ref, bf16[2048,64]{1,0:T(8,128)(2,1)S(1)} %get-tuple-element.27.k_ref, bf16[64,2048]{1,0:T(8,128)(2,1)S(1)} %get-tuple-element.28.vt_ref, ...), custom_call_target="tpu_custom_call" | custom-call | flops 4294967296 | bytes 3145728 | tf_op jit(solution)/shard_map/attend_strip/pallas_call | solution.py:304
  120.4 0.0 collective-permute-done.1.above_ref
  120.4 0.0 collective-permute-done.2.below_ref
  120.5 1.4 attend_edges.1
  121.9 0.0 copy-start.1
  121.9 0.7 copy-done.1
  122.6 0.0 all-to-all-done.near_ref
  122.6 1.9 %collective-permute-start.3 = (bf16[16,768,128]{2,1,0:T(8,128)(2,1)S(1)}, bf16[16,768,128]{2,1,0:T(8,128)(2,1)}, u32[]{:S(2)}, u32[]{:S(2)}) collective-permute-start(bf16[16,768,128]{2,1,0:T(8,128)(2,1)S(1)} %all-to-all-done.near_ref), channel_id=1, source_target_pairs={{0,32},{32,0},{1,33},{33,1},{2,34},{34,2},{3,35},{35,3},{4,36},{36... | collective-permute-start | bytes 9437192 | tf_op jit(solution)/shard_map/ppermute | solution.py:332
  124.5 3.5 %all-to-all-start.1 = ((bf16[16,64,128]{2,1,0:T(8,128)(2,1)}), bf16[16,64,128]{2,1,0:T(8,128)(2,1)S(1)}, u32[]{:S(2)}, u32[]{:S(2)}) async-start(bf16[16,64,128]{2,1,0:T(8,128)(2,1)} %copy-done.1), calls=%async_computation.1 | async-start | bytes 524288 | tf_op jit(solution)/shard_map/all_to_all | solution.py:333
  128.1 0.0 copy-done.5
  128.1 0.1 reshape.14.valid_ref
  128.2 7.9 %all-to-all-done.1.ctx_ref = bf16[16,64,128]{2,1,0:T(8,128)(2,1)S(1)} async-done(((bf16[16,64,128]{2,1,0:T(8,128)(2,1)}), bf16[16,64,128]{2,1,0:T(8,128)(2,1)S(1)}, u32[]{:S(2)}, u32[]{:S(2)}) %all-to-all-start.1) | async-done | bytes 262176 | tf_op jit(solution)/shard_map/all_to_all | solution.py:333
  136.1 0.0 collective-permute-done.3.far_ref
  136.1 0.0 copy-done.4
  136.1 0.9 copy-done.2
  137.0 4.1 %finish.1 = bf16[128,768]{1,0:T(8,128)(2,1)} custom-call(bf16[16,64,128]{2,1,0:T(8,128)(2,1)S(1)} %all-to-all-done.1.ctx_ref, bf16[16,768,128]{2,1,0:T(8,128)(2,1)S(1)} %all-to-all-done.near_ref, bf16[16,768,128]{2,1,0:T(8,128)(2,1)} %collective-permute-done.3.far_ref, bf16[128,768]{1,0:T(8,128)(2,1)S(1)} %bitcast.6, s32[128,1]{1,0:T(8,128)S(1)} %reshape.14.valid_ref, ...), custom_call_target="tpu_custom_call" | custom-call | flops 754974720 | bytes 7340032 | tf_op jit(solution)/shard_map/finish/pallas_call | solution.py:334
  (3 shorter events, 0.0 us)
Async XLA Ops:
  6.5 94.7 %all-gather.4.cloned.1.call-start = ((), (), s32[]{:S(2)}) async-start(), calls=%async_computation.2 | async-start | bytes 3551232 | tf_op jit(solution)/shard_map/all_gather | solution.py:266
  52.2 7.6 %copy-start.3 = (bf16[384,256]{1,0:T(8,128)(2,1)S(1)}, bf16[384,256]{1,0:T(8,128)(2,1)}, u32[]{:S(2)}) copy-start(bf16[384,256]{1,0:T(8,128)(2,1)} %get-tuple-element.23.mine_ref) | copy-start | bytes 589828
  52.2 70.4 %all-to-all-start = ((bf16[16,768,128]{2,1,0:T(8,128)(2,1)}), bf16[16,768,128]{2,1,0:T(8,128)(2,1)S(1)}, u32[]{:S(2)}, u32[]{:S(2)}) async-start(bf16[16,768,128]{2,1,0:T(8,128)(2,1)} %get-tuple-element.21), calls=%async_computation | async-start | bytes 6291456 | tf_op jit(solution)/shard_map/all_to_all | solution.py:280
  59.9 41.4 %collective-permute-start = (bf16[384,256]{1,0:T(8,128)(2,1)S(1)}, bf16[384,256]{1,0:T(8,128)(2,1)S(1)}, u32[]{:S(2)}, u32[]{:S(2)}) collective-permute-start(bf16[384,256]{1,0:T(8,128)(2,1)S(1)} %copy-done.3), channel_id=1, source_target_pairs={{0,16},{16,0},{1,17},{17,1},{2,18},{18,2},{3,19},{19,3},{4,20},{20... | collective-permute-start | bytes 589832 | tf_op jit(solution)/shard_map/ppermute | solution.py:281
  101.2 1.9 %copy-start = (bf16[2176,768]{1,0:T(8,128)(2,1)S(1)}, bf16[2176,768]{1,0:T(8,128)(2,1)}, u32[]{:S(2)}) copy-start(bf16[2176,768]{1,0:T(8,128)(2,1)} %all-gather.4.cloned.1.call-done) | copy-start | bytes 10027012
  104.7 15.7 %collective-permute-start.1 = (bf16[128,512]{1,0:T(8,128)(2,1)S(1)}, bf16[128,512]{1,0:T(8,128)(2,1)S(1)}, u32[]{:S(2)}, u32[]{:S(2)}) collective-permute-start(bf16[128,512]{1,0:T(8,128)(2,1)S(1)} %get-tuple-element.25), channel_id=1, source_target_pairs={{0,1},{1,2},{2,3},{3,4},{4,5},{5,6},{6,7},{7,8},{8,9},{9,10},{10,1... | collective-permute-start | bytes 393224 | tf_op jit(solution)/shard_map/ppermute | solution.py:300
  106.6 13.8 %collective-permute-start.2 = (bf16[128,512]{1,0:T(8,128)(2,1)S(1)}, bf16[128,512]{1,0:T(8,128)(2,1)S(1)}, u32[]{:S(2)}, u32[]{:S(2)}) collective-permute-start(bf16[128,512]{1,0:T(8,128)(2,1)S(1)} %get-tuple-element.26), channel_id=1, source_target_pairs={{1,0},{2,1},{3,2},{4,3},{5,4},{6,5},{7,6},{8,7},{9,8},{10,9},{11,1... | collective-permute-start | bytes 393224 | tf_op jit(solution)/shard_map/ppermute | solution.py:301
  114.2 13.9 %copy-start.5 = (s32[8,16]{1,0:T(8,128)S(1)}, s32[8,16]{1,0:T(8,128)}, u32[]{:S(2)}) copy-start(s32[8,16]{1,0:T(8,128)} %param.10) | copy-start | bytes 1540
  114.2 21.9 %copy-start.4 = (f32[768]{0:T(1024)S(1)}, f32[768]{0:T(1024)}, u32[]{:S(2)}) copy-start(f32[768]{0:T(1024)} %gain_ref.3) | copy-start | bytes 9220
  121.9 0.7 copy-start.1
  122.6 13.5 %collective-permute-start.3 = (bf16[16,768,128]{2,1,0:T(8,128)(2,1)S(1)}, bf16[16,768,128]{2,1,0:T(8,128)(2,1)}, u32[]{:S(2)}, u32[]{:S(2)}) collective-permute-start(bf16[16,768,128]{2,1,0:T(8,128)(2,1)S(1)} %all-to-all-done.near_ref), channel_id=1, source_target_pairs={{0,32},{32,0},{1,33},{33,1},{2,34},{34,2},{3,35},{35,3},{4,36},{36... | collective-permute-start | bytes 9437192 | tf_op jit(solution)/shard_map/ppermute | solution.py:332
  124.5 11.6 %all-to-all-start.1 = ((bf16[16,64,128]{2,1,0:T(8,128)(2,1)}), bf16[16,64,128]{2,1,0:T(8,128)(2,1)S(1)}, u32[]{:S(2)}, u32[]{:S(2)}) async-start(bf16[16,64,128]{2,1,0:T(8,128)(2,1)} %copy-done.1), calls=%async_computation.1 | async-start | bytes 524288 | tf_op jit(solution)/shard_map/all_to_all | solution.py:333
  136.1 0.9 copy-start.2
Sparse Core Ops, SparseCore 0:
  9.5 50.1 all-gather.3

commit v4 on v3

--- a/solution.py
+++ b/solution.py
@@ -16,9 +16,10 @@
 LANES = 128
 EDGE = 32
 WIDE = 256
+SPLIT = 480
 MASKED = -1e30
 LON = ("y", "xl", "c")
-PLANE = ("xh", "y", "xl")
+CHIPS = ("y", "xl")
 LAT = ("xh", "z")
 BF = jnp.bfloat16
 F32 = jnp.float32
@@ -37,6 +38,10 @@
 
 def whole():
     return pl.BlockSpec(memory_space=pltpu.VMEM)
+
+
+def lon_place():
+    return (lax.axis_index("y") * 2 + lax.axis_index("xl")) * 2 + lax.axis_index("c")
 
 
 def prepare(tokens_ref, gain_ref, mask_ref, qkv_ref, out_ref, up_ref, down_ref, norm_out, piece_out):
@@ -46,7 +51,7 @@
     seen = jnp.broadcast_to(mask_ref[0].astype(F32), (8, STRIPES))
     norm_out[pl.ds(TOK, 8), :] = jnp.concatenate([seen, jnp.zeros((8, D - STRIPES), F32)], axis=1).astype(BF)
 
-    place_j = (lax.axis_index("y") * 2 + lax.axis_index("xl")) * 2 + lax.axis_index("c")
+    place_j = lon_place()
     head = lax.rem(place_j, HEADS)
     block = head // 2
     odd = lax.rem(head, 2) == 1
@@ -81,39 +86,61 @@
         fill(up_ref[:, pl.ds(start, LANES)], up_ref[:, pl.ds(start + LANES, LANES)])
 
 
-def sort_rows(rows_ref, mlp_hbm, head_out, mlp_rows, sems):
-    place_j = (lax.axis_index("y") * 2 + lax.axis_index("xl")) * 2 + lax.axis_index("c")
+def sort_gather(rows_ref, order_ref, gather_out):
+    place_j = lon_place()
+    xh = lax.axis_index("xh")
 
     @pl.when(place_j < 6)
     def _():
-        for part in range(16):
-            mlp_rows[pl.ds(part * 48, 48), :] = rows_ref[part, pl.ds(48, 48), :]
+        for part in range(SPLIT // 48):
+            gather_out[pl.ds(part * 48, 48), :] = rows_ref[part % 16, xh, pl.ds(48, 48), :]
 
     @pl.when(place_j >= 6)
     def _():
-        for part in range(16):
-            mlp_rows[pl.ds(part * 24, 24), :] = rows_ref[part, pl.ds(48, 24), :]
-            mlp_rows[pl.ds(D // 2 + part * 24, 24), :] = rows_ref[part, pl.ds(72, 24), :]
-
-    copies = [pltpu.make_async_copy(mlp_rows, mlp_hbm.at[peer], sems.at[peer]) for peer in range(16)]
+        for part in range(SPLIT // 24):
+            source = rows_ref.at[part % 16, (part // 16) ^ xh]
+            gather_out[pl.ds(part * 24, 24), :] = source[pl.ds(48, 24), :]
+
+
+def sort_spread(rows_ref, spread_hbm, rest, sems):
+    place_j = lon_place()
+    xh = lax.axis_index("xh")
+
+    @pl.when(place_j < 6)
+    def _():
+        for part in range(SPLIT // 48, 32):
+            source = rows_ref.at[part % 16, (part // 16) ^ xh]
+            rest[pl.ds(part * 48 - SPLIT, 48), :] = source[pl.ds(48, 48), :]
+
+    @pl.when(place_j >= 6)
+    def _():
+        for part in range(32):
+            source = rows_ref.at[part % 16, (part // 16) ^ xh]
+            if part * 24 >= SPLIT:
+                rest[pl.ds(part * 24 - SPLIT, 24), :] = source[pl.ds(48, 24), :]
+            rest[pl.ds(D - SPLIT + part * 24, 24), :] = source[pl.ds(72, 24), :]
+
+    copies = [pltpu.make_async_copy(rest, spread_hbm.at[peer], sems.at[peer]) for peer in range(8)]
     for copy in copies:
         copy.start()
-    for part in range(16):
-        head_out[pl.ds(part * 24, 24), pl.ds(0, LANES)] = rows_ref[part, pl.ds(0, 24), :]
-        head_out[pl.ds(part * 24, 24), pl.ds(LANES, LANES)] = rows_ref[part, pl.ds(24, 24), :]
     for copy in copies:
         copy.wait()
 
 
-def project(normed_ref, mine_ref, twin_ref, q_out, k_out, vt_out, up_out, down_out, bias_out):
-    lower = lax.axis_index("xh") == 0
-    first = jnp.where(lower, mine_ref[...], twin_ref[...])
-    last = jnp.where(lower, twin_ref[...], mine_ref[...])
-    weight = jnp.concatenate([first, last], axis=0)
+def sort_head(rows_ref, head_out):
+    xh = lax.axis_index("xh")
+    for part in range(32):
+        source = rows_ref.at[part % 16, (part // 16) ^ xh]
+        head_out[pl.ds(part * 24, 24), pl.ds(0, LANES)] = source[pl.ds(0, 24), :]
+        head_out[pl.ds(part * 24, 24), pl.ds(LANES, LANES)] = source[pl.ds(24, 24), :]
+
+
+def project(strip_ref, weight_ref, q_out, k_out, vt_out, up_out, down_out, bias_out):
+    weight = weight_ref[...]
     tops = []
     ends = []
     for tile in range(STRIPES):
-        full = jnp.dot(normed_ref[tile, pl.ds(0, TOK), :], weight, preferred_element_type=F32)
+        full = jnp.dot(strip_ref[tile, pl.ds(0, TOK), :], weight, preferred_element_type=F32)
         qk = full[:, :LANES]
         qk_t = jnp.transpose(qk)
         v_t = jnp.transpose(full[:, LANES:])[:HEAD]
@@ -122,7 +149,7 @@
         k_out[span, :] = qk[:, HEAD:].astype(BF)
         vt_out[:, span] = v_t.astype(BF)
         kv_t = jnp.concatenate([qk_t[HEAD:], v_t], axis=0)
-        seen = jnp.broadcast_to(normed_ref[tile, pl.ds(TOK, 8), :LANES].astype(F32)[:1], (LANES, LANES))
+        seen = jnp.broadcast_to(strip_ref[tile, pl.ds(TOK, 8), :LANES].astype(F32)[:1], (LANES, LANES))
         bias_out[:, span] = jnp.where(jnp.transpose(seen)[:STRIPES] > 0, 0.0, MASKED)
         tops.append(kv_t[:, :EDGE])
         ends.append(kv_t[:, TOK - EDGE :])
@@ -207,7 +234,7 @@
             out_ref[group * 4 + index] = result[:, index * TOK : (index + 1) * TOK]
 
 
-def finish(ctx_ref, near_ref, far_ref, tokens_ref, valid_ref, gain_ref, out_ref):
+def finish(ctx_ref, gather_ref, near_ref, far_ref, tokens_ref, valid_ref, gain_ref, out_ref):
     core = lax.axis_index("c")
 
     def run(even_ref, odd_ref):
@@ -215,17 +242,15 @@
         context = jnp.transpose(context_t.astype(F32)).astype(BF)
         valid = valid_ref[...].astype(F32)
 
-        def block(part, half, start, size):
+        def column(part):
             ref = odd_ref if part % 2 else even_ref
-            return ref[half * 8 + part // 2, pl.ds(start, size), :]
+            return [gather_ref[part], ref[part // 2]]
 
         def into(rows, part):
-            sides = []
-            for unit in range(2):
-                low = block(part, 0, unit * D // 2, D // 2)
-                high = block(part, 1, unit * D // 2, D // 2)
-                sides.append(jnp.concatenate([low, high], axis=0))
-            return jnp.dot(rows, jnp.concatenate(sides, axis=1), preferred_element_type=F32)
+            head, rest = column(part)
+            left = jnp.concatenate([head, rest[: D - SPLIT]], axis=0)
+            weight = jnp.concatenate([left, rest[D - SPLIT :]], axis=1)
+            return jnp.dot(rows, weight, preferred_element_type=F32)
 
         attended = jnp.concatenate([into(context, part) for part in range(6, 9)], axis=1)
         hidden = (tokens_ref[...].astype(F32) + valid * attended).astype(BF)
@@ -233,10 +258,10 @@
         normed = norm_rows(residual, gain_ref[...].reshape(1, D)).astype(BF)
         inner = jnp.concatenate([jax.nn.gelu(into(normed, part)).astype(BF) for part in range(9, 15)], axis=1)
         for chunk in range(3):
-            parts = (2 * chunk, 2 * chunk + 1)
-            low = jnp.concatenate([block(part, 0, 0, D) for part in parts], axis=1)
-            high = jnp.concatenate([block(part, 1, 0, D) for part in parts], axis=1)
-            down = jnp.dot(inner, jnp.concatenate([low, high], axis=0), preferred_element_type=F32)
+            weight = jnp.concatenate(
+                [jnp.concatenate(column(2 * chunk + side), axis=0) for side in range(2)], axis=1
+            )
+            down = jnp.dot(inner, weight, preferred_element_type=F32)
             span = slice(chunk * WIDE, (chunk + 1) * WIDE)
             out_ref[:, span] = (residual[:, span] + valid * down).astype(BF)
 
@@ -263,22 +288,37 @@
         compiler_params=params(56),
         name="prepare",
     )(own, gain_attn, block_mask, w_qkv, w_out, w_up, w_down)
+    twin = lax.ppermute(piece, "xh", [(0, 1), (1, 0)])
     strip = lax.all_gather(normed, LON, axis=0)
-    rows = lax.all_gather(piece, "z", axis=0)
-    mlp_rows, head_half = pl.pallas_call(
-        sort_rows,
-        out_shape=(
-            jax.ShapeDtypeStruct((16, D, LANES), BF),
-            jax.ShapeDtypeStruct((D // 2, 2 * LANES), BF),
-        ),
+    both = jnp.stack([piece, twin])
+    rows = lax.all_gather(both, "z", axis=0)
+    spread_rows = pl.pallas_call(
+        sort_spread,
+        out_shape=jax.ShapeDtypeStruct((8, FFW - SPLIT, LANES), BF),
         in_specs=[whole()],
-        out_specs=(pl.BlockSpec(memory_space=pl.ANY), whole()),
-        scratch_shapes=[pltpu.VMEM((D, LANES), BF), pltpu.SemaphoreType.DMA((16,))],
+        out_specs=pl.BlockSpec(memory_space=pl.ANY),
+        scratch_shapes=[pltpu.VMEM((FFW - SPLIT, LANES), BF), pltpu.SemaphoreType.DMA((8,))],
         compiler_params=params(56),
-        name="sort_rows",
+        name="sort_spread",
     )(rows)
-    near = lax.all_to_all(mlp_rows, PLANE, 0, 0)
-    twin = lax.ppermute(head_half, "xh", [(0, 1), (1, 0)])
+    near = lax.all_to_all(spread_rows, CHIPS, 0, 0)
+    gather_rows = pl.pallas_call(
+        sort_gather,
+        out_shape=jax.ShapeDtypeStruct((SPLIT, LANES), BF),
+        in_specs=[whole(), pl.BlockSpec(memory_space=pl.ANY)],
+        out_specs=whole(),
+        compiler_params=params(56),
+        name="sort_gather",
+    )(rows, spread_rows)
+    gathered = lax.all_gather(gather_rows, LON, axis=0)
+    head_w = pl.pallas_call(
+        sort_head,
+        out_shape=jax.ShapeDtypeStruct((D, 2 * LANES), BF),
+        in_specs=[whole()],
+        out_specs=whole(),
+        compiler_params=params(56),
+        name="sort_head",
+    )(rows)
     halo = jax.ShapeDtypeStruct((LANES, 4 * LANES), BF)
     keys = STRIPES * TOK
     q_t, k_n, v_t, to_up, to_down, bias = pl.pallas_call(
@@ -291,12 +331,12 @@
             halo,
             jax.ShapeDtypeStruct((STRIPES, keys), F32),
         ),
-        in_specs=[whole()] * 3,
+        in_specs=[whole()] * 2,
         out_specs=(whole(),) * 6,
         compiler_params=params(14),
         cost_estimate=pl.CostEstimate(flops=2 * 2048 * 768 * 256, bytes_accessed=5 << 20, transcendentals=0),
         name="project",
-    )(strip, head_half, twin)
+    )(strip, head_w)
     above = lax.ppermute(to_down, LAT, [(i, i + 1) for i in range(31)])
     below = lax.ppermute(to_up, LAT, [(i + 1, i) for i in range(31)])
 
@@ -334,12 +374,12 @@
     mixed = pl.pallas_call(
         finish,
         out_shape=jax.ShapeDtypeStruct((TOK, D), BF),
-        in_specs=[whole()] * 6,
+        in_specs=[whole()] * 7,
         out_specs=whole(),
         compiler_params=params(20),
         cost_estimate=pl.CostEstimate(flops=2 * 128 * 768 * 3840, bytes_accessed=7 << 20, transcendentals=128 * 1536),
         name="finish",
-    )(mine, near, far, own, patch_valid.reshape(TOK, 1), gain_mlp)
+    )(mine, gathered, near, far, own, patch_valid.reshape(TOK, 1), gain_mlp)
     return mixed.reshape(lat_rows, lon_cols, D)
 
 

time: 148 us -> 125 us (0.84)
  the two profiles are of different devices: /device:TPU:4 before, /device:TPU:1 now
where the time goes in v4:
time: 125 us; the launch traced here: 124 us
  blocking collectives  36.1 us (29%)
  starting transfers between devices  33.2 us (27%)
  Pallas kernels  22.1 us (18%)
  waiting for transfers between devices  13.8 us (11%)
  between operations  13.5 us (11%)
  local copies, waits for them, and re-layouts  4.58 us (4%)
    all_gather x1, blocking collectives, body(): rows = lax.all_gather(both, 'z', axis=0)  36.1 us
    ppermute x1, starting transfers between devices, body(): far = lax.ppermute(near, 'c', [(0, 1), (1, 0)])  16.5 us
    all_gather x1, waiting for transfers between devices, body(): gathered = lax.all_gather(gather_rows, LON, axis=0)  12.3 us
    pallas_call x1, Pallas kernels, body(): pl.pallas_call(attend_strip, out_shape=(jax.ShapeDtypeStruct((HEAD, keys)...  6.22 us
    ppermute x1, starting transfers between devices, body(): twin = lax.ppermute(piece, 'xh', [(0, 1), (1, 0)])  5.48 us
    all_to_all x1, starting transfers between devices, body(): near = lax.all_to_all(spread_rows, CHIPS, 0, 0)  5.12 us
    unnamed x12, local copies, waits for them, and re-layouts  4.5 us
    pallas_call x1, Pallas kernels, body(): pl.pallas_call(finish, out_shape=jax.ShapeDtypeStruct((TOK, D), BF), in_s...  3.79 us
  transfers between devices with their start and end apart: 8, of which 2 were waited for; matrix products, arithmetic and copies ran while one was open for 1% of the time, Pallas kernels for 13%

profile of v4, /device:TPU:1, one launch (start us, length us, event | category | flops | bytes accessed | tf_op | source)
XLA Modules:
  0.0 124.0 jit_solution(7759694276614511490)
XLA Ops:
  6.5 2.1 %prepare.1 = (bf16[136,768]{1,0:T(8,128)(2,1)}, bf16[96,128]{1,0:T(8,128)(2,1)}) custom-call(bf16[128,768]{1,0:T(8,128)(2,1)} %bitcast.9, f32[768]{0:T(1024)} %gain_ref.2, s32[1,1,16]{2,1,0:T(1,128)} %mask_ref.1, bf16[24,2304]{1,0:T(8,128)(2,1)} %qkv_ref.1, bf16[24,768]{1,0:T(8,128)(2,1)} %out_ref.1, bf16[24,1536]{1,0:T(8,128)(2,1)} %up_ref.1, ...), custom_call_target="tpu_custom_call" | custom-call | tf_op jit(solution)/shard_map/prepare/pallas_call | solution.py:280
  8.6 0.0 all-gather.6.cloned.1.call-update
  8.6 5.5 %collective-permute-start = (bf16[96,128]{1,0:T(8,128)(2,1)}, bf16[96,128]{1,0:T(8,128)(2,1)S(1)}, u32[]{:S(2)}, u32[]{:S(2)}) collective-permute-start(bf16[96,128]{1,0:T(8,128)(2,1)} %get-tuple-element.18), channel_id=1, source_target_pairs={{0,16},{16,0},{1,17},{17,1},{2,18},{18,2},{3,19},{19,3},{4,20},{20... | collective-permute-start | bytes 73736 | tf_op jit(solution)/shard_map/ppermute | solution.py:291
  14.1 1.4 %collective-permute-done = bf16[96,128]{1,0:T(8,128)(2,1)S(1)} collective-permute-done((bf16[96,128]{1,0:T(8,128)(2,1)}, bf16[96,128]{1,0:T(8,128)(2,1)S(1)}, u32[]{:S(2)}, u32[]{:S(2)}) %collective-permute-start) | collective-permute-done | bytes 24608 | tf_op jit(solution)/shard_map/ppermute | solution.py:291
  15.5 0.7 pad_maximum_fusion
  16.3 36.1 %all-gather = bf16[32,96,128]{2,1,0:T(8,128)(2,1)} all-gather(bf16[2,96,128]{2,1,0:T(8,128)(2,1)S(1)} %pad_maximum_fusion), channel_id=2, replica_groups=mesh['y'=4,'xl'=2,'c'=2,'xh'=2,'z'=16] {'z'}, dimensions={0}, use_global_device_ids=true | all-gather | bytes 835584 | tf_op jit(solution)/shard_map/all_gather | solution.py:294
  52.4 2.6 %sort_spread.1.order_ref = bf16[8,1056,128]{2,1,0:T(8,128)(2,1)} custom-call(bf16[16,2,96,128]{3,2,1,0:T(8,128)(2,1)} %bitcast.11), custom_call_target="tpu_custom_call" | custom-call | tf_op jit(solution)/shard_map/sort_spread/pallas_call | solution.py:295
  55.0 5.1 %all-to-all-start = ((bf16[8,1056,128]{2,1,0:T(8,128)(2,1)}), bf16[8,1056,128]{2,1,0:T(8,128)(2,1)S(1)}, u32[]{:S(2)}, u32[]{:S(2)}) async-start(bf16[8,1056,128]{2,1,0:T(8,128)(2,1)} %sort_spread.1.order_ref), calls=%async_computation | async-start | bytes 4325376 | tf_op jit(solution)/shard_map/all_to_all | solution.py:304
  60.1 0.0 all-gather.8.cloned.1.call-start
  60.1 1.8 %sort_gather.1 = bf16[480,128]{1,0:T(8,128)(2,1)} custom-call(bf16[16,2,96,128]{3,2,1,0:T(8,128)(2,1)} %bitcast.12, bf16[8,1056,128]{2,1,0:T(8,128)(2,1)} %sort_spread.1.order_ref), custom_call_target="tpu_custom_call" | custom-call | tf_op jit(solution)/shard_map/sort_gather/pallas_call | solution.py:305
  61.9 0.0 all-gather.8.cloned.1.call-update
  62.0 2.0 %sort_head.1.weight_ref = bf16[768,256]{1,0:T(8,128)(2,1)} custom-call(bf16[16,2,96,128]{3,2,1,0:T(8,128)(2,1)} %bitcast.13), custom_call_target="tpu_custom_call" | custom-call | tf_op jit(solution)/shard_map/sort_head/pallas_call | solution.py:314
  63.9 1.9 %copy-done = bf16[2176,768]{1,0:T(8,128)(2,1)S(1)} copy-done((bf16[2176,768]{1,0:T(8,128)(2,1)S(1)}, bf16[2176,768]{1,0:T(8,128)(2,1)}, u32[]{:S(2)}) %copy-start) | copy-done | bytes 3342360
  65.9 1.0 copy-done.2
  66.9 1.5 %project.1 = (bf16[64,2048]{1,0:T(8,128)(2,1)S(1)}, bf16[2048,64]{1,0:T(8,128)(2,1)S(1)}, bf16[64,2048]{1,0:T(8,128)(2,1)S(1)}, bf16[128,512]{1,0:T(8,128)(2,1)S...) custom-call(bf16[16,136,768]{2,1,0:T(8,128)(2,1)S(1)} %bitcast.7, bf16[768,256]{1,0:T(8,128)(2,1)S(1)} %copy-done.2), custom_call_target="tpu_custom_call" | custom-call | flops 805306368 | bytes 5242880 | tf_op jit(solution)/shard_map/project/pallas_call | solution.py:324
  68.4 1.3 %collective-permute-start.1 = (bf16[128,512]{1,0:T(8,128)(2,1)S(1)}, bf16[128,512]{1,0:T(8,128)(2,1)S(1)}, u32[]{:S(2)}, u32[]{:S(2)}) collective-permute-start(bf16[128,512]{1,0:T(8,128)(2,1)S(1)} %get-tuple-element.21), channel_id=1, source_target_pairs={{0,1},{1,2},{2,3},{3,4},{4,5},{5,6},{6,7},{7,8},{8,9},{9,10},{10,1... | collective-permute-start | bytes 393224 | tf_op jit(solution)/shard_map/ppermute | solution.py:340
  69.7 1.3 %collective-permute-start.2 = (bf16[128,512]{1,0:T(8,128)(2,1)S(1)}, bf16[128,512]{1,0:T(8,128)(2,1)S(1)}, u32[]{:S(2)}, u32[]{:S(2)}) collective-permute-start(bf16[128,512]{1,0:T(8,128)(2,1)S(1)} %get-tuple-element.22), channel_id=1, source_target_pairs={{1,0},{2,1},{3,2},{4,3},{5,4},{6,5},{7,6},{8,7},{9,8},{10,9},{11,1... | collective-permute-start | bytes 393224 | tf_op jit(solution)/shard_map/ppermute | solution.py:341
  71.0 0.0 copy-start.5
  71.0 0.0 copy-start.4
  71.0 6.2 %attend_strip.1 = (f32[64,2048]{1,0:T(8,128)S(1)}, f32[8,2048]{1,0:T(8,128)S(1)}, f32[8,2048]{1,0:T(8,128)S(1)}) custom-call(bf16[64,2048]{1,0:T(8,128)(2,1)S(1)} %get-tuple-element.20.q_ref, bf16[2048,64]{1,0:T(8,128)(2,1)S(1)} %get-tuple-element.23.k_ref, bf16[64,2048]{1,0:T(8,128)(2,1)S(1)} %get-tuple-element.24.vt_ref, ...), custom_call_target="tpu_custom_call" | custom-call | flops 4294967296 | bytes 3145728 | tf_op jit(solution)/shard_map/attend_strip/pallas_call | solution.py:344
  77.3 0.0 copy-start.3
  77.3 0.0 collective-permute-done.2.below_ref
  77.3 2.1 %attend_edges.1 = bf16[16,64,128]{2,1,0:T(8,128)(2,1)} custom-call(bf16[64,2048]{1,0:T(8,128)(2,1)S(1)} %get-tuple-element.20.q_ref, bf16[128,512]{1,0:T(8,128)(2,1)S(1)} %collective-permute-done.1.above_ref, bf16[128,512]{1,0:T(8,128)(2,1)S(1)} %collective-permute-done.2.below_ref, f32[64,2048]{1,0:T(8,128)S(1)} %get-tuple-element.26.acc_ref, ...), custom_call_target="tpu_custom_call" | custom-call | tf_op jit(solution)/shard_map/attend_edges/pallas_call | solution.py:362
  79.4 0.0 all-to-all-done.near_ref
  79.4 16.5 %collective-permute-start.3 = (bf16[8,1056,128]{2,1,0:T(8,128)(2,1)S(1)}, bf16[8,1056,128]{2,1,0:T(8,128)(2,1)}, u32[]{:S(2)}, u32[]{:S(2)}) collective-permute-start(bf16[8,1056,128]{2,1,0:T(8,128)(2,1)S(1)} %all-to-all-done.near_ref), channel_id=1, source_target_pairs={{0,32},{32,0},{1,33},{33,1},{2,34},{34,2},{3,35},{35,3},{4,36},{36... | collective-permute-start | bytes 6488072 | tf_op jit(solution)/shard_map/ppermute | solution.py:372
  96.0 3.4 %all-to-all-start.1 = ((bf16[16,64,128]{2,1,0:T(8,128)(2,1)}), bf16[16,64,128]{2,1,0:T(8,128)(2,1)S(1)}, u32[]{:S(2)}, u32[]{:S(2)}) async-start(bf16[16,64,128]{2,1,0:T(8,128)(2,1)} %attend_edges.1), calls=%async_computation.1 | async-start | bytes 524288 | tf_op jit(solution)/shard_map/all_to_all | solution.py:373
  99.4 0.1 reshape.15.valid_ref
  99.5 12.3 %all-gather.8.cloned.1.call-done = bf16[7680,128]{1,0:T(8,128)(2,1)} async-done(((bf16[480,128]{1,0:T(8,128)(2,1)}), bf16[7680,128]{1,0:T(8,128)(2,1)}) %all-gather.8.cloned.1.call-update) | async-done | bytes 1966096 | tf_op jit(solution)/shard_map/all_gather | solution.py:313
  111.8 0.0 all-to-all-done.1.ctx_ref
  111.9 0.0 collective-permute-done.3.far_ref
  111.9 1.5 %copy-done.1 = bf16[7680,128]{1,0:T(8,128)(2,1)S(1)} copy-done((bf16[7680,128]{1,0:T(8,128)(2,1)S(1)}, bf16[7680,128]{1,0:T(8,128)(2,1)}, u32[]{:S(2)}) %copy-start.1) | copy-done | bytes 1966104
  113.4 3.8 %finish.1 = bf16[128,768]{1,0:T(8,128)(2,1)} custom-call(bf16[16,64,128]{2,1,0:T(8,128)(2,1)S(1)} %all-to-all-done.1.ctx_ref, bf16[16,480,128]{2,1,0:T(8,128)(2,1)S(1)} %bitcast.8, bf16[8,1056,128]{2,1,0:T(8,128)(2,1)S(1)} %all-to-all-done.near_ref, bf16[8,1056,128]{2,1,0:T(8,128)(2,1)} %collective-permute-done.3.far_ref, bf16[128,768]{1,0:T(8,128)(2,1)S(1)} %bitcast.10, ...), custom_call_target="tpu_custom_call" | custom-call | flops 754974720 | bytes 7340032 | tf_op jit(solution)/shard_map/finish/pallas_call | solution.py:374
  (9 shorter events, 0.0 us)
Async XLA Ops:
  6.5 57.4 %all-gather.6.cloned.1.call-start = ((), (), s32[]{:S(2)}) async-start(), calls=%async_computation.2 | async-start | bytes 3551232 | tf_op jit(solution)/shard_map/all_gather | solution.py:292
  8.6 6.9 %collective-permute-start = (bf16[96,128]{1,0:T(8,128)(2,1)}, bf16[96,128]{1,0:T(8,128)(2,1)S(1)}, u32[]{:S(2)}, u32[]{:S(2)}) collective-permute-start(bf16[96,128]{1,0:T(8,128)(2,1)} %get-tuple-element.18), channel_id=1, source_target_pairs={{0,16},{16,0},{1,17},{17,1},{2,18},{18,2},{3,19},{19,3},{4,20},{20... | collective-permute-start | bytes 73736 | tf_op jit(solution)/shard_map/ppermute | solution.py:291
  55.0 24.5 %all-to-all-start = ((bf16[8,1056,128]{2,1,0:T(8,128)(2,1)}), bf16[8,1056,128]{2,1,0:T(8,128)(2,1)S(1)}, u32[]{:S(2)}, u32[]{:S(2)}) async-start(bf16[8,1056,128]{2,1,0:T(8,128)(2,1)} %sort_spread.1.order_ref), calls=%async_computation | async-start | bytes 4325376 | tf_op jit(solution)/shard_map/all_to_all | solution.py:304
  60.1 51.8 %all-gather.8.cloned.1.call-start = ((), (), s32[]{:S(2)}) async-start(), calls=%async_computation.3 | async-start | bytes 2088960 | tf_op jit(solution)/shard_map/all_gather | solution.py:313
  63.9 1.9 %copy-start = (bf16[2176,768]{1,0:T(8,128)(2,1)S(1)}, bf16[2176,768]{1,0:T(8,128)(2,1)}, u32[]{:S(2)}) copy-start(bf16[2176,768]{1,0:T(8,128)(2,1)} %all-gather.6.cloned.1.call-done) | copy-start | bytes 10027012
  65.9 1.0 copy-start.2
  68.4 8.9 %collective-permute-start.1 = (bf16[128,512]{1,0:T(8,128)(2,1)S(1)}, bf16[128,512]{1,0:T(8,128)(2,1)S(1)}, u32[]{:S(2)}, u32[]{:S(2)}) collective-permute-start(bf16[128,512]{1,0:T(8,128)(2,1)S(1)} %get-tuple-element.21), channel_id=1, source_target_pairs={{0,1},{1,2},{2,3},{3,4},{4,5},{5,6},{6,7},{7,8},{8,9},{9,10},{10,1... | collective-permute-start | bytes 393224 | tf_op jit(solution)/shard_map/ppermute | solution.py:340
  69.7 7.6 %collective-permute-start.2 = (bf16[128,512]{1,0:T(8,128)(2,1)S(1)}, bf16[128,512]{1,0:T(8,128)(2,1)S(1)}, u32[]{:S(2)}, u32[]{:S(2)}) collective-permute-start(bf16[128,512]{1,0:T(8,128)(2,1)S(1)} %get-tuple-element.22), channel_id=1, source_target_pairs={{1,0},{2,1},{3,2},{4,3},{5,4},{6,5},{7,6},{8,7},{9,8},{10,9},{11,1... | collective-permute-start | bytes 393224 | tf_op jit(solution)/shard_map/ppermute | solution.py:341
  71.0 28.4 %copy-start.5 = (s32[8,16]{1,0:T(8,128)S(1)}, s32[8,16]{1,0:T(8,128)}, u32[]{:S(2)}) copy-start(s32[8,16]{1,0:T(8,128)} %param.10) | copy-start | bytes 1540
  71.0 40.8 %copy-start.4 = (f32[768]{0:T(1024)S(1)}, f32[768]{0:T(1024)}, u32[]{:S(2)}) copy-start(f32[768]{0:T(1024)} %gain_ref.3) | copy-start | bytes 9220
  77.3 34.6 %copy-start.3 = (bf16[8,16,768]{2,1,0:T(8,128)(2,1)S(1)}, bf16[8,16,768]{2,1,0:T(8,128)(2,1)}, u32[]{:S(2)}) copy-start(bf16[8,16,768]{2,1,0:T(8,128)(2,1)} %param.9) | copy-start | bytes 589828
  79.4 32.4 %collective-permute-start.3 = (bf16[8,1056,128]{2,1,0:T(8,128)(2,1)S(1)}, bf16[8,1056,128]{2,1,0:T(8,128)(2,1)}, u32[]{:S(2)}, u32[]{:S(2)}) collective-permute-start(bf16[8,1056,128]{2,1,0:T(8,128)(2,1)S(1)} %all-to-all-done.near_ref), channel_id=1, source_target_pairs={{0,32},{32,0},{1,33},{33,1},{2,34},{34,2},{3,35},{35,3},{4,36},{36... | collective-permute-start | bytes 6488072 | tf_op jit(solution)/shard_map/ppermute | solution.py:372
  96.0 15.9 %all-to-all-start.1 = ((bf16[16,64,128]{2,1,0:T(8,128)(2,1)}), bf16[16,64,128]{2,1,0:T(8,128)(2,1)S(1)}, u32[]{:S(2)}, u32[]{:S(2)}) async-start(bf16[16,64,128]{2,1,0:T(8,128)(2,1)} %attend_edges.1), calls=%async_computation.1 | async-start | bytes 524288 | tf_op jit(solution)/shard_map/all_to_all | solution.py:373
  111.9 1.5 %copy-start.1 = (bf16[7680,128]{1,0:T(8,128)(2,1)S(1)}, bf16[7680,128]{1,0:T(8,128)(2,1)}, u32[]{:S(2)}) copy-start(bf16[7680,128]{1,0:T(8,128)(2,1)} %all-gather.8.cloned.1.call-done) | copy-start | bytes 5898244
Sparse Core Ops, SparseCore 0:
  9.5 49.3 all-gather.5
  63.1 48.7 all-gather.7

commit v5 on v4

--- a/solution.py
+++ b/solution.py
@@ -16,7 +16,7 @@
 LANES = 128
 EDGE = 32
 WIDE = 256
-SPLIT = 480
+SPLIT = 528
 MASKED = -1e30
 LON = ("y", "xl", "c")
 CHIPS = ("y", "xl")
@@ -86,7 +86,7 @@
         fill(up_ref[:, pl.ds(start, LANES)], up_ref[:, pl.ds(start + LANES, LANES)])
 
 
-def sort_gather(rows_ref, order_ref, gather_out):
+def sort_gather(rows_ref, gather_out):
     place_j = lon_place()
     xh = lax.axis_index("xh")
 
@@ -102,7 +102,7 @@
             gather_out[pl.ds(part * 24, 24), :] = source[pl.ds(48, 24), :]
 
 
-def sort_spread(rows_ref, spread_hbm, rest, sems):
+def sort_spread(rows_ref, order_ref, spread_hbm, rest, sems):
     place_j = lon_place()
     xh = lax.axis_index("xh")
 
@@ -292,31 +292,31 @@
     strip = lax.all_gather(normed, LON, axis=0)
     both = jnp.stack([piece, twin])
     rows = lax.all_gather(both, "z", axis=0)
+    gather_rows = pl.pallas_call(
+        sort_gather,
+        out_shape=jax.ShapeDtypeStruct((SPLIT, LANES), BF),
+        in_specs=[whole()],
+        out_specs=whole(),
+        compiler_params=params(6),
+        name="sort_gather",
+    )(rows)
+    gathered = lax.all_gather(gather_rows, LON, axis=0)
     spread_rows = pl.pallas_call(
         sort_spread,
         out_shape=jax.ShapeDtypeStruct((8, FFW - SPLIT, LANES), BF),
-        in_specs=[whole()],
+        in_specs=[whole(), pl.BlockSpec(memory_space=pl.ANY)],
         out_specs=pl.BlockSpec(memory_space=pl.ANY),
         scratch_shapes=[pltpu.VMEM((FFW - SPLIT, LANES), BF), pltpu.SemaphoreType.DMA((8,))],
-        compiler_params=params(56),
+        compiler_params=params(6),
         name="sort_spread",
-    )(rows)
+    )(rows, gather_rows)
     near = lax.all_to_all(spread_rows, CHIPS, 0, 0)
-    gather_rows = pl.pallas_call(
-        sort_gather,
-        out_shape=jax.ShapeDtypeStruct((SPLIT, LANES), BF),
-        in_specs=[whole(), pl.BlockSpec(memory_space=pl.ANY)],
-        out_specs=whole(),
-        compiler_params=params(56),
-        name="sort_gather",
-    )(rows, spread_rows)
-    gathered = lax.all_gather(gather_rows, LON, axis=0)
     head_w = pl.pallas_call(
         sort_head,
         out_shape=jax.ShapeDtypeStruct((D, 2 * LANES), BF),
         in_specs=[whole()],
         out_specs=whole(),
-        compiler_params=params(56),
+        compiler_params=params(6),
         name="sort_head",
     )(rows)
     halo = jax.ShapeDtypeStruct((LANES, 4 * LANES), BF)

time: 125 us -> 121 us (0.968)
  Pallas kernels: 22.1 us -> 19.2 us
  blocking collectives: 36.1 us -> 33.4 us
  starting transfers between devices: 33.2 us -> 35.8 us
    all_gather x1, waiting for transfers between devices: 12.3 us -> 8.1 us  [body(): gathered = lax.all_gather(gather_rows, LON, axis=0)]
    all_to_all x1, waiting for transfers between devices: 0.01 us -> 3.52 us  [body(): near = lax.all_to_all(spread_rows, CHIPS, 0, 0)]
    all_gather x1, blocking collectives: 36.1 us -> 33.4 us  [body(): rows = lax.all_gather(both, 'z', axis=0)]
    pallas_call x1, Pallas kernels: 1.97 us -> 0.07 us  [body(): pl.pallas_call(sort_head, out_shape=jax.ShapeDtypeStruct((D, 2 * LANES),...]
    ppermute x1, starting transfers between devices: 16.5 us -> 18 us  [body(): far = lax.ppermute(near, 'c', [(0, 1), (1, 0)])]
  transfers between devices with their start and end apart: 8 -> 8, of which waited for: 2 -> 3; matrix products, arithmetic and copies ran while one was open for 1% -> 1% of each run, Pallas kernels for 13% -> 11%
where the time goes in v5:
time: 121 us
  starting transfers between devices  35.8 us (30%)
  blocking collectives  33.4 us (28%)
  Pallas kernels  19.2 us (16%)
  between operations  13.6 us (11%)
  waiting for transfers between devices  13.1 us (11%)
  local copies, waits for them, and re-layouts  4.94 us (4%)
    all_gather x1, blocking collectives, body(): rows = lax.all_gather(both, 'z', axis=0)  33.4 us
    ppermute x1, starting transfers between devices, body(): far = lax.ppermute(near, 'c', [(0, 1), (1, 0)])  18 us
    all_gather x1, waiting for transfers between devices, body(): gathered = lax.all_gather(gather_rows, LON, axis=0)  8.1 us
    pallas_call x1, Pallas kernels, body(): pl.pallas_call(attend_strip, out_shape=(jax.ShapeDtypeStruct((HEAD, keys)...  6.22 us
    ppermute x1, starting transfers between devices, body(): twin = lax.ppermute(piece, 'xh', [(0, 1), (1, 0)])  5.48 us
    all_to_all x1, starting transfers between devices, body(): near = lax.all_to_all(spread_rows, CHIPS, 0, 0)  5.13 us
    unnamed x12, local copies, waits for them, and re-layouts  4.86 us
    pallas_call x1, Pallas kernels, body(): pl.pallas_call(finish, out_shape=jax.ShapeDtypeStruct((TOK, D), BF), in_s...  3.75 us
  transfers between devices with their start and end apart: 8, of which 3 were waited for; matrix products, arithmetic and copies ran while one was open for 1% of the time, Pallas kernels for 11%

profile of v5, /device:TPU:1, one launch (start us, length us, event | category | flops | bytes accessed | tf_op | source)
XLA Modules:
  0.0 120.7 jit_solution(13367331199619843442)
XLA Ops:
  6.5 2.0 %prepare.1 = (bf16[136,768]{1,0:T(8,128)(2,1)}, bf16[96,128]{1,0:T(8,128)(2,1)}) custom-call(bf16[128,768]{1,0:T(8,128)(2,1)} %bitcast.12, f32[768]{0:T(1024)} %gain_ref.2, s32[1,1,16]{2,1,0:T(1,128)} %mask_ref.1, bf16[24,2304]{1,0:T(8,128)(2,1)} %qkv_ref.1, bf16[24,768]{1,0:T(8,128)(2,1)} %out_ref.1, bf16[24,1536]{1,0:T(8,128)(2,1)} %up_ref.1, ...), custom_call_target="tpu_custom_call" | custom-call | tf_op jit(solution)/shard_map/prepare/pallas_call | solution.py:280
  8.6 0.0 all-gather.6.cloned.1.call-update
  8.6 0.0 all-gather.8.cloned.1.call-start
  8.7 5.5 %collective-permute-start = (bf16[96,128]{1,0:T(8,128)(2,1)}, bf16[96,128]{1,0:T(8,128)(2,1)S(1)}, u32[]{:S(2)}, u32[]{:S(2)}) collective-permute-start(bf16[96,128]{1,0:T(8,128)(2,1)} %get-tuple-element.18), channel_id=1, source_target_pairs={{0,16},{16,0},{1,17},{17,1},{2,18},{18,2},{3,19},{19,3},{4,20},{20... | collective-permute-start | bytes 73736 | tf_op jit(solution)/shard_map/ppermute | solution.py:291
  14.1 1.4 %collective-permute-done = bf16[96,128]{1,0:T(8,128)(2,1)S(1)} collective-permute-done((bf16[96,128]{1,0:T(8,128)(2,1)}, bf16[96,128]{1,0:T(8,128)(2,1)S(1)}, u32[]{:S(2)}, u32[]{:S(2)}) %collective-permute-start) | collective-permute-done | bytes 24608 | tf_op jit(solution)/shard_map/ppermute | solution.py:291
  15.6 0.7 pad_maximum_fusion
  16.3 33.4 %all-gather = bf16[32,96,128]{2,1,0:T(8,128)(2,1)S(1)} all-gather(bf16[2,96,128]{2,1,0:T(8,128)(2,1)S(1)} %pad_maximum_fusion), channel_id=2, replica_groups=mesh['y'=4,'xl'=2,'c'=2,'xh'=2,'z'=16] {'z'}, dimensions={0}, use_global_device_ids=true | all-gather | bytes 835584 | tf_op jit(solution)/shard_map/all_gather | solution.py:294
  49.7 0.7 sort_gather.1.order_ref
  50.3 0.0 all-gather.8.cloned.1.call-update
  50.3 2.8 %sort_spread.1 = bf16[8,1008,128]{2,1,0:T(8,128)(2,1)S(1)} custom-call(bf16[16,2,96,128]{3,2,1,0:T(8,128)(2,1)S(1)} %bitcast.8, bf16[528,128]{1,0:T(8,128)(2,1)} %sort_gather.1.order_ref), custom_call_target="tpu_custom_call" | custom-call | tf_op jit(solution)/shard_map/sort_spread/pallas_call | solution.py:304
  53.1 1.3 %copy-done = bf16[8,1008,128]{2,1,0:T(8,128)(2,1)} copy-done((bf16[8,1008,128]{2,1,0:T(8,128)(2,1)}, bf16[8,1008,128]{2,1,0:T(8,128)(2,1)S(1)}, u32[]{:S(2)}) %copy-start) | copy-done | bytes 2064408
  54.4 5.1 %all-to-all-start = ((bf16[8,1008,128]{2,1,0:T(8,128)(2,1)}), bf16[8,1008,128]{2,1,0:T(8,128)(2,1)S(1)}, u32[]{:S(2)}, u32[]{:S(2)}) async-start(bf16[8,1008,128]{2,1,0:T(8,128)(2,1)} %copy-done), calls=%async_computation | async-start | bytes 4128768 | tf_op jit(solution)/shard_map/all_to_all | solution.py:313
  59.6 0.1 sort_head.1.weight_ref
  59.6 0.0 all-gather.6.cloned.1.call-done
  59.7 1.9 %copy-done.1 = bf16[2176,768]{1,0:T(8,128)(2,1)S(1)} copy-done((bf16[2176,768]{1,0:T(8,128)(2,1)S(1)}, bf16[2176,768]{1,0:T(8,128)(2,1)}, u32[]{:S(2)}) %copy-start.1) | copy-done | bytes 3342360
  61.6 1.5 %project.1 = (bf16[64,2048]{1,0:T(8,128)(2,1)S(1)}, bf16[2048,64]{1,0:T(8,128)(2,1)S(1)}, bf16[64,2048]{1,0:T(8,128)(2,1)S(1)}, bf16[128,512]{1,0:T(8,128)(2,1)S...) custom-call(bf16[16,136,768]{2,1,0:T(8,128)(2,1)S(1)} %bitcast.10, bf16[768,256]{1,0:T(8,128)(2,1)S(1)} %sort_head.1.weight_ref), custom_call_target="tpu_custom_call" | custom-call | flops 805306368 | bytes 5242880 | tf_op jit(solution)/shard_map/project/pallas_call | solution.py:324
  63.2 2.4 %collective-permute-start.1 = (bf16[128,512]{1,0:T(8,128)(2,1)S(1)}, bf16[128,512]{1,0:T(8,128)(2,1)S(1)}, u32[]{:S(2)}, u32[]{:S(2)}) collective-permute-start(bf16[128,512]{1,0:T(8,128)(2,1)S(1)} %get-tuple-element.21), channel_id=1, source_target_pairs={{0,1},{1,2},{2,3},{3,4},{4,5},{5,6},{6,7},{7,8},{8,9},{9,10},{10,1... | collective-permute-start | bytes 393224 | tf_op jit(solution)/shard_map/ppermute | solution.py:340
  65.6 1.3 %collective-permute-start.2 = (bf16[128,512]{1,0:T(8,128)(2,1)S(1)}, bf16[128,512]{1,0:T(8,128)(2,1)S(1)}, u32[]{:S(2)}, u32[]{:S(2)}) collective-permute-start(bf16[128,512]{1,0:T(8,128)(2,1)S(1)} %get-tuple-element.22), channel_id=1, source_target_pairs={{1,0},{2,1},{3,2},{4,3},{5,4},{6,5},{7,6},{8,7},{9,8},{10,9},{11,1... | collective-permute-start | bytes 393224 | tf_op jit(solution)/shard_map/ppermute | solution.py:341
  66.9 0.0 copy-start.5
  66.9 0.0 copy-start.4
  66.9 6.2 %attend_strip.1 = (f32[64,2048]{1,0:T(8,128)S(1)}, f32[8,2048]{1,0:T(8,128)S(1)}, f32[8,2048]{1,0:T(8,128)S(1)}) custom-call(bf16[64,2048]{1,0:T(8,128)(2,1)S(1)} %get-tuple-element.20.q_ref, bf16[2048,64]{1,0:T(8,128)(2,1)S(1)} %get-tuple-element.23.k_ref, bf16[64,2048]{1,0:T(8,128)(2,1)S(1)} %get-tuple-element.24.vt_ref, ...), custom_call_target="tpu_custom_call" | custom-call | flops 4294967296 | bytes 3145728 | tf_op jit(solution)/shard_map/attend_strip/pallas_call | solution.py:344
  73.1 0.0 copy-start.3
  73.1 0.0 collective-permute-done.1.above_ref
  73.2 2.1 %attend_edges.1 = bf16[16,64,128]{2,1,0:T(8,128)(2,1)} custom-call(bf16[64,2048]{1,0:T(8,128)(2,1)S(1)} %get-tuple-element.20.q_ref, bf16[128,512]{1,0:T(8,128)(2,1)S(1)} %collective-permute-done.1.above_ref, bf16[128,512]{1,0:T(8,128)(2,1)S(1)} %collective-permute-done.2.below_ref, f32[64,2048]{1,0:T(8,128)S(1)} %get-tuple-element.26.acc_ref, ...), custom_call_target="tpu_custom_call" | custom-call | tf_op jit(solution)/shard_map/attend_edges/pallas_call | solution.py:362
  75.3 3.5 %all-to-all-done.near_ref = bf16[8,1008,128]{2,1,0:T(8,128)(2,1)S(1)} async-done(((bf16[8,1008,128]{2,1,0:T(8,128)(2,1)}), bf16[8,1008,128]{2,1,0:T(8,128)(2,1)S(1)}, u32[]{:S(2)}, u32[]{:S(2)}) %all-to-all-start) | async-done | bytes 2064416 | tf_op jit(solution)/shard_map/all_to_all | solution.py:313
  78.8 18.0 %collective-permute-start.3 = (bf16[8,1008,128]{2,1,0:T(8,128)(2,1)S(1)}, bf16[8,1008,128]{2,1,0:T(8,128)(2,1)}, u32[]{:S(2)}, u32[]{:S(2)}) collective-permute-start(bf16[8,1008,128]{2,1,0:T(8,128)(2,1)S(1)} %all-to-all-done.near_ref), channel_id=1, source_target_pairs={{0,32},{32,0},{1,33},{33,1},{2,34},{34,2},{3,35},{35,3},{4,36},{36... | collective-permute-start | bytes 6193160 | tf_op jit(solution)/shard_map/ppermute | solution.py:372
  96.8 3.4 %all-to-all-start.1 = ((bf16[16,64,128]{2,1,0:T(8,128)(2,1)}), bf16[16,64,128]{2,1,0:T(8,128)(2,1)S(1)}, u32[]{:S(2)}, u32[]{:S(2)}) async-start(bf16[16,64,128]{2,1,0:T(8,128)(2,1)} %attend_edges.1), calls=%async_computation.1 | async-start | bytes 524288 | tf_op jit(solution)/shard_map/all_to_all | solution.py:373
  100.3 0.1 reshape.15.valid_ref
  100.3 8.1 %all-gather.8.cloned.1.call-done = bf16[8448,128]{1,0:T(8,128)(2,1)} async-done(((bf16[528,128]{1,0:T(8,128)(2,1)}), bf16[8448,128]{1,0:T(8,128)(2,1)}) %all-gather.8.cloned.1.call-update) | async-done | bytes 2162704 | tf_op jit(solution)/shard_map/all_gather | solution.py:303
  108.4 0.0 all-to-all-done.1.ctx_ref
  108.5 1.6 %copy-done.2 = bf16[8448,128]{1,0:T(8,128)(2,1)S(1)} copy-done((bf16[8448,128]{1,0:T(8,128)(2,1)S(1)}, bf16[8448,128]{1,0:T(8,128)(2,1)}, u32[]{:S(2)}) %copy-start.2) | copy-done | bytes 2162712
  110.1 3.8 %finish.1 = bf16[128,768]{1,0:T(8,128)(2,1)} custom-call(bf16[16,64,128]{2,1,0:T(8,128)(2,1)S(1)} %all-to-all-done.1.ctx_ref, bf16[16,528,128]{2,1,0:T(8,128)(2,1)S(1)} %bitcast.11, bf16[8,1008,128]{2,1,0:T(8,128)(2,1)S(1)} %all-to-all-done.near_ref, bf16[8,1008,128]{2,1,0:T(8,128)(2,1)} %collective-permute-done.3.far_ref, bf16[128,768]{1,0:T(8,128)(2,1)S(1)} %bitcast.13, ...), custom_call_target="tpu_custom_call" | custom-call | flops 754974720 | bytes 7340032 | tf_op jit(solution)/shard_map/finish/pallas_call | solution.py:374
  (9 shorter events, 0.0 us)
Async XLA Ops:
  6.5 53.1 %all-gather.6.cloned.1.call-start = ((), (), s32[]{:S(2)}) async-start(), calls=%async_computation.2 | async-start | bytes 3551232 | tf_op jit(solution)/shard_map/all_gather | solution.py:292
  8.6 99.8 %all-gather.8.cloned.1.call-start = ((), (), s32[]{:S(2)}) async-start(), calls=%async_computation.3 | async-start | bytes 2297856 | tf_op jit(solution)/shard_map/all_gather | solution.py:303
  8.7 6.9 %collective-permute-start = (bf16[96,128]{1,0:T(8,128)(2,1)}, bf16[96,128]{1,0:T(8,128)(2,1)S(1)}, u32[]{:S(2)}, u32[]{:S(2)}) collective-permute-start(bf16[96,128]{1,0:T(8,128)(2,1)} %get-tuple-element.18), channel_id=1, source_target_pairs={{0,16},{16,0},{1,17},{17,1},{2,18},{18,2},{3,19},{19,3},{4,20},{20... | collective-permute-start | bytes 73736 | tf_op jit(solution)/shard_map/ppermute | solution.py:291
  53.1 1.3 %copy-start = (bf16[8,1008,128]{2,1,0:T(8,128)(2,1)}, bf16[8,1008,128]{2,1,0:T(8,128)(2,1)S(1)}, u32[]{:S(2)}) copy-start(bf16[8,1008,128]{2,1,0:T(8,128)(2,1)S(1)} %sort_spread.1) | copy-start | bytes 6193156
  54.4 24.4 %all-to-all-start = ((bf16[8,1008,128]{2,1,0:T(8,128)(2,1)}), bf16[8,1008,128]{2,1,0:T(8,128)(2,1)S(1)}, u32[]{:S(2)}, u32[]{:S(2)}) async-start(bf16[8,1008,128]{2,1,0:T(8,128)(2,1)} %copy-done), calls=%async_computation | async-start | bytes 4128768 | tf_op jit(solution)/shard_map/all_to_all | solution.py:313
  59.7 1.9 %copy-start.1 = (bf16[2176,768]{1,0:T(8,128)(2,1)S(1)}, bf16[2176,768]{1,0:T(8,128)(2,1)}, u32[]{:S(2)}) copy-start(bf16[2176,768]{1,0:T(8,128)(2,1)} %all-gather.6.cloned.1.call-done) | copy-start | bytes 10027012
  63.2 10.0 %collective-permute-start.1 = (bf16[128,512]{1,0:T(8,128)(2,1)S(1)}, bf16[128,512]{1,0:T(8,128)(2,1)S(1)}, u32[]{:S(2)}, u32[]{:S(2)}) collective-permute-start(bf16[128,512]{1,0:T(8,128)(2,1)S(1)} %get-tuple-element.21), channel_id=1, source_target_pairs={{0,1},{1,2},{2,3},{3,4},{4,5},{5,6},{6,7},{7,8},{8,9},{9,10},{10,1... | collective-permute-start | bytes 393224 | tf_op jit(solution)/shard_map/ppermute | solution.py:340
  65.6 7.6 %collective-permute-start.2 = (bf16[128,512]{1,0:T(8,128)(2,1)S(1)}, bf16[128,512]{1,0:T(8,128)(2,1)S(1)}, u32[]{:S(2)}, u32[]{:S(2)}) collective-permute-start(bf16[128,512]{1,0:T(8,128)(2,1)S(1)} %get-tuple-element.22), channel_id=1, source_target_pairs={{1,0},{2,1},{3,2},{4,3},{5,4},{6,5},{7,6},{8,7},{9,8},{10,9},{11,1... | collective-permute-start | bytes 393224 | tf_op jit(solution)/shard_map/ppermute | solution.py:341
  66.9 33.4 %copy-start.5 = (s32[8,16]{1,0:T(8,128)S(1)}, s32[8,16]{1,0:T(8,128)}, u32[]{:S(2)}) copy-start(s32[8,16]{1,0:T(8,128)} %param.10) | copy-start | bytes 1540
  66.9 41.6 %copy-start.4 = (f32[768]{0:T(1024)S(1)}, f32[768]{0:T(1024)}, u32[]{:S(2)}) copy-start(f32[768]{0:T(1024)} %gain_ref.3) | copy-start | bytes 9220
  73.1 35.3 %copy-start.3 = (bf16[8,16,768]{2,1,0:T(8,128)(2,1)S(1)}, bf16[8,16,768]{2,1,0:T(8,128)(2,1)}, u32[]{:S(2)}) copy-start(bf16[8,16,768]{2,1,0:T(8,128)(2,1)} %param.9) | copy-start | bytes 589828
  78.8 29.6 %collective-permute-start.3 = (bf16[8,1008,128]{2,1,0:T(8,128)(2,1)S(1)}, bf16[8,1008,128]{2,1,0:T(8,128)(2,1)}, u32[]{:S(2)}, u32[]{:S(2)}) collective-permute-start(bf16[8,1008,128]{2,1,0:T(8,128)(2,1)S(1)} %all-to-all-done.near_ref), channel_id=1, source_target_pairs={{0,32},{32,0},{1,33},{33,1},{2,34},{34,2},{3,35},{35,3},{4,36},{36... | collective-permute-start | bytes 6193160 | tf_op jit(solution)/shard_map/ppermute | solution.py:372
  96.8 11.6 %all-to-all-start.1 = ((bf16[16,64,128]{2,1,0:T(8,128)(2,1)}), bf16[16,64,128]{2,1,0:T(8,128)(2,1)S(1)}, u32[]{:S(2)}, u32[]{:S(2)}) async-start(bf16[16,64,128]{2,1,0:T(8,128)(2,1)} %attend_edges.1), calls=%async_computation.1 | async-start | bytes 524288 | tf_op jit(solution)/shard_map/all_to_all | solution.py:373
  108.5 1.6 %copy-start.2 = (bf16[8448,128]{1,0:T(8,128)(2,1)S(1)}, bf16[8448,128]{1,0:T(8,128)(2,1)}, u32[]{:S(2)}) copy-start(bf16[8448,128]{1,0:T(8,128)(2,1)} %all-gather.8.cloned.1.call-done) | copy-start | bytes 6488068
Sparse Core Ops, SparseCore 0:
  9.5 49.3 all-gather.5
  61.0 47.3 all-gather.7

commit v6 on v5

--- a/solution.py
+++ b/solution.py
@@ -234,22 +234,37 @@
             out_ref[group * 4 + index] = result[:, index * TOK : (index + 1) * TOK]
 
 
-def finish(ctx_ref, gather_ref, near_ref, far_ref, tokens_ref, valid_ref, gain_ref, out_ref):
+def finish(
+    ctx_ref, gather_hbm, near_hbm, far_hbm, tokens_ref, valid_ref, gain_ref, out_ref, weights, sems
+):
     core = lax.axis_index("c")
 
-    def run(even_ref, odd_ref):
+    def run(even_hbm, odd_hbm):
+        def copies(part):
+            rest = odd_hbm if part % 2 else even_hbm
+            return (
+                pltpu.make_async_copy(
+                    gather_hbm.at[part], weights.at[part, pl.ds(0, SPLIT), :], sems.at[2 * part]
+                ),
+                pltpu.make_async_copy(
+                    rest.at[part // 2], weights.at[part, pl.ds(SPLIT, FFW - SPLIT), :], sems.at[2 * part + 1]
+                ),
+            )
+
+        for part in (6, 7, 8, 9, 10, 11, 12, 13, 14, 0, 1, 2, 3, 4, 5):
+            for copy in copies(part):
+                copy.start()
         context_t = ctx_ref[pl.ds(0, HEADS)].reshape(D, TOK)
         context = jnp.transpose(context_t.astype(F32)).astype(BF)
         valid = valid_ref[...].astype(F32)
 
-        def column(part):
-            ref = odd_ref if part % 2 else even_ref
-            return [gather_ref[part], ref[part // 2]]
+        def settle(part):
+            for copy in copies(part):
+                copy.wait()
 
         def into(rows, part):
-            head, rest = column(part)
-            left = jnp.concatenate([head, rest[: D - SPLIT]], axis=0)
-            weight = jnp.concatenate([left, rest[D - SPLIT :]], axis=1)
+            settle(part)
+            weight = jnp.concatenate([weights[part, :D, :], weights[part, D:, :]], axis=1)
             return jnp.dot(rows, weight, preferred_element_type=F32)
 
         attended = jnp.concatenate([into(context, part) for part in range(6, 9)], axis=1)
@@ -258,20 +273,20 @@
         normed = norm_rows(residual, gain_ref[...].reshape(1, D)).astype(BF)
         inner = jnp.concatenate([jax.nn.gelu(into(normed, part)).astype(BF) for part in range(9, 15)], axis=1)
         for chunk in range(3):
-            weight = jnp.concatenate(
-                [jnp.concatenate(column(2 * chunk + side), axis=0) for side in range(2)], axis=1
-            )
+            settle(2 * chunk)
+            settle(2 * chunk + 1)
+            weight = jnp.concatenate([weights[2 * chunk], weights[2 * chunk + 1]], axis=1)
             down = jnp.dot(inner, weight, preferred_element_type=F32)
             span = slice(chunk * WIDE, (chunk + 1) * WIDE)
             out_ref[:, span] = (residual[:, span] + valid * down).astype(BF)
 
     @pl.when(core == 0)
     def _():
-        run(near_ref, far_ref)
+        run(near_hbm, far_hbm)
 
     @pl.when(core == 1)
     def _():
-        run(far_ref, near_ref)
+        run(far_hbm, near_hbm)
 
 
 def body(tokens, patch_valid, block_mask, gain_attn, gain_mlp, w_qkv, w_out, w_up, w_down):
@@ -374,9 +389,10 @@
     mixed = pl.pallas_call(
         finish,
         out_shape=jax.ShapeDtypeStruct((TOK, D), BF),
-        in_specs=[whole()] * 7,
+        in_specs=[whole()] + [pl.BlockSpec(memory_space=pl.ANY)] * 3 + [whole()] * 3,
         out_specs=whole(),
-        compiler_params=params(20),
+        scratch_shapes=[pltpu.VMEM((STRIPES, FFW, LANES), BF), pltpu.SemaphoreType.DMA((32,))],
+        compiler_params=params(56),
         cost_estimate=pl.CostEstimate(flops=2 * 128 * 768 * 3840, bytes_accessed=7 << 20, transcendentals=128 * 1536),
         name="finish",
     )(mine, gathered, near, far, own, patch_valid.reshape(TOK, 1), gain_mlp)

time: 121 us -> 125 us (1.033)
  waiting for transfers between devices: 13.1 us -> 18.8 us
  starting transfers between devices: 35.8 us -> 34 us
  local copies, waits for them, and re-layouts: 4.94 us -> 3.37 us
  Pallas kernels: 19.2 us -> 20.7 us
    all_gather x1, waiting for transfers between devices: 8.1 us -> 14.7 us  [body(): gathered = lax.all_gather(gather_rows, LON, axis=0)]
    pallas_call x1, Pallas kernels: 3.75 us -> 6.66 us  [body(): pl.pallas_call(finish, out_shape=jax.ShapeDtypeStruct((TOK, D), BF), in_s...]
    all_to_all x1, waiting for transfers between devices: 3.52 us -> 0.78 us  [body(): near = lax.all_to_all(spread_rows, CHIPS, 0, 0)]
    ppermute x1, starting transfers between devices: 18 us -> 15.5 us  [body(): far = lax.ppermute(near, 'c', [(0, 1), (1, 0)])]
    unnamed x12 -> x8, local copies, waits for them, and re-layouts: 4.86 us -> 2.65 us
    all_gather x1, waiting for transfers between devices: 0.02 us -> 1.91 us  [body(): strip = lax.all_gather(normed, LON, axis=0)]
    pallas_call x1, Pallas kernels: 2.78 us -> 1.43 us  [body(): pl.pallas_call(sort_spread, out_shape=jax.ShapeDtypeStruct((8, FFW - SPLI...]
  transfers between devices with their start and end apart: 8 -> 8, of which waited for: 3 -> 4; matrix products, arithmetic and copies ran while one was open for 1% -> 1% of each run, Pallas kernels for 11% -> 10%
where the time goes in v6:
time: 125 us
  starting transfers between devices  34 us (27%)
  blocking collectives  33.4 us (27%)
  Pallas kernels  20.7 us (17%)
  waiting for transfers between devices  18.8 us (15%)
  between operations  13.5 us (11%)
  local copies, waits for them, and re-layouts  3.37 us (3%)
    all_gather x1, blocking collectives, body(): rows = lax.all_gather(both, 'z', axis=0)  33.4 us
    ppermute x1, starting transfers between devices, body(): far = lax.ppermute(near, 'c', [(0, 1), (1, 0)])  15.5 us
    all_gather x1, waiting for transfers between devices, body(): gathered = lax.all_gather(gather_rows, LON, axis=0)  14.7 us
    pallas_call x1, Pallas kernels, body(): pl.pallas_call(finish, out_shape=jax.ShapeDtypeStruct((TOK, D), BF), in_s...  6.66 us
    pallas_call x1, Pallas kernels, body(): pl.pallas_call(attend_strip, out_shape=(jax.ShapeDtypeStruct((HEAD, keys)...  6.22 us
    ppermute x1, starting transfers between devices, body(): twin = lax.ppermute(piece, 'xh', [(0, 1), (1, 0)])  5.48 us
    all_to_all x1, starting transfers between devices, body(): near = lax.all_to_all(spread_rows, CHIPS, 0, 0)  5.14 us
    all_to_all x1, starting transfers between devices, body(): mine = lax.all_to_all(context, LON, 0, 0)  3.44 us
  transfers between devices with their start and end apart: 8, of which 4 were waited for; matrix products, arithmetic and copies ran while one was open for 1% of the time, Pallas kernels for 10%

profile of v6, /device:TPU:1, one launch (start us, length us, event | category | flops | bytes accessed | tf_op | source)
XLA Modules:
  0.0 124.6 jit_solution(12912715501184580220)
XLA Ops:
  6.5 0.0 all-gather.6.cloned.1.call-start
  6.5 2.0 %prepare.1 = (bf16[136,768]{1,0:T(8,128)(2,1)}, bf16[96,128]{1,0:T(8,128)(2,1)}) custom-call(bf16[128,768]{1,0:T(8,128)(2,1)} %bitcast.12, f32[768]{0:T(1024)} %gain_ref.2, s32[1,1,16]{2,1,0:T(1,128)} %mask_ref.1, bf16[24,2304]{1,0:T(8,128)(2,1)} %qkv_ref.1, bf16[24,768]{1,0:T(8,128)(2,1)} %out_ref.1, bf16[24,1536]{1,0:T(8,128)(2,1)} %up_ref.1, ...), custom_call_target="tpu_custom_call" | custom-call | tf_op jit(solution)/shard_map/prepare/pallas_call | solution.py:295
  8.6 0.0 all-gather.6.cloned.1.call-update
  8.6 0.0 all-gather.8.cloned.1.call-start
  8.6 5.5 %collective-permute-start = (bf16[96,128]{1,0:T(8,128)(2,1)}, bf16[96,128]{1,0:T(8,128)(2,1)S(1)}, u32[]{:S(2)}, u32[]{:S(2)}) collective-permute-start(bf16[96,128]{1,0:T(8,128)(2,1)} %get-tuple-element.18), channel_id=1, source_target_pairs={{0,16},{16,0},{1,17},{17,1},{2,18},{18,2},{3,19},{19,3},{4,20},{20... | collective-permute-start | bytes 73736 | tf_op jit(solution)/shard_map/ppermute | solution.py:306
  14.1 1.4 %collective-permute-done = bf16[96,128]{1,0:T(8,128)(2,1)S(1)} collective-permute-done((bf16[96,128]{1,0:T(8,128)(2,1)}, bf16[96,128]{1,0:T(8,128)(2,1)S(1)}, u32[]{:S(2)}, u32[]{:S(2)}) %collective-permute-start) | collective-permute-done | bytes 24608 | tf_op jit(solution)/shard_map/ppermute | solution.py:306
  15.5 0.7 pad_maximum_fusion
  16.3 33.4 %all-gather = bf16[32,96,128]{2,1,0:T(8,128)(2,1)S(1)} all-gather(bf16[2,96,128]{2,1,0:T(8,128)(2,1)S(1)} %pad_maximum_fusion), channel_id=2, replica_groups=mesh['y'=4,'xl'=2,'c'=2,'xh'=2,'z'=16] {'z'}, dimensions={0}, use_global_device_ids=true | all-gather | bytes 835584 | tf_op jit(solution)/shard_map/all_gather | solution.py:309
  49.6 0.7 sort_gather.1.order_ref
  50.3 0.0 all-gather.8.cloned.1.call-update
  50.3 1.4 %sort_spread.1 = bf16[8,1008,128]{2,1,0:T(8,128)(2,1)} custom-call(bf16[16,2,96,128]{3,2,1,0:T(8,128)(2,1)S(1)} %bitcast.8, bf16[528,128]{1,0:T(8,128)(2,1)} %sort_gather.1.order_ref), custom_call_target="tpu_custom_call" | custom-call | tf_op jit(solution)/shard_map/sort_spread/pallas_call | solution.py:319
  51.8 5.1 %all-to-all-start = ((bf16[8,1008,128]{2,1,0:T(8,128)(2,1)}), bf16[8,1008,128]{2,1,0:T(8,128)(2,1)S(1)}, u32[]{:S(2)}, u32[]{:S(2)}) async-start(bf16[8,1008,128]{2,1,0:T(8,128)(2,1)} %sort_spread.1), calls=%async_computation | async-start | bytes 4128768 | tf_op jit(solution)/shard_map/all_to_all | solution.py:328
  56.9 0.1 sort_head.1.weight_ref
  57.0 1.9 %all-gather.6.cloned.1.call-done = bf16[2176,768]{1,0:T(8,128)(2,1)} async-done(((bf16[136,768]{1,0:T(8,128)(2,1)}), bf16[2176,768]{1,0:T(8,128)(2,1)}) %all-gather.6.cloned.1.call-update) | async-done | bytes 3342352 | tf_op jit(solution)/shard_map/all_gather | solution.py:307
  58.9 1.9 %copy-done = bf16[2176,768]{1,0:T(8,128)(2,1)S(1)} copy-done((bf16[2176,768]{1,0:T(8,128)(2,1)S(1)}, bf16[2176,768]{1,0:T(8,128)(2,1)}, u32[]{:S(2)}) %copy-start) | copy-done | bytes 3342360
  60.8 1.5 %project.1 = (bf16[64,2048]{1,0:T(8,128)(2,1)S(1)}, bf16[2048,64]{1,0:T(8,128)(2,1)S(1)}, bf16[64,2048]{1,0:T(8,128)(2,1)S(1)}, bf16[128,512]{1,0:T(8,128)(2,1)S...) custom-call(bf16[16,136,768]{2,1,0:T(8,128)(2,1)S(1)} %bitcast.10, bf16[768,256]{1,0:T(8,128)(2,1)S(1)} %sort_head.1.weight_ref), custom_call_target="tpu_custom_call" | custom-call | flops 805306368 | bytes 5242880 | tf_op jit(solution)/shard_map/project/pallas_call | solution.py:339
  62.4 3.2 %collective-permute-start.1 = (bf16[128,512]{1,0:T(8,128)(2,1)S(1)}, bf16[128,512]{1,0:T(8,128)(2,1)S(1)}, u32[]{:S(2)}, u32[]{:S(2)}) collective-permute-start(bf16[128,512]{1,0:T(8,128)(2,1)S(1)} %get-tuple-element.21), channel_id=1, source_target_pairs={{0,1},{1,2},{2,3},{3,4},{4,5},{5,6},{6,7},{7,8},{8,9},{9,10},{10,1... | collective-permute-start | bytes 393224 | tf_op jit(solution)/shard_map/ppermute | solution.py:355
  65.6 1.3 %collective-permute-start.2 = (bf16[128,512]{1,0:T(8,128)(2,1)S(1)}, bf16[128,512]{1,0:T(8,128)(2,1)S(1)}, u32[]{:S(2)}, u32[]{:S(2)}) collective-permute-start(bf16[128,512]{1,0:T(8,128)(2,1)S(1)} %get-tuple-element.22), channel_id=1, source_target_pairs={{1,0},{2,1},{3,2},{4,3},{5,4},{6,5},{7,6},{8,7},{9,8},{10,9},{11,1... | collective-permute-start | bytes 393224 | tf_op jit(solution)/shard_map/ppermute | solution.py:356
  66.9 0.0 copy-start.3
  66.9 6.2 %attend_strip.1 = (f32[64,2048]{1,0:T(8,128)S(1)}, f32[8,2048]{1,0:T(8,128)S(1)}, f32[8,2048]{1,0:T(8,128)S(1)}) custom-call(bf16[64,2048]{1,0:T(8,128)(2,1)S(1)} %get-tuple-element.20.q_ref, bf16[2048,64]{1,0:T(8,128)(2,1)S(1)} %get-tuple-element.23.k_ref, bf16[64,2048]{1,0:T(8,128)(2,1)S(1)} %get-tuple-element.24.vt_ref, ...), custom_call_target="tpu_custom_call" | custom-call | flops 4294967296 | bytes 3145728 | tf_op jit(solution)/shard_map/attend_strip/pallas_call | solution.py:359
  73.1 0.0 collective-permute-done.1.above_ref
  73.1 0.0 collective-permute-done.2.below_ref
  73.1 2.1 %attend_edges.1 = bf16[16,64,128]{2,1,0:T(8,128)(2,1)} custom-call(bf16[64,2048]{1,0:T(8,128)(2,1)S(1)} %get-tuple-element.20.q_ref, bf16[128,512]{1,0:T(8,128)(2,1)S(1)} %collective-permute-done.1.above_ref, bf16[128,512]{1,0:T(8,128)(2,1)S(1)} %collective-permute-done.2.below_ref, f32[64,2048]{1,0:T(8,128)S(1)} %get-tuple-element.26.acc_ref, ...), custom_call_target="tpu_custom_call" | custom-call | tf_op jit(solution)/shard_map/attend_edges/pallas_call | solution.py:377
  75.3 0.8 all-to-all-done.near_hbm
  76.0 15.5 %collective-permute-start.3 = (bf16[8,1008,128]{2,1,0:T(8,128)(2,1)S(1)}, bf16[8,1008,128]{2,1,0:T(8,128)(2,1)}, u32[]{:S(2)}, u32[]{:S(2)}) collective-permute-start(bf16[8,1008,128]{2,1,0:T(8,128)(2,1)S(1)} %all-to-all-done.near_hbm), channel_id=1, source_target_pairs={{0,32},{32,0},{1,33},{33,1},{2,34},{34,2},{3,35},{35,3},{4,36},{36... | collective-permute-start | bytes 6193160 | tf_op jit(solution)/shard_map/ppermute | solution.py:387
  91.5 3.4 %all-to-all-start.1 = ((bf16[16,64,128]{2,1,0:T(8,128)(2,1)}), bf16[16,64,128]{2,1,0:T(8,128)(2,1)S(1)}, u32[]{:S(2)}, u32[]{:S(2)}) async-start(bf16[16,64,128]{2,1,0:T(8,128)(2,1)} %attend_edges.1), calls=%async_computation.1 | async-start | bytes 524288 | tf_op jit(solution)/shard_map/all_to_all | solution.py:388
  95.0 0.7 reshape.15.valid_ref
  95.7 14.7 %all-gather.8.cloned.1.call-done = bf16[8448,128]{1,0:T(8,128)(2,1)} async-done(((bf16[528,128]{1,0:T(8,128)(2,1)}), bf16[8448,128]{1,0:T(8,128)(2,1)}) %all-gather.8.cloned.1.call-update) | async-done | bytes 2162704 | tf_op jit(solution)/shard_map/all_gather | solution.py:318
  110.3 0.0 all-to-all-done.1.ctx_ref
  110.3 0.0 collective-permute-done.3.far_hbm
  110.4 0.7 copy-done.2
  111.1 6.7 %finish.1 = bf16[128,768]{1,0:T(8,128)(2,1)} custom-call(bf16[16,64,128]{2,1,0:T(8,128)(2,1)} %copy-done.2, bf16[16,528,128]{2,1,0:T(8,128)(2,1)} %bitcast.11, bf16[8,1008,128]{2,1,0:T(8,128)(2,1)} %copy-done.1, bf16[8,1008,128]{2,1,0:T(8,128)(2,1)} %collective-permute-done.3.far_hbm, bf16[128,768]{1,0:T(8,128)(2,1)} %bitcast.13, ...), custom_call_target="tpu_custom_call" | custom-call | flops 754974720 | bytes 7340032 | tf_op jit(solution)/shard_map/finish/pallas_call | solution.py:389
  (5 shorter events, 0.0 us)
Async XLA Ops:
  6.5 52.4 %all-gather.6.cloned.1.call-start = ((), (), s32[]{:S(2)}) async-start(), calls=%async_computation.2 | async-start | bytes 3551232 | tf_op jit(solution)/shard_map/all_gather | solution.py:307
  8.6 101.7 %all-gather.8.cloned.1.call-start = ((), (), s32[]{:S(2)}) async-start(), calls=%async_computation.3 | async-start | bytes 2297856 | tf_op jit(solution)/shard_map/all_gather | solution.py:318
  8.6 6.9 %collective-permute-start = (bf16[96,128]{1,0:T(8,128)(2,1)}, bf16[96,128]{1,0:T(8,128)(2,1)S(1)}, u32[]{:S(2)}, u32[]{:S(2)}) collective-permute-start(bf16[96,128]{1,0:T(8,128)(2,1)} %get-tuple-element.18), channel_id=1, source_target_pairs={{0,16},{16,0},{1,17},{17,1},{2,18},{18,2},{3,19},{19,3},{4,20},{20... | collective-permute-start | bytes 73736 | tf_op jit(solution)/shard_map/ppermute | solution.py:306
  51.8 24.3 %all-to-all-start = ((bf16[8,1008,128]{2,1,0:T(8,128)(2,1)}), bf16[8,1008,128]{2,1,0:T(8,128)(2,1)S(1)}, u32[]{:S(2)}, u32[]{:S(2)}) async-start(bf16[8,1008,128]{2,1,0:T(8,128)(2,1)} %sort_spread.1), calls=%async_computation | async-start | bytes 4128768 | tf_op jit(solution)/shard_map/all_to_all | solution.py:328
  58.9 1.9 %copy-start = (bf16[2176,768]{1,0:T(8,128)(2,1)S(1)}, bf16[2176,768]{1,0:T(8,128)(2,1)}, u32[]{:S(2)}) copy-start(bf16[2176,768]{1,0:T(8,128)(2,1)} %all-gather.6.cloned.1.call-done) | copy-start | bytes 10027012
  62.4 10.7 %collective-permute-start.1 = (bf16[128,512]{1,0:T(8,128)(2,1)S(1)}, bf16[128,512]{1,0:T(8,128)(2,1)S(1)}, u32[]{:S(2)}, u32[]{:S(2)}) collective-permute-start(bf16[128,512]{1,0:T(8,128)(2,1)S(1)} %get-tuple-element.21), channel_id=1, source_target_pairs={{0,1},{1,2},{2,3},{3,4},{4,5},{5,6},{6,7},{7,8},{8,9},{9,10},{10,1... | collective-permute-start | bytes 393224 | tf_op jit(solution)/shard_map/ppermute | solution.py:355
  65.6 7.5 %collective-permute-start.2 = (bf16[128,512]{1,0:T(8,128)(2,1)S(1)}, bf16[128,512]{1,0:T(8,128)(2,1)S(1)}, u32[]{:S(2)}, u32[]{:S(2)}) collective-permute-start(bf16[128,512]{1,0:T(8,128)(2,1)S(1)} %get-tuple-element.22), channel_id=1, source_target_pairs={{1,0},{2,1},{3,2},{4,3},{5,4},{6,5},{7,6},{8,7},{9,8},{10,9},{11,1... | collective-permute-start | bytes 393224 | tf_op jit(solution)/shard_map/ppermute | solution.py:356
  66.9 28.1 %copy-start.3 = (s32[8,16]{1,0:T(8,128)S(1)}, s32[8,16]{1,0:T(8,128)}, u32[]{:S(2)}) copy-start(s32[8,16]{1,0:T(8,128)} %param.10) | copy-start | bytes 1540
  76.0 34.3 %copy-start.1 = (bf16[8,1008,128]{2,1,0:T(8,128)(2,1)}, bf16[8,1008,128]{2,1,0:T(8,128)(2,1)S(1)}, u32[]{:S(2)}) copy-start(bf16[8,1008,128]{2,1,0:T(8,128)(2,1)S(1)} %all-to-all-done.near_hbm) | copy-start | bytes 6193156
  76.0 34.3 %collective-permute-start.3 = (bf16[8,1008,128]{2,1,0:T(8,128)(2,1)S(1)}, bf16[8,1008,128]{2,1,0:T(8,128)(2,1)}, u32[]{:S(2)}, u32[]{:S(2)}) collective-permute-start(bf16[8,1008,128]{2,1,0:T(8,128)(2,1)S(1)} %all-to-all-done.near_hbm), channel_id=1, source_target_pairs={{0,32},{32,0},{1,33},{33,1},{2,34},{34,2},{3,35},{35,3},{4,36},{36... | collective-permute-start | bytes 6193160 | tf_op jit(solution)/shard_map/ppermute | solution.py:387
  91.5 18.8 %all-to-all-start.1 = ((bf16[16,64,128]{2,1,0:T(8,128)(2,1)}), bf16[16,64,128]{2,1,0:T(8,128)(2,1)S(1)}, u32[]{:S(2)}, u32[]{:S(2)}) async-start(bf16[16,64,128]{2,1,0:T(8,128)(2,1)} %attend_edges.1), calls=%async_computation.1 | async-start | bytes 524288 | tf_op jit(solution)/shard_map/all_to_all | solution.py:388
  110.3 0.7 copy-start.2
Sparse Core Ops, SparseCore 0:
  9.5 49.3 all-gather.5
  61.0 49.2 all-gather.7

commit v7 on v5

--- a/solution.py
+++ b/solution.py
@@ -234,8 +234,17 @@
             out_ref[group * 4 + index] = result[:, index * TOK : (index + 1) * TOK]
 
 
-def finish(ctx_ref, gather_ref, near_ref, far_ref, tokens_ref, valid_ref, gain_ref, out_ref):
+def finish(
+    ctx_ref, gather_hbm, near_ref, far_ref, tokens_ref, valid_ref, gain_ref, out_ref, gather_ref, sems
+):
     core = lax.axis_index("c")
+    order = (6, 7, 8, 9, 10, 11, 12, 13, 14, 0, 1, 2, 3, 4, 5)
+
+    def piece(part):
+        return pltpu.make_async_copy(gather_hbm.at[part], gather_ref.at[part], sems.at[part])
+
+    for part in order:
+        piece(part).start()
 
     def run(even_ref, odd_ref):
         context_t = ctx_ref[pl.ds(0, HEADS)].reshape(D, TOK)
@@ -244,6 +253,7 @@
 
         def column(part):
             ref = odd_ref if part % 2 else even_ref
+            piece(part).wait()
             return [gather_ref[part], ref[part // 2]]
 
         def into(rows, part):
@@ -374,9 +384,10 @@
     mixed = pl.pallas_call(
         finish,
         out_shape=jax.ShapeDtypeStruct((TOK, D), BF),
-        in_specs=[whole()] * 7,
+        in_specs=[whole(), pl.BlockSpec(memory_space=pl.ANY)] + [whole()] * 5,
         out_specs=whole(),
-        compiler_params=params(20),
+        scratch_shapes=[pltpu.VMEM((STRIPES, SPLIT, LANES), BF), pltpu.SemaphoreType.DMA((15,))],
+        compiler_params=params(51),
         cost_estimate=pl.CostEstimate(flops=2 * 128 * 768 * 3840, bytes_accessed=7 << 20, transcendentals=128 * 1536),
         name="finish",
     )(mine, gathered, near, far, own, patch_valid.reshape(TOK, 1), gain_mlp)

time: 121 us -> 123 us (1.017)
  Pallas kernels: 19.2 us -> 22.4 us
  local copies, waits for them, and re-layouts: 4.94 us -> 3.34 us
    pallas_call x1, Pallas kernels: 3.75 us -> 6.96 us  [body(): pl.pallas_call(finish, out_shape=jax.ShapeDtypeStruct((TOK, D), BF), in_s...]
    unnamed x12 -> x10, local copies, waits for them, and re-layouts: 4.86 us -> 3.26 us
where the time goes in v7:
time: 123 us; the launch traced here: 122 us
  starting transfers between devices  35.8 us (29%)
  blocking collectives  33.4 us (27%)
  Pallas kernels  22.4 us (18%)
  between operations  13.6 us (11%)
  waiting for transfers between devices  13 us (11%)
  local copies, waits for them, and re-layouts  3.34 us (3%)
    all_gather x1, blocking collectives, body(): rows = lax.all_gather(both, 'z', axis=0)  33.4 us
    ppermute x1, starting transfers between devices, body(): far = lax.ppermute(near, 'c', [(0, 1), (1, 0)])  18 us
    all_gather x1, waiting for transfers between devices, body(): gathered = lax.all_gather(gather_rows, LON, axis=0)  7.99 us
    pallas_call x1, Pallas kernels, body(): pl.pallas_call(finish, out_shape=jax.ShapeDtypeStruct((TOK, D), BF), in_s...  6.96 us
    pallas_call x1, Pallas kernels, body(): pl.pallas_call(attend_strip, out_shape=(jax.ShapeDtypeStruct((HEAD, keys)...  6.22 us
    ppermute x1, starting transfers between devices, body(): twin = lax.ppermute(piece, 'xh', [(0, 1), (1, 0)])  5.48 us
    all_to_all x1, starting transfers between devices, body(): near = lax.all_to_all(spread_rows, CHIPS, 0, 0)  5.13 us
    all_to_all x1, waiting for transfers between devices, body(): near = lax.all_to_all(spread_rows, CHIPS, 0, 0)  3.55 us
  transfers between devices with their start and end apart: 8, of which 3 were waited for; matrix products, arithmetic and copies ran while one was open for 1% of the time, Pallas kernels for 11%

profile of v7, /device:TPU:1, one launch (start us, length us, event | category | flops | bytes accessed | tf_op | source)
XLA Modules:
  0.0 122.2 jit_solution(8867554367247594465)
XLA Ops:
  6.5 2.0 %prepare.1 = (bf16[136,768]{1,0:T(8,128)(2,1)}, bf16[96,128]{1,0:T(8,128)(2,1)}) custom-call(bf16[128,768]{1,0:T(8,128)(2,1)} %bitcast.11, f32[768]{0:T(1024)} %gain_ref.2, s32[1,1,16]{2,1,0:T(1,128)} %mask_ref.1, bf16[24,2304]{1,0:T(8,128)(2,1)} %qkv_ref.1, bf16[24,768]{1,0:T(8,128)(2,1)} %out_ref.1, bf16[24,1536]{1,0:T(8,128)(2,1)} %up_ref.1, ...), custom_call_target="tpu_custom_call" | custom-call | tf_op jit(solution)/shard_map/prepare/pallas_call | solution.py:290
  8.6 0.0 all-gather.6.cloned.1.call-update
  8.6 0.0 all-gather.8.cloned.1.call-start
  8.7 5.5 %collective-permute-start = (bf16[96,128]{1,0:T(8,128)(2,1)}, bf16[96,128]{1,0:T(8,128)(2,1)S(1)}, u32[]{:S(2)}, u32[]{:S(2)}) collective-permute-start(bf16[96,128]{1,0:T(8,128)(2,1)} %get-tuple-element.18), channel_id=1, source_target_pairs={{0,16},{16,0},{1,17},{17,1},{2,18},{18,2},{3,19},{19,3},{4,20},{20... | collective-permute-start | bytes 73736 | tf_op jit(solution)/shard_map/ppermute | solution.py:301
  14.1 1.4 %collective-permute-done = bf16[96,128]{1,0:T(8,128)(2,1)S(1)} collective-permute-done((bf16[96,128]{1,0:T(8,128)(2,1)}, bf16[96,128]{1,0:T(8,128)(2,1)S(1)}, u32[]{:S(2)}, u32[]{:S(2)}) %collective-permute-start) | collective-permute-done | bytes 24608 | tf_op jit(solution)/shard_map/ppermute | solution.py:301
  15.6 0.7 pad_maximum_fusion
  16.3 33.4 %all-gather = bf16[32,96,128]{2,1,0:T(8,128)(2,1)S(1)} all-gather(bf16[2,96,128]{2,1,0:T(8,128)(2,1)S(1)} %pad_maximum_fusion), channel_id=2, replica_groups=mesh['y'=4,'xl'=2,'c'=2,'xh'=2,'z'=16] {'z'}, dimensions={0}, use_global_device_ids=true | all-gather | bytes 835584 | tf_op jit(solution)/shard_map/all_gather | solution.py:304
  49.7 0.7 sort_gather.1.order_ref
  50.3 0.0 all-gather.8.cloned.1.call-update
  50.3 2.8 %sort_spread.1 = bf16[8,1008,128]{2,1,0:T(8,128)(2,1)S(1)} custom-call(bf16[16,2,96,128]{3,2,1,0:T(8,128)(2,1)S(1)} %bitcast.8, bf16[528,128]{1,0:T(8,128)(2,1)} %sort_gather.1.order_ref), custom_call_target="tpu_custom_call" | custom-call | tf_op jit(solution)/shard_map/sort_spread/pallas_call | solution.py:314
  53.1 1.3 %copy-done = bf16[8,1008,128]{2,1,0:T(8,128)(2,1)} copy-done((bf16[8,1008,128]{2,1,0:T(8,128)(2,1)}, bf16[8,1008,128]{2,1,0:T(8,128)(2,1)S(1)}, u32[]{:S(2)}) %copy-start) | copy-done | bytes 2064408
  54.4 5.1 %all-to-all-start = ((bf16[8,1008,128]{2,1,0:T(8,128)(2,1)}), bf16[8,1008,128]{2,1,0:T(8,128)(2,1)S(1)}, u32[]{:S(2)}, u32[]{:S(2)}) async-start(bf16[8,1008,128]{2,1,0:T(8,128)(2,1)} %copy-done), calls=%async_computation | async-start | bytes 4128768 | tf_op jit(solution)/shard_map/all_to_all | solution.py:323
  59.6 0.1 sort_head.1.weight_ref
  59.6 0.0 all-gather.6.cloned.1.call-done
  59.7 1.9 %copy-done.1 = bf16[2176,768]{1,0:T(8,128)(2,1)S(1)} copy-done((bf16[2176,768]{1,0:T(8,128)(2,1)S(1)}, bf16[2176,768]{1,0:T(8,128)(2,1)}, u32[]{:S(2)}) %copy-start.1) | copy-done | bytes 3342360
  61.6 1.5 %project.1 = (bf16[64,2048]{1,0:T(8,128)(2,1)S(1)}, bf16[2048,64]{1,0:T(8,128)(2,1)S(1)}, bf16[64,2048]{1,0:T(8,128)(2,1)S(1)}, bf16[128,512]{1,0:T(8,128)(2,1)S...) custom-call(bf16[16,136,768]{2,1,0:T(8,128)(2,1)S(1)} %bitcast.10, bf16[768,256]{1,0:T(8,128)(2,1)S(1)} %sort_head.1.weight_ref), custom_call_target="tpu_custom_call" | custom-call | flops 805306368 | bytes 5242880 | tf_op jit(solution)/shard_map/project/pallas_call | solution.py:334
  63.2 2.4 %collective-permute-start.1 = (bf16[128,512]{1,0:T(8,128)(2,1)S(1)}, bf16[128,512]{1,0:T(8,128)(2,1)S(1)}, u32[]{:S(2)}, u32[]{:S(2)}) collective-permute-start(bf16[128,512]{1,0:T(8,128)(2,1)S(1)} %get-tuple-element.21), channel_id=1, source_target_pairs={{0,1},{1,2},{2,3},{3,4},{4,5},{5,6},{6,7},{7,8},{8,9},{9,10},{10,1... | collective-permute-start | bytes 393224 | tf_op jit(solution)/shard_map/ppermute | solution.py:350
  65.6 1.3 %collective-permute-start.2 = (bf16[128,512]{1,0:T(8,128)(2,1)S(1)}, bf16[128,512]{1,0:T(8,128)(2,1)S(1)}, u32[]{:S(2)}, u32[]{:S(2)}) collective-permute-start(bf16[128,512]{1,0:T(8,128)(2,1)S(1)} %get-tuple-element.22), channel_id=1, source_target_pairs={{1,0},{2,1},{3,2},{4,3},{5,4},{6,5},{7,6},{8,7},{9,8},{10,9},{11,1... | collective-permute-start | bytes 393224 | tf_op jit(solution)/shard_map/ppermute | solution.py:351
  66.9 0.0 copy-start.4
  66.9 0.0 copy-start.3
  66.9 6.2 %attend_strip.1 = (f32[64,2048]{1,0:T(8,128)S(1)}, f32[8,2048]{1,0:T(8,128)S(1)}, f32[8,2048]{1,0:T(8,128)S(1)}) custom-call(bf16[64,2048]{1,0:T(8,128)(2,1)S(1)} %get-tuple-element.20.q_ref, bf16[2048,64]{1,0:T(8,128)(2,1)S(1)} %get-tuple-element.23.k_ref, bf16[64,2048]{1,0:T(8,128)(2,1)S(1)} %get-tuple-element.24.vt_ref, ...), custom_call_target="tpu_custom_call" | custom-call | flops 4294967296 | bytes 3145728 | tf_op jit(solution)/shard_map/attend_strip/pallas_call | solution.py:354
  73.1 0.0 copy-start.2
  73.1 0.0 collective-permute-done.2.below_ref
  73.2 2.1 %attend_edges.1 = bf16[16,64,128]{2,1,0:T(8,128)(2,1)} custom-call(bf16[64,2048]{1,0:T(8,128)(2,1)S(1)} %get-tuple-element.20.q_ref, bf16[128,512]{1,0:T(8,128)(2,1)S(1)} %collective-permute-done.1.above_ref, bf16[128,512]{1,0:T(8,128)(2,1)S(1)} %collective-permute-done.2.below_ref, f32[64,2048]{1,0:T(8,128)S(1)} %get-tuple-element.26.acc_ref, ...), custom_call_target="tpu_custom_call" | custom-call | tf_op jit(solution)/shard_map/attend_edges/pallas_call | solution.py:372
  75.3 3.5 %all-to-all-done.near_ref = bf16[8,1008,128]{2,1,0:T(8,128)(2,1)S(1)} async-done(((bf16[8,1008,128]{2,1,0:T(8,128)(2,1)}), bf16[8,1008,128]{2,1,0:T(8,128)(2,1)S(1)}, u32[]{:S(2)}, u32[]{:S(2)}) %all-to-all-start) | async-done | bytes 2064416 | tf_op jit(solution)/shard_map/all_to_all | solution.py:323
  78.8 18.0 %collective-permute-start.3 = (bf16[8,1008,128]{2,1,0:T(8,128)(2,1)S(1)}, bf16[8,1008,128]{2,1,0:T(8,128)(2,1)}, u32[]{:S(2)}, u32[]{:S(2)}) collective-permute-start(bf16[8,1008,128]{2,1,0:T(8,128)(2,1)S(1)} %all-to-all-done.near_ref), channel_id=1, source_target_pairs={{0,32},{32,0},{1,33},{33,1},{2,34},{34,2},{3,35},{35,3},{4,36},{36... | collective-permute-start | bytes 6193160 | tf_op jit(solution)/shard_map/ppermute | solution.py:382
  96.8 3.4 %all-to-all-start.1 = ((bf16[16,64,128]{2,1,0:T(8,128)(2,1)}), bf16[16,64,128]{2,1,0:T(8,128)(2,1)S(1)}, u32[]{:S(2)}, u32[]{:S(2)}) async-start(bf16[16,64,128]{2,1,0:T(8,128)(2,1)} %attend_edges.1), calls=%async_computation.1 | async-start | bytes 524288 | tf_op jit(solution)/shard_map/all_to_all | solution.py:383
  100.3 0.1 reshape.15.valid_ref
  100.4 8.0 %all-gather.8.cloned.1.call-done = bf16[8448,128]{1,0:T(8,128)(2,1)} async-done(((bf16[528,128]{1,0:T(8,128)(2,1)}), bf16[8448,128]{1,0:T(8,128)(2,1)}) %all-gather.8.cloned.1.call-update) | async-done | bytes 2162704 | tf_op jit(solution)/shard_map/all_gather | solution.py:313
  108.3 0.0 all-to-all-done.1.ctx_ref
  108.3 0.0 collective-permute-done.3.far_ref
  108.4 7.0 %finish.1 = bf16[128,768]{1,0:T(8,128)(2,1)} custom-call(bf16[16,64,128]{2,1,0:T(8,128)(2,1)S(1)} %all-to-all-done.1.ctx_ref, bf16[16,528,128]{2,1,0:T(8,128)(2,1)} %bitcast.13, bf16[8,1008,128]{2,1,0:T(8,128)(2,1)S(1)} %all-to-all-done.near_ref, bf16[8,1008,128]{2,1,0:T(8,128)(2,1)} %collective-permute-done.3.far_ref, bf16[128,768]{1,0:T(8,128)(2,1)S(1)} %bitcast.12, ...), custom_call_target="tpu_custom_call" | custom-call | flops 754974720 | bytes 7340032 | tf_op jit(solution)/shard_map/finish/pallas_call | solution.py:384
  (7 shorter events, 0.0 us)
Async XLA Ops:
  6.5 53.1 %all-gather.6.cloned.1.call-start = ((), (), s32[]{:S(2)}) async-start(), calls=%async_computation.2 | async-start | bytes 3551232 | tf_op jit(solution)/shard_map/all_gather | solution.py:302
  8.6 99.7 %all-gather.8.cloned.1.call-start = ((), (), s32[]{:S(2)}) async-start(), calls=%async_computation.3 | async-start | bytes 2297856 | tf_op jit(solution)/shard_map/all_gather | solution.py:313
  8.7 6.9 %collective-permute-start = (bf16[96,128]{1,0:T(8,128)(2,1)}, bf16[96,128]{1,0:T(8,128)(2,1)S(1)}, u32[]{:S(2)}, u32[]{:S(2)}) collective-permute-start(bf16[96,128]{1,0:T(8,128)(2,1)} %get-tuple-element.18), channel_id=1, source_target_pairs={{0,16},{16,0},{1,17},{17,1},{2,18},{18,2},{3,19},{19,3},{4,20},{20... | collective-permute-start | bytes 73736 | tf_op jit(solution)/shard_map/ppermute | solution.py:301
  53.1 1.3 %copy-start = (bf16[8,1008,128]{2,1,0:T(8,128)(2,1)}, bf16[8,1008,128]{2,1,0:T(8,128)(2,1)S(1)}, u32[]{:S(2)}) copy-start(bf16[8,1008,128]{2,1,0:T(8,128)(2,1)S(1)} %sort_spread.1) | copy-start | bytes 6193156
  54.4 24.4 %all-to-all-start = ((bf16[8,1008,128]{2,1,0:T(8,128)(2,1)}), bf16[8,1008,128]{2,1,0:T(8,128)(2,1)S(1)}, u32[]{:S(2)}, u32[]{:S(2)}) async-start(bf16[8,1008,128]{2,1,0:T(8,128)(2,1)} %copy-done), calls=%async_computation | async-start | bytes 4128768 | tf_op jit(solution)/shard_map/all_to_all | solution.py:323
  59.7 1.9 %copy-start.1 = (bf16[2176,768]{1,0:T(8,128)(2,1)S(1)}, bf16[2176,768]{1,0:T(8,128)(2,1)}, u32[]{:S(2)}) copy-start(bf16[2176,768]{1,0:T(8,128)(2,1)} %all-gather.6.cloned.1.call-done) | copy-start | bytes 10027012
  63.2 10.0 %collective-permute-start.1 = (bf16[128,512]{1,0:T(8,128)(2,1)S(1)}, bf16[128,512]{1,0:T(8,128)(2,1)S(1)}, u32[]{:S(2)}, u32[]{:S(2)}) collective-permute-start(bf16[128,512]{1,0:T(8,128)(2,1)S(1)} %get-tuple-element.21), channel_id=1, source_target_pairs={{0,1},{1,2},{2,3},{3,4},{4,5},{5,6},{6,7},{7,8},{8,9},{9,10},{10,1... | collective-permute-start | bytes 393224 | tf_op jit(solution)/shard_map/ppermute | solution.py:350
  65.6 7.6 %collective-permute-start.2 = (bf16[128,512]{1,0:T(8,128)(2,1)S(1)}, bf16[128,512]{1,0:T(8,128)(2,1)S(1)}, u32[]{:S(2)}, u32[]{:S(2)}) collective-permute-start(bf16[128,512]{1,0:T(8,128)(2,1)S(1)} %get-tuple-element.22), channel_id=1, source_target_pairs={{1,0},{2,1},{3,2},{4,3},{5,4},{6,5},{7,6},{8,7},{9,8},{10,9},{11,1... | collective-permute-start | bytes 393224 | tf_op jit(solution)/shard_map/ppermute | solution.py:351
  66.9 33.4 %copy-start.4 = (s32[8,16]{1,0:T(8,128)S(1)}, s32[8,16]{1,0:T(8,128)}, u32[]{:S(2)}) copy-start(s32[8,16]{1,0:T(8,128)} %param.10) | copy-start | bytes 1540
  66.9 41.5 %copy-start.3 = (f32[768]{0:T(1024)S(1)}, f32[768]{0:T(1024)}, u32[]{:S(2)}) copy-start(f32[768]{0:T(1024)} %gain_ref.3) | copy-start | bytes 9220
  73.1 35.2 %copy-start.2 = (bf16[8,16,768]{2,1,0:T(8,128)(2,1)S(1)}, bf16[8,16,768]{2,1,0:T(8,128)(2,1)}, u32[]{:S(2)}) copy-start(bf16[8,16,768]{2,1,0:T(8,128)(2,1)} %param.9) | copy-start | bytes 589828
  78.8 29.5 %collective-permute-start.3 = (bf16[8,1008,128]{2,1,0:T(8,128)(2,1)S(1)}, bf16[8,1008,128]{2,1,0:T(8,128)(2,1)}, u32[]{:S(2)}, u32[]{:S(2)}) collective-permute-start(bf16[8,1008,128]{2,1,0:T(8,128)(2,1)S(1)} %all-to-all-done.near_ref), channel_id=1, source_target_pairs={{0,32},{32,0},{1,33},{33,1},{2,34},{34,2},{3,35},{35,3},{4,36},{36... | collective-permute-start | bytes 6193160 | tf_op jit(solution)/shard_map/ppermute | solution.py:382
  96.8 11.5 %all-to-all-start.1 = ((bf16[16,64,128]{2,1,0:T(8,128)(2,1)}), bf16[16,64,128]{2,1,0:T(8,128)(2,1)S(1)}, u32[]{:S(2)}, u32[]{:S(2)}) async-start(bf16[16,64,128]{2,1,0:T(8,128)(2,1)} %attend_edges.1), calls=%async_computation.1 | async-start | bytes 524288 | tf_op jit(solution)/shard_map/all_to_all | solution.py:383
Sparse Core Ops, SparseCore 0:
  9.5 49.3 all-gather.5
  61.0 47.2 all-gather.7

commit v8 on v5

--- a/solution.py
+++ b/solution.py
@@ -16,7 +16,7 @@
 LANES = 128
 EDGE = 32
 WIDE = 256
-SPLIT = 528
+SPLIT = 720
 MASKED = -1e30
 LON = ("y", "xl", "c")
 CHIPS = ("y", "xl")

time: 121 us -> 122 us (level)
  waiting for transfers between devices: 13.1 us -> 17 us
  starting transfers between devices: 35.8 us -> 32.3 us
  local copies, waits for them, and re-layouts: 4.94 us -> 7.23 us
  Pallas kernels: 19.2 us -> 17.4 us
    all_gather x1, waiting for transfers between devices: 8.1 us -> 15.6 us  [body(): gathered = lax.all_gather(gather_rows, LON, axis=0)]
    ppermute x1, starting transfers between devices: 18 us -> 13.3 us  [body(): far = lax.ppermute(near, 'c', [(0, 1), (1, 0)])]
    all_to_all x1, waiting for transfers between devices: 3.52 us -> 0.01 us  [body(): near = lax.all_to_all(spread_rows, CHIPS, 0, 0)]
    unnamed x12 -> x16, local copies, waits for them, and re-layouts: 4.86 us -> 6.51 us
  transfers between devices with their start and end apart: 8 -> 8, of which waited for: 3 -> 2; matrix products, arithmetic and copies ran while one was open for 1% -> 1% of each run, Pallas kernels for 11% -> 10%
where the time goes in v8:
time: 122 us
  blocking collectives  33.4 us (27%)
  starting transfers between devices  32.3 us (26%)
  Pallas kernels  17.4 us (14%)
  waiting for transfers between devices  17 us (14%)
  between operations  13.6 us (11%)
  local copies, waits for them, and re-layouts  7.23 us (6%)
    all_gather x1, blocking collectives, body(): rows = lax.all_gather(both, 'z', axis=0)  33.4 us
    all_gather x1, waiting for transfers between devices, body(): gathered = lax.all_gather(gather_rows, LON, axis=0)  15.6 us
    ppermute x1, starting transfers between devices, body(): far = lax.ppermute(near, 'c', [(0, 1), (1, 0)])  13.3 us
    unnamed x16, local copies, waits for them, and re-layouts  6.51 us
    pallas_call x1, Pallas kernels, body(): pl.pallas_call(attend_strip, out_shape=(jax.ShapeDtypeStruct((HEAD, keys)...  6.22 us
    ppermute x1, starting transfers between devices, body(): twin = lax.ppermute(piece, 'xh', [(0, 1), (1, 0)])  5.48 us
    all_to_all x1, starting transfers between devices, body(): near = lax.all_to_all(spread_rows, CHIPS, 0, 0)  5.13 us
    all_to_all x1, starting transfers between devices, body(): mine = lax.all_to_all(context, LON, 0, 0)  4.1 us
  transfers between devices with their start and end apart: 8, of which 2 were waited for; matrix products, arithmetic and copies ran while one was open for 1% of the time, Pallas kernels for 10%

profile of v8, /device:TPU:1, one launch (start us, length us, event | category | flops | bytes accessed | tf_op | source)
XLA Modules:
  0.0 121.6 jit_solution(13518541547344144686)
XLA Ops:
  6.5 2.1 %prepare.1 = (bf16[136,768]{1,0:T(8,128)(2,1)}, bf16[96,128]{1,0:T(8,128)(2,1)}) custom-call(bf16[128,768]{1,0:T(8,128)(2,1)} %bitcast.12, f32[768]{0:T(1024)} %gain_ref.2, s32[1,1,16]{2,1,0:T(1,128)} %mask_ref.1, bf16[24,2304]{1,0:T(8,128)(2,1)} %qkv_ref.1, bf16[24,768]{1,0:T(8,128)(2,1)} %out_ref.1, bf16[24,1536]{1,0:T(8,128)(2,1)} %up_ref.1, ...), custom_call_target="tpu_custom_call" | custom-call | tf_op jit(solution)/shard_map/prepare/pallas_call | solution.py:280
  8.6 0.0 all-gather.6.cloned.1.call-update
  8.6 0.0 all-gather.8.cloned.1.call-start
  8.7 5.5 %collective-permute-start = (bf16[96,128]{1,0:T(8,128)(2,1)}, bf16[96,128]{1,0:T(8,128)(2,1)S(1)}, u32[]{:S(2)}, u32[]{:S(2)}) collective-permute-start(bf16[96,128]{1,0:T(8,128)(2,1)} %get-tuple-element.18), channel_id=1, source_target_pairs={{0,16},{16,0},{1,17},{17,1},{2,18},{18,2},{3,19},{19,3},{4,20},{20... | collective-permute-start | bytes 73736 | tf_op jit(solution)/shard_map/ppermute | solution.py:291
  14.2 1.4 %collective-permute-done = bf16[96,128]{1,0:T(8,128)(2,1)S(1)} collective-permute-done((bf16[96,128]{1,0:T(8,128)(2,1)}, bf16[96,128]{1,0:T(8,128)(2,1)S(1)}, u32[]{:S(2)}, u32[]{:S(2)}) %collective-permute-start) | collective-permute-done | bytes 24608 | tf_op jit(solution)/shard_map/ppermute | solution.py:291
  15.6 0.7 pad_maximum_fusion
  16.3 33.4 %all-gather = bf16[32,96,128]{2,1,0:T(8,128)(2,1)S(1)} all-gather(bf16[2,96,128]{2,1,0:T(8,128)(2,1)S(1)} %pad_maximum_fusion), channel_id=2, replica_groups=mesh['y'=4,'xl'=2,'c'=2,'xh'=2,'z'=16] {'z'}, dimensions={0}, use_global_device_ids=true | all-gather | bytes 835584 | tf_op jit(solution)/shard_map/all_gather | solution.py:294
  49.7 0.7 sort_gather.1.order_ref
  50.4 0.0 all-gather.8.cloned.1.call-update
  50.4 2.3 %sort_spread.1 = bf16[8,816,128]{2,1,0:T(8,128)(2,1)S(1)} custom-call(bf16[16,2,96,128]{3,2,1,0:T(8,128)(2,1)S(1)} %bitcast.8, bf16[720,128]{1,0:T(8,128)(2,1)} %sort_gather.1.order_ref), custom_call_target="tpu_custom_call" | custom-call | tf_op jit(solution)/shard_map/sort_spread/pallas_call | solution.py:304
  52.7 1.2 copy-done
  53.9 5.1 %all-to-all-start = ((bf16[8,816,128]{2,1,0:T(8,128)(2,1)}), bf16[8,816,128]{2,1,0:T(8,128)(2,1)S(1)}, u32[]{:S(2)}, u32[]{:S(2)}) async-start(bf16[8,816,128]{2,1,0:T(8,128)(2,1)} %copy-done), calls=%async_computation | async-start | bytes 3342336 | tf_op jit(solution)/shard_map/all_to_all | solution.py:313
  59.0 0.1 sort_head.1.weight_ref
  59.1 0.0 all-gather.6.cloned.1.call-done
  59.1 1.9 %copy-done.1 = bf16[2176,768]{1,0:T(8,128)(2,1)S(1)} copy-done((bf16[2176,768]{1,0:T(8,128)(2,1)S(1)}, bf16[2176,768]{1,0:T(8,128)(2,1)}, u32[]{:S(2)}) %copy-start.1) | copy-done | bytes 3342360
  61.0 1.5 %project.1 = (bf16[64,2048]{1,0:T(8,128)(2,1)S(1)}, bf16[2048,64]{1,0:T(8,128)(2,1)S(1)}, bf16[64,2048]{1,0:T(8,128)(2,1)S(1)}, bf16[128,512]{1,0:T(8,128)(2,1)S...) custom-call(bf16[16,136,768]{2,1,0:T(8,128)(2,1)S(1)} %bitcast.10, bf16[768,256]{1,0:T(8,128)(2,1)S(1)} %sort_head.1.weight_ref), custom_call_target="tpu_custom_call" | custom-call | flops 805306368 | bytes 5242880 | tf_op jit(solution)/shard_map/project/pallas_call | solution.py:324
  62.6 3.0 %collective-permute-start.1 = (bf16[128,512]{1,0:T(8,128)(2,1)S(1)}, bf16[128,512]{1,0:T(8,128)(2,1)S(1)}, u32[]{:S(2)}, u32[]{:S(2)}) collective-permute-start(bf16[128,512]{1,0:T(8,128)(2,1)S(1)} %get-tuple-element.21), channel_id=1, source_target_pairs={{0,1},{1,2},{2,3},{3,4},{4,5},{5,6},{6,7},{7,8},{8,9},{9,10},{10,1... | collective-permute-start | bytes 393224 | tf_op jit(solution)/shard_map/ppermute | solution.py:340
  65.6 1.3 %collective-permute-start.2 = (bf16[128,512]{1,0:T(8,128)(2,1)S(1)}, bf16[128,512]{1,0:T(8,128)(2,1)S(1)}, u32[]{:S(2)}, u32[]{:S(2)}) collective-permute-start(bf16[128,512]{1,0:T(8,128)(2,1)S(1)} %get-tuple-element.22), channel_id=1, source_target_pairs={{1,0},{2,1},{3,2},{4,3},{5,4},{6,5},{7,6},{8,7},{9,8},{10,9},{11,1... | collective-permute-start | bytes 393224 | tf_op jit(solution)/shard_map/ppermute | solution.py:341
  66.9 6.2 %attend_strip.1 = (f32[64,2048]{1,0:T(8,128)S(1)}, f32[8,2048]{1,0:T(8,128)S(1)}, f32[8,2048]{1,0:T(8,128)S(1)}) custom-call(bf16[64,2048]{1,0:T(8,128)(2,1)S(1)} %get-tuple-element.20.q_ref, bf16[2048,64]{1,0:T(8,128)(2,1)S(1)} %get-tuple-element.23.k_ref, bf16[64,2048]{1,0:T(8,128)(2,1)S(1)} %get-tuple-element.24.vt_ref, ...), custom_call_target="tpu_custom_call" | custom-call | flops 4294967296 | bytes 3145728 | tf_op jit(solution)/shard_map/attend_strip/pallas_call | solution.py:344
  73.1 0.0 copy-start.7
  73.1 0.0 copy-start.4
  73.1 0.0 copy-start.6
  73.1 0.0 collective-permute-done.1.above_ref
  73.2 1.4 %attend_edges.1 = bf16[16,64,128]{2,1,0:T(8,128)(2,1)S(1)} custom-call(bf16[64,2048]{1,0:T(8,128)(2,1)S(1)} %get-tuple-element.20.q_ref, bf16[128,512]{1,0:T(8,128)(2,1)S(1)} %collective-permute-done.1.above_ref, bf16[128,512]{1,0:T(8,128)(2,1)S(1)} %collective-permute-done.2.below_ref, f32[64,2048]{1,0:T(8,128)S(1)} %get-tuple-element.26.acc_ref, ...), custom_call_target="tpu_custom_call" | custom-call | tf_op jit(solution)/shard_map/attend_edges/pallas_call | solution.py:362
  74.6 0.7 copy-done.3
  75.3 13.3 %collective-permute-start.3 = (bf16[8,816,128]{2,1,0:T(8,128)(2,1)S(1)}, bf16[8,816,128]{2,1,0:T(8,128)(2,1)S(1)}, u32[]{:S(2)}, u32[]{:S(2)}) collective-permute-start(bf16[8,816,128]{2,1,0:T(8,128)(2,1)S(1)} %all-to-all-done.near_ref), channel_id=1, source_target_pairs={{0,32},{32,0},{1,33},{33,1},{2,34},{34,2},{3,35},{35,3},{4,36},{36... | collective-permute-start | bytes 5013512 | tf_op jit(solution)/shard_map/ppermute | solution.py:372
  88.6 4.1 %all-to-all-start.1 = ((bf16[16,64,128]{2,1,0:T(8,128)(2,1)}), bf16[16,64,128]{2,1,0:T(8,128)(2,1)}, u32[]{:S(2)}, u32[]{:S(2)}) async-start(bf16[16,64,128]{2,1,0:T(8,128)(2,1)} %copy-done.3), calls=%async_computation.1 | async-start | bytes 524288 | tf_op jit(solution)/shard_map/all_to_all | solution.py:373
  92.7 0.7 reshape.15.valid_ref
  93.4 15.6 %all-gather.8.cloned.1.call-done = bf16[11520,128]{1,0:T(8,128)(2,1)} async-done(((bf16[720,128]{1,0:T(8,128)(2,1)}), bf16[11520,128]{1,0:T(8,128)(2,1)}) %all-gather.8.cloned.1.call-update) | async-done | bytes 2949136 | tf_op jit(solution)/shard_map/all_gather | solution.py:303
  109.0 1.8 %copy-done.2 = bf16[11520,128]{1,0:T(8,128)(2,1)S(1)} copy-done((bf16[11520,128]{1,0:T(8,128)(2,1)S(1)}, bf16[11520,128]{1,0:T(8,128)(2,1)}, u32[]{:S(2)}) %copy-start.2) | copy-done | bytes 2949144
  110.8 0.8 copy-done.5
  111.7 3.1 %finish.1 = bf16[128,768]{1,0:T(8,128)(2,1)} custom-call(bf16[16,64,128]{2,1,0:T(8,128)(2,1)} %all-to-all-done.1.ctx_ref, bf16[16,720,128]{2,1,0:T(8,128)(2,1)S(1)} %bitcast.11, bf16[8,816,128]{2,1,0:T(8,128)(2,1)S(1)} %all-to-all-done.near_ref, bf16[8,816,128]{2,1,0:T(8,128)(2,1)S(1)} %collective-permute-done.3.far_ref, bf16[128,768]{1,0:T(8,128)(2,1)S(1)} %bitcast.13, ...), custom_call_target="tpu_custom_call" | custom-call | flops 754974720 | bytes 7340032 | tf_op jit(solution)/shard_map/finish/pallas_call | solution.py:374
  (13 shorter events, 0.0 us)
Async XLA Ops:
  6.5 52.5 %all-gather.6.cloned.1.call-start = ((), (), s32[]{:S(2)}) async-start(), calls=%async_computation.2 | async-start | bytes 3551232 | tf_op jit(solution)/shard_map/all_gather | solution.py:292
  8.6 100.3 %all-gather.8.cloned.1.call-start = ((), (), s32[]{:S(2)}) async-start(), calls=%async_computation.3 | async-start | bytes 3133440 | tf_op jit(solution)/shard_map/all_gather | solution.py:303
  8.7 6.9 %collective-permute-start = (bf16[96,128]{1,0:T(8,128)(2,1)}, bf16[96,128]{1,0:T(8,128)(2,1)S(1)}, u32[]{:S(2)}, u32[]{:S(2)}) collective-permute-start(bf16[96,128]{1,0:T(8,128)(2,1)} %get-tuple-element.18), channel_id=1, source_target_pairs={{0,16},{16,0},{1,17},{17,1},{2,18},{18,2},{3,19},{19,3},{4,20},{20... | collective-permute-start | bytes 73736 | tf_op jit(solution)/shard_map/ppermute | solution.py:291
  52.7 1.2 copy-start
  53.9 21.4 %all-to-all-start = ((bf16[8,816,128]{2,1,0:T(8,128)(2,1)}), bf16[8,816,128]{2,1,0:T(8,128)(2,1)S(1)}, u32[]{:S(2)}, u32[]{:S(2)}) async-start(bf16[8,816,128]{2,1,0:T(8,128)(2,1)} %copy-done), calls=%async_computation | async-start | bytes 3342336 | tf_op jit(solution)/shard_map/all_to_all | solution.py:313
  59.1 1.9 %copy-start.1 = (bf16[2176,768]{1,0:T(8,128)(2,1)S(1)}, bf16[2176,768]{1,0:T(8,128)(2,1)}, u32[]{:S(2)}) copy-start(bf16[2176,768]{1,0:T(8,128)(2,1)} %all-gather.6.cloned.1.call-done) | copy-start | bytes 10027012
  62.6 10.6 %collective-permute-start.1 = (bf16[128,512]{1,0:T(8,128)(2,1)S(1)}, bf16[128,512]{1,0:T(8,128)(2,1)S(1)}, u32[]{:S(2)}, u32[]{:S(2)}) collective-permute-start(bf16[128,512]{1,0:T(8,128)(2,1)S(1)} %get-tuple-element.21), channel_id=1, source_target_pairs={{0,1},{1,2},{2,3},{3,4},{4,5},{5,6},{6,7},{7,8},{8,9},{9,10},{10,1... | collective-permute-start | bytes 393224 | tf_op jit(solution)/shard_map/ppermute | solution.py:340
  65.6 7.6 %collective-permute-start.2 = (bf16[128,512]{1,0:T(8,128)(2,1)S(1)}, bf16[128,512]{1,0:T(8,128)(2,1)S(1)}, u32[]{:S(2)}, u32[]{:S(2)}) collective-permute-start(bf16[128,512]{1,0:T(8,128)(2,1)S(1)} %get-tuple-element.22), channel_id=1, source_target_pairs={{1,0},{2,1},{3,2},{4,3},{5,4},{6,5},{7,6},{8,7},{9,8},{10,9},{11,1... | collective-permute-start | bytes 393224 | tf_op jit(solution)/shard_map/ppermute | solution.py:341
  73.1 19.6 %copy-start.7 = (s32[8,16]{1,0:T(8,128)S(1)}, s32[8,16]{1,0:T(8,128)}, u32[]{:S(2)}) copy-start(s32[8,16]{1,0:T(8,128)} %param.10) | copy-start | bytes 1540
  73.1 35.9 %copy-start.4 = (bf16[8,16,768]{2,1,0:T(8,128)(2,1)S(1)}, bf16[8,16,768]{2,1,0:T(8,128)(2,1)}, u32[]{:S(2)}) copy-start(bf16[8,16,768]{2,1,0:T(8,128)(2,1)} %param.9) | copy-start | bytes 589828
  73.1 35.8 %copy-start.6 = (f32[768]{0:T(1024)S(1)}, f32[768]{0:T(1024)}, u32[]{:S(2)}) copy-start(f32[768]{0:T(1024)} %gain_ref.3) | copy-start | bytes 9220
  74.6 0.7 copy-start.3
  75.3 33.7 %collective-permute-start.3 = (bf16[8,816,128]{2,1,0:T(8,128)(2,1)S(1)}, bf16[8,816,128]{2,1,0:T(8,128)(2,1)S(1)}, u32[]{:S(2)}, u32[]{:S(2)}) collective-permute-start(bf16[8,816,128]{2,1,0:T(8,128)(2,1)S(1)} %all-to-all-done.near_ref), channel_id=1, source_target_pairs={{0,32},{32,0},{1,33},{33,1},{2,34},{34,2},{3,35},{35,3},{4,36},{36... | collective-permute-start | bytes 5013512 | tf_op jit(solution)/shard_map/ppermute | solution.py:372
  88.6 20.4 %all-to-all-start.1 = ((bf16[16,64,128]{2,1,0:T(8,128)(2,1)}), bf16[16,64,128]{2,1,0:T(8,128)(2,1)}, u32[]{:S(2)}, u32[]{:S(2)}) async-start(bf16[16,64,128]{2,1,0:T(8,128)(2,1)} %copy-done.3), calls=%async_computation.1 | async-start | bytes 524288 | tf_op jit(solution)/shard_map/all_to_all | solution.py:373
  109.0 1.8 %copy-start.2 = (bf16[11520,128]{1,0:T(8,128)(2,1)S(1)}, bf16[11520,128]{1,0:T(8,128)(2,1)}, u32[]{:S(2)}) copy-start(bf16[11520,128]{1,0:T(8,128)(2,1)} %all-gather.8.cloned.1.call-done) | copy-start | bytes 8847364
  110.8 0.8 copy-start.5
Sparse Core Ops, SparseCore 0:
  9.5 49.3 all-gather.5
  61.0 47.8 all-gather.7
